TPU v7x, 256 devices: a whole 4x4x8 slice. The times are simulated.
256 devices in a mesh: region: 32 (over y_hi, z, core), tracer: 8 (over y_lo, x).
Axes of the slice: x: 4, y: 4 (y_hi: 2, y_lo: 2; y = y_hi * 2 + y_lo), z: 8, core: 2. Of those that a mesh axis runs over, the one named last changes fastest.
Arguments:
- tracers: float32 [256, 64, 6144], P('tracer', 'region'), may hold values from 0.2 to 1.5
- fluxes: float32 [2, 64, 6144], P(None, 'region', 'tracer'), may hold values from -0.4 to 0.4
- rate_coeff: float32 [1024], replicated, may hold values from 0.005 to 0.05
- first_reactant: int32 [1024], replicated, may hold values from 0 to 255
- second_reactant: int32 [1024], replicated, may hold values from 0 to 255
- product_species: int32 [1024], replicated, may hold values from 0 to 255
Outputs:
- tracers_out: float32 [256, 64, 6144], P('tracer', 'region')
All inputs are finite; a program needn't handle non-finite values.
Results may differ from a plain program's by a relative error of at most 0.0001.
Values sent between devices are 32-bit elements; how exact they have to be, the bound alone decides.
No kernel may reach another device: no remote copies, remote signals or barrier semaphores. Data moves between devices by JAX's collectives and lax.ppermute only.
A program may use at most 64 MiB of HBM per device.

v0:
```python
import jax
import jax.numpy as jnp
from jax import lax
from jax.experimental import pallas as pl
from jax.experimental.pallas import tpu as pltpu
from jax.sharding import PartitionSpec as P

TRACERS = 256
NY = 48
SUBSTEPS = 4
LANES = 128
CHUNKS = 2
F32 = jnp.float32
BF16 = jnp.bfloat16
VMEM = pl.BlockSpec(memory_space=pltpu.VMEM)


def as_tiles(tracers):
    own, cols, length = tracers.shape
    tiles = tracers.reshape(own, cols, length // LANES, LANES)
    return jnp.transpose(tiles, (0, 2, 1, 3)).reshape(-1, LANES).reshape(own, -1, LANES)


def cut_kernel(x_ref, *o_refs):
    part = o_refs[0].shape[1]
    for k, o_ref in enumerate(o_refs):
        o_ref[...] = x_ref[:, k * part : (k + 1) * part, :]


def cut(tiles):
    own, length, _ = tiles.shape
    part = length // CHUNKS
    parts = pl.pallas_call(
        cut_kernel,
        grid=(own // 8,),
        in_specs=[pl.BlockSpec((8, length, LANES), lambda i: (i, 0, 0))],
        out_specs=[pl.BlockSpec((8, part, LANES), lambda i: (i, 0, 0))] * CHUNKS,
        out_shape=[jax.ShapeDtypeStruct((own, part, LANES), F32)] * CHUNKS,
        name="cut",
    )(tiles)
    return [array.reshape(own * part, LANES) for array in parts]


def from_tiles(tiles, shape):
    own, cols, length = shape
    tiles = tiles.reshape(own, length // LANES, cols, LANES)
    return jnp.transpose(tiles, (0, 2, 1, 3)).reshape(shape)


def transport_kernel(winds, left, own, right, out):
    groups, count, twice = out.shape
    width = twice // 2
    pieces = width // LANES
    stride = own.shape[0] // count
    pairs = winds.shape[3] // width
    rows = 16
    y = lax.rem(lax.broadcasted_iota(jnp.int32, (4, width), 1), NY)

    def south(array):
        return pltpu.roll(array, 1, 1)

    def north(array):
        return pltpu.roll(array, width - 1, 1)

    def at_source(u, carry):
        for half in range(pairs):
            t = u * pairs + half
            lanes = slice(half * width, (half + 1) * width)
            east = winds[u, 0, 1:5, lanes]
            east_next = winds[u, 0, 2:6, lanes]
            upward = winds[u, 1, 1:5, lanes]
            upward_next = jnp.where(y == NY - 1, 0.0, north(upward))
            upward = jnp.where(y == 0, 0.0, upward)
            here = (
                1.0
                + jnp.minimum(east, 0.0)
                - jnp.maximum(east_next, 0.0)
                + jnp.minimum(upward, 0.0)
                - jnp.maximum(upward_next, 0.0)
            )
            west_of = jnp.maximum(east, 0.0)
            east_of = -jnp.minimum(east_next, 0.0)
            south_of = jnp.maximum(upward, 0.0)
            north_of = -jnp.minimum(upward_next, 0.0)

            def step(q, at, west, east):
                row = slice(at, at + 1)
                return (
                    here[row] * q
                    + west_of[row] * west
                    + east_of[row] * east
                    + south_of[row] * south(q)
                    + north_of[row] * north(q)
                )

            for first in range(0, count, rows):

                def column(ref, c):
                    start = first * stride + 2 * pieces * t + c
                    return jnp.concatenate(
                        [ref[pl.ds(start + 2 * m, rows, stride=stride), :] for m in range(pieces)], axis=1
                    )

                q = [column(ref, c) for ref in (left, own, right) for c in range(2)]
                q = [step(q[i + 1], i, q[i], q[i + 2]) for i in range(4)]
                for c in range(2):
                    out[t, first : first + rows, c * width : (c + 1) * width] = step(
                        q[c + 1], c + 1, q[c], q[c + 2]
                    )
        return carry

    lax.fori_loop(0, winds.shape[0], at_source, 0)


def transport(winds, left, own, right, shape):
    return pl.pallas_call(
        transport_kernel,
        in_specs=[VMEM] * 4,
        out_specs=VMEM,
        out_shape=jax.ShapeDtypeStruct(shape, F32),
        compiler_params=pltpu.CompilerParams(vmem_limit_bytes=32 << 20),
        name="transport",
    )(winds, left, own, right)


def join_kernel(*refs):
    *y_refs, x_ref = refs
    groups, rows, twice = y_refs[0].shape
    width = twice // 2
    pieces = width // LANES
    stride = x_ref.shape[0] // rows
    for chunk, y_ref in enumerate(y_refs):
        for t in range(groups):
            for c in range(2):
                for m in range(pieces):
                    at = chunk * (stride // CHUNKS) + 2 * (t * pieces + m) + c
                    lane = c * width + m * LANES
                    x_ref[pl.ds(at, rows, stride=stride), :] = y_ref[t, :, lane : lane + LANES]


def join(blocks, shape):
    own, cols, length = shape
    groups, _, twice = blocks[0].shape
    rows = own * cols * length // LANES
    steps = own // 8
    tiles = pl.pallas_call(
        join_kernel,
        grid=(steps,),
        in_specs=[pl.BlockSpec((groups, 8, twice), lambda i: (0, i, 0))] * CHUNKS,
        out_specs=pl.BlockSpec((rows // steps, LANES), lambda i: (i, 0)),
        out_shape=jax.ShapeDtypeStruct((rows, LANES), F32),
        name="join",
    )(*blocks)
    return from_tiles(tiles, shape)


def split(values):
    high = values.astype(BF16)
    low = (values - high.astype(F32)).astype(BF16)
    return jnp.concatenate([high, low], axis=0)


def react_kernel(cells, pick1, pick2, change, rates, out):
    amounts = cells[...]
    rate = jnp.concatenate([rates[...]] * (amounts.shape[1] // LANES), axis=1)
    for step in range(SUBSTEPS):
        parts = split(amounts)
        first = jnp.dot(pick1[...], parts, preferred_element_type=F32)
        second = jnp.dot(pick2[...], parts, preferred_element_type=F32)
        velocity = split(rate * first * second)
        amounts = amounts + jnp.dot(change[...], velocity, preferred_element_type=F32)
    out[...] = amounts


def react(cells, pick1, pick2, change, rates):
    return pl.pallas_call(
        react_kernel,
        in_specs=[VMEM] * 5,
        out_specs=VMEM,
        out_shape=jax.ShapeDtypeStruct(cells.shape, F32),
        compiler_params=pltpu.CompilerParams(vmem_limit_bytes=48 << 20),
        name="react",
    )(cells, pick1, pick2, change, rates)


def neighbours(array):
    count = lax.axis_size("region")
    left = lax.ppermute(array, "region", [(i, (i + 1) % count) for i in range(count)])
    right = lax.ppermute(array, "region", [((i + 1) % count, i) for i in range(count)])
    return left, right


def tables(first_reactant, second_reactant, product_species, rate_coeff):
    species = jnp.arange(2 * TRACERS, dtype=jnp.int32) % TRACERS
    pick1 = (first_reactant[:, None] == species[None, :]).astype(BF16)
    pick2 = (second_reactant[:, None] == species[None, :]).astype(BF16)
    kinds = jnp.arange(TRACERS, dtype=jnp.int32)[:, None]
    change = (
        (product_species[None, :] == kinds).astype(F32)
        - (first_reactant[None, :] == kinds).astype(F32)
        - (second_reactant[None, :] == kinds).astype(F32)
    ).astype(BF16)
    change = jnp.concatenate([change, change], axis=1)
    rates = jnp.broadcast_to(rate_coeff[:, None], (rate_coeff.shape[0], LANES))
    return pick1, pick2, change, rates


def exchange(blocks):
    return lax.all_to_all(blocks, "tracer", split_axis=0, concat_axis=0, tiled=True)


def body(tracers, fluxes, rate_coeff, first_reactant, second_reactant, product_species):
    groups = lax.axis_size("tracer")
    count, cols, length = tracers.shape
    width = length // groups // CHUNKS

    own = cut(as_tiles(tracers))
    left, right = neighbours(fluxes)
    winds = lax.all_gather(jnp.concatenate([left, fluxes, right], axis=1), "tracer")
    sides = [neighbours(array) for array in own]
    table = tables(first_reactant, second_reactant, product_species, rate_coeff)
    winds, table = lax.optimization_barrier((winds, table))

    per = groups // CHUNKS
    returned = []
    for k in range(CHUNKS):
        left, right = sides[k]
        moved = transport(
            winds[k * per : (k + 1) * per], left, own[k], right, (groups, count, cols * width)
        )
        cells = exchange(moved).reshape(groups * count, cols * width)
        reacted = react(cells, *table)
        returned.append(exchange(reacted.reshape(groups, count, cols * width)))
    return join(returned, tracers.shape)


def solution(mesh):
    in_specs = (P("tracer", "region", None), P(None, "region", "tracer"), P(), P(), P(), P())
    out_specs = P("tracer", "region", None)
    return jax.shard_map(body, mesh=mesh, in_specs=in_specs, out_specs=out_specs, check_vma=False)
```

profile of v0, /device:TPU:2, one launch (start us, length us, event | category | flops | bytes accessed | tf_op | source)
XLA Modules:
  0.0 131.6 jit_solution(9007791918895491017)
XLA Ops:
  0.0 0.0 collective-permute-start
  0.0 8.0 %collective-permute-start.1 = (f32[2,2,768]{2,1,0:T(2,128)}, f32[2,2,768]{2,1,0:T(2,128)S(1)}, u32[]{:S(2)}, u32[]{:S(2)}) collective-permute-start(f32[2,2,768]{2,1,0:T(2,128)} %param.7), channel_id=1, source_target_pairs={{8,0},{16,8},{24,16},{32,24},{40,32},{48,40},{56,48},{64,56},{72,6... | collective-permute-start | bytes 36872 | tf_op jit(solution)/shard_map/ppermute | solution.py:189
  8.0 3.6 %cut.1 = (f32[32,48,128]{2,1,0:T(8,128)}, f32[32,48,128]{2,1,0:T(8,128)}) custom-call(f32[32,96,128]{2,1,0:T(8,128)} %bitcast.22), custom_call_target="tpu_custom_call" | custom-call | tf_op jit(solution)/shard_map/cut/pallas_call | solution.py:33
  11.6 5.4 %collective-permute-start.5 = (f32[1536,128]{1,0:T(8,128)}, f32[1536,128]{1,0:T(8,128)S(1)}, u32[]{:S(2)}, u32[]{:S(2)}) collective-permute-start(f32[1536,128]{1,0:T(8,128)} %bitcast.20), channel_id=1, source_target_pairs={{8,0},{16,8},{24,16},{32,24},{40,32},{48,40},{56,48},{64,56},{72,6... | collective-permute-start | bytes 2359304 | tf_op jit(solution)/shard_map/ppermute | solution.py:189
  17.0 0.0 collective-permute-start.2
  17.0 0.7 compare_convert_fusion
  17.7 0.0 copy-start.9
  17.7 0.0 copy-start.11
  17.7 0.3 subtract_convert_fusion
  18.0 0.1 pad_maximum_fusion.change
  18.2 0.0 collective-permute-done
  18.2 5.4 %collective-permute-start.3 = (f32[1536,128]{1,0:T(8,128)}, f32[1536,128]{1,0:T(8,128)}, u32[]{:S(2)}, u32[]{:S(2)}) collective-permute-start(f32[1536,128]{1,0:T(8,128)} %bitcast.4.own), channel_id=1, source_target_pairs={{8,0},{16,8},{24,16},{32,24},{40,32},{48,40},{56,48},{64,56},{72,6... | collective-permute-start | bytes 2359304 | tf_op jit(solution)/shard_map/ppermute | solution.py:189
  23.6 28.5 %all-gather = f32[16,6,768]{2,1,0:T(8,128)S(1)} all-gather(f32[2,6,768]{2,1,0:T(8,128)S(1)} %pad_maximum_fusion.1), channel_id=2, replica_groups=mesh['region'=32,'tracer'=8] {'tracer'}, dimensions={0}, use_global_device_ids=true | all-gather | bytes 331776 | tf_op jit(solution)/shard_map/all_gather | solution.py:219
  52.1 1.0 broadcast_in_dim.2.rates
  53.2 2.2 %transport.3 = f32[8,32,768]{2,1,0:T(8,128)S(1)} custom-call(f32[4,2,6,768]{3,2,1,0:T(8,128)S(1)} %get-tuple-element.19.winds, f32[1536,128]{1,0:T(8,128)S(1)} %collective-permute-done.4.left, f32[1536,128]{1,0:T(8,128)S(1)} %bitcast.21, f32[1536,128]{1,0:T(8,128)S(1)} %collective-permute-done.5.right), custom_call_target="tpu_custom_call" | custom-call | tf_op jit(solution)/shard_map/transport/pallas_call | solution.py:116
  55.4 0.9 copy-done.4
  56.3 5.9 %all-to-all-start.2 = ((f32[8,32,768]{2,1,0:T(8,128)}), f32[8,32,768]{2,1,0:T(8,128)}, u32[]{:S(2)}, u32[]{:S(2)}) async-start(f32[8,32,768]{2,1,0:T(8,128)} %copy-done.4), calls=%async_computation.2 | async-start | bytes 1572864 | tf_op jit(solution)/shard_map/all_to_all | solution.py:209
  62.2 3.8 %transport.2 = f32[8,32,768]{2,1,0:T(8,128)S(1)} custom-call(f32[4,2,6,768]{3,2,1,0:T(8,128)S(1)} %get-tuple-element.20.winds, f32[1536,128]{1,0:T(8,128)} %collective-permute-done.2.left, f32[1536,128]{1,0:T(8,128)} %bitcast.4.own, f32[1536,128]{1,0:T(8,128)} %collective-permute-done.3.right), custom_call_target="tpu_custom_call" | custom-call | tf_op jit(solution)/shard_map/transport/pallas_call | solution.py:116
  66.0 0.0 copy-start.5
  66.0 0.9 copy-done.5
  66.9 6.9 %all-to-all-done.2 = f32[8,32,768]{2,1,0:T(8,128)} async-done(((f32[8,32,768]{2,1,0:T(8,128)}), f32[8,32,768]{2,1,0:T(8,128)}, u32[]{:S(2)}, u32[]{:S(2)}) %all-to-all-start.2) | async-done | bytes 786464 | tf_op jit(solution)/shard_map/all_to_all | solution.py:209
  73.8 6.5 %all-to-all-start = ((f32[8,32,768]{2,1,0:T(8,128)}), f32[8,32,768]{2,1,0:T(8,128)}, u32[]{:S(2)}, u32[]{:S(2)}) async-start(f32[8,32,768]{2,1,0:T(8,128)} %copy-done.5), calls=%async_computation | async-start | bytes 1572864 | tf_op jit(solution)/shard_map/all_to_all | solution.py:209
  80.3 1.0 copy-done
  81.3 11.5 %react.3 = f32[256,768]{1,0:T(8,128)S(1)} custom-call(f32[256,768]{1,0:T(8,128)} %bitcast.8.cells, bf16[1024,512]{1,0:T(8,128)(2,1)S(1)} %get-tuple-element.14.pick1, bf16[1024,512]{1,0:T(8,128)(2,1)S(1)} %get-tuple-element.15.pick2, bf16[256,2048]{1,0:T(8,128)(2,1)S(1)} %pad_maximum_fusion.change, f32[1024,128]{1,0:T(8,128)S(1)} %copy-done), custom_call_target="tpu_custom_call" | custom-call | tf_op jit(solution)/shard_map/react/pallas_call | solution.py:176
  92.8 0.9 copy-done.2
  93.7 5.7 %all-to-all-start.3 = ((f32[8,32,768]{2,1,0:T(8,128)}), f32[8,32,768]{2,1,0:T(8,128)}, u32[]{:S(2)}, u32[]{:S(2)}) async-start(f32[8,32,768]{2,1,0:T(8,128)} %bitcast.17), calls=%async_computation.3 | async-start | bytes 1572864 | tf_op jit(solution)/shard_map/all_to_all | solution.py:209
  99.4 1.0 copy-done.1
  100.5 11.5 %react.2 = f32[256,768]{1,0:T(8,128)S(1)} custom-call(f32[256,768]{1,0:T(8,128)} %bitcast.5.cells, bf16[1024,512]{1,0:T(8,128)(2,1)S(1)} %get-tuple-element.14.pick1, bf16[1024,512]{1,0:T(8,128)(2,1)S(1)} %get-tuple-element.15.pick2, bf16[256,2048]{1,0:T(8,128)(2,1)S(1)} %pad_maximum_fusion.change, f32[1024,128]{1,0:T(8,128)S(1)} %copy-done.1), custom_call_target="tpu_custom_call" | custom-call | tf_op jit(solution)/shard_map/react/pallas_call | solution.py:176
  112.0 0.0 copy-start.3
  112.0 0.9 copy-done.3
  112.8 14.7 %all_to_all.20.refs_0_ = f32[8,32,768]{2,1,0:T(8,128)} all-to-all(f32[8,32,768]{2,1,0:T(8,128)} %bitcast.18), channel_id=1, replica_groups=mesh['region'=32,'tracer'=8] {'tracer'}, dimensions={0} | all-to-all | bytes 1572864 | tf_op jit(solution)/shard_map/all_to_all | solution.py:209
  127.6 4.0 %join.1 = f32[3072,128]{1,0:T(8,128)} custom-call(f32[8,32,768]{2,1,0:T(8,128)} %all_to_all.20.refs_0_, f32[8,32,768]{2,1,0:T(8,128)} %all-to-all-done.3.refs_1_), custom_call_target="tpu_custom_call" | custom-call | tf_op jit(solution)/shard_map/join/pallas_call | solution.py:146
  (25 shorter events, 0.1 us)
Async XLA Ops:
  0.0 17.0 %copy-start.7 = (s32[1024]{0:T(1024)S(1)}, s32[1024]{0:T(1024)}, u32[]{:S(2)}) copy-start(s32[1024]{0:T(1024)} %param.10) | copy-start | bytes 12292
  0.0 17.0 %copy-start.8 = (s32[1024]{0:T(1024)S(1)}, s32[1024]{0:T(1024)}, u32[]{:S(2)}) copy-start(s32[1024]{0:T(1024)} %param.9) | copy-start | bytes 12292
  0.0 18.2 %collective-permute-start = (f32[2,2,768]{2,1,0:T(2,128)}, f32[2,2,768]{2,1,0:T(2,128)S(1)}, u32[]{:S(2)}, u32[]{:S(2)}) collective-permute-start(f32[2,2,768]{2,1,0:T(2,128)} %param.7), channel_id=1, source_target_pairs={{0,8},{8,16},{16,24},{24,32},{32,40},{40,48},{48,56},{56,64},{64,7... | collective-permute-start | bytes 36872 | tf_op jit(solution)/shard_map/ppermute | solution.py:188
  0.0 23.6 %collective-permute-start.1 = (f32[2,2,768]{2,1,0:T(2,128)}, f32[2,2,768]{2,1,0:T(2,128)S(1)}, u32[]{:S(2)}, u32[]{:S(2)}) collective-permute-start(f32[2,2,768]{2,1,0:T(2,128)} %param.7), channel_id=1, source_target_pairs={{8,0},{16,8},{24,16},{32,24},{40,32},{48,40},{56,48},{64,56},{72,6... | collective-permute-start | bytes 36872 | tf_op jit(solution)/shard_map/ppermute | solution.py:189
  8.0 9.6 %copy-start.10 = (s32[1024]{0:T(1024)S(1)}, s32[1024]{0:T(1024)}, u32[]{:S(2)}) copy-start(s32[1024]{0:T(1024)} %param.11) | copy-start | bytes 12292
  11.6 41.6 %collective-permute-start.4 = (f32[1536,128]{1,0:T(8,128)}, f32[1536,128]{1,0:T(8,128)S(1)}, u32[]{:S(2)}, u32[]{:S(2)}) collective-permute-start(f32[1536,128]{1,0:T(8,128)} %bitcast.19), channel_id=1, source_target_pairs={{0,8},{8,16},{16,24},{24,32},{32,40},{40,48},{48,56},{56,64},{64,7... | collective-permute-start | bytes 2359304 | tf_op jit(solution)/shard_map/ppermute | solution.py:188
  11.6 41.6 %collective-permute-start.5 = (f32[1536,128]{1,0:T(8,128)}, f32[1536,128]{1,0:T(8,128)S(1)}, u32[]{:S(2)}, u32[]{:S(2)}) collective-permute-start(f32[1536,128]{1,0:T(8,128)} %bitcast.20), channel_id=1, source_target_pairs={{8,0},{16,8},{24,16},{32,24},{40,32},{48,40},{56,48},{64,56},{72,6... | collective-permute-start | bytes 2359304 | tf_op jit(solution)/shard_map/ppermute | solution.py:189
  17.0 45.2 %collective-permute-start.2 = (f32[1536,128]{1,0:T(8,128)}, f32[1536,128]{1,0:T(8,128)}, u32[]{:S(2)}, u32[]{:S(2)}) collective-permute-start(f32[1536,128]{1,0:T(8,128)} %bitcast.4.own), channel_id=1, source_target_pairs={{0,8},{8,16},{16,24},{24,32},{32,40},{40,48},{48,56},{56,64},{64,7... | collective-permute-start | bytes 2359304 | tf_op jit(solution)/shard_map/ppermute | solution.py:188
  17.7 5.9 %copy-start.9 = (f32[2,2,768]{2,1,0:T(2,128)S(1)}, f32[2,2,768]{2,1,0:T(2,128)}, u32[]{:S(2)}) copy-start(f32[2,2,768]{2,1,0:T(2,128)} %param.7) | copy-start | bytes 36868
  17.7 34.4 %copy-start.11 = (f32[1024]{0:T(1024)S(1)}, f32[1024]{0:T(1024)}, u32[]{:S(2)}) copy-start(f32[1024]{0:T(1024)} %param.8) | copy-start | bytes 12292
  18.0 35.1 %copy-start.6 = (f32[32,48,128]{2,1,0:T(8,128)S(1)}, f32[32,48,128]{2,1,0:T(8,128)}, u32[]{:S(2)}) copy-start(f32[32,48,128]{2,1,0:T(8,128)} %get-tuple-element.18) | copy-start | bytes 2359300
  18.2 44.0 %collective-permute-start.3 = (f32[1536,128]{1,0:T(8,128)}, f32[1536,128]{1,0:T(8,128)}, u32[]{:S(2)}, u32[]{:S(2)}) collective-permute-start(f32[1536,128]{1,0:T(8,128)} %bitcast.4.own), channel_id=1, source_target_pairs={{8,0},{16,8},{24,16},{32,24},{40,32},{48,40},{56,48},{64,56},{72,6... | collective-permute-start | bytes 2359304 | tf_op jit(solution)/shard_map/ppermute | solution.py:189
  55.4 0.9 copy-start.4
  56.3 17.5 %all-to-all-start.2 = ((f32[8,32,768]{2,1,0:T(8,128)}), f32[8,32,768]{2,1,0:T(8,128)}, u32[]{:S(2)}, u32[]{:S(2)}) async-start(f32[8,32,768]{2,1,0:T(8,128)} %copy-done.4), calls=%async_computation.2 | async-start | bytes 1572864 | tf_op jit(solution)/shard_map/all_to_all | solution.py:209
  66.0 0.9 copy-start.5
  73.8 19.9 %all-to-all-start = ((f32[8,32,768]{2,1,0:T(8,128)}), f32[8,32,768]{2,1,0:T(8,128)}, u32[]{:S(2)}, u32[]{:S(2)}) async-start(f32[8,32,768]{2,1,0:T(8,128)} %copy-done.5), calls=%async_computation | async-start | bytes 1572864 | tf_op jit(solution)/shard_map/all_to_all | solution.py:209
  80.3 1.0 copy-start
  92.8 0.9 copy-start.2
  93.7 19.1 %all-to-all-start.3 = ((f32[8,32,768]{2,1,0:T(8,128)}), f32[8,32,768]{2,1,0:T(8,128)}, u32[]{:S(2)}, u32[]{:S(2)}) async-start(f32[8,32,768]{2,1,0:T(8,128)} %bitcast.17), calls=%async_computation.3 | async-start | bytes 1572864 | tf_op jit(solution)/shard_map/all_to_all | solution.py:209
  99.4 1.0 copy-start.1
  112.0 0.9 copy-start.3
where the time goes:
time: 132 us
  blocking collectives  43.2 us (33%)
  starting transfers between devices  36.9 us (28%)
  Pallas kernels  36.6 us (28%)
  waiting for transfers between devices  6.93 us (5%)
  local copies, waits for them, and re-layouts  6.65 us (5%)
    all_gather x1, blocking collectives, body(): lax.all_gather(jnp.concatenate([left, fluxes, right], axis=1), 'tracer')  28.5 us
    pallas_call x2, Pallas kernels, react(): pl.pallas_call(react_kernel, in_specs=[VMEM] * 5, out_specs=VMEM, out_sha...  23 us
    ppermute x3, starting transfers between devices, neighbours(): lax.ppermute(array, 'region', [((i + 1) % count, i) for i in range(count)])  18.8 us
    all_to_all x3, starting transfers between devices, exchange(): lax.all_to_all(blocks, 'tracer', split_axis=0, concat_axis=0, tiled=True)  18.1 us
    all_to_all x1, blocking collectives, exchange(): lax.all_to_all(blocks, 'tracer', split_axis=0, concat_axis=0, tiled=True)  14.7 us
    all_to_all x3, waiting for transfers between devices, exchange(): lax.all_to_all(blocks, 'tracer', split_axis=0, concat_axis=0, tiled=True)  6.91 us
    pallas_call x2, Pallas kernels, transport(): pl.pallas_call(transport_kernel, in_specs=[VMEM] * 4, out_specs=VMEM, out...  6.02 us
    unnamed x24, local copies, waits for them, and re-layouts  5.62 us
  transfers between devices with their start and end apart: 9, of which 1 were waited for; matrix products, arithmetic and copies ran while one was open for 2% of the time, Pallas kernels for 25%

commit v1 on v0

v1 whole, which is shorter than its diff:
```python
import functools

import jax
import jax.numpy as jnp
from jax import lax
from jax.experimental import pallas as pl
from jax.experimental.pallas import tpu as pltpu
from jax.sharding import PartitionSpec as P

TRACERS = 256
NY = 48
SUBSTEPS = 4
LANES = 128
CHUNKS = 2
F32 = jnp.float32
BF16 = jnp.bfloat16
VMEM = pl.BlockSpec(memory_space=pltpu.VMEM)


def as_tiles(tracers):
    own, cols, length = tracers.shape
    tiles = tracers.reshape(own, cols, length // LANES, LANES)
    return jnp.transpose(tiles, (0, 2, 1, 3)).reshape(-1, LANES)


def from_tiles(tiles, shape):
    own, cols, length = shape
    tiles = tiles.reshape(own, length // LANES, cols, LANES)
    return jnp.transpose(tiles, (0, 2, 1, 3)).reshape(shape)


def transport_kernel(chunk, before, winds, after, left, own, right, out):
    pairs, count, twice = out.shape
    width = twice // 2
    pieces = width // LANES
    stride = own.shape[0] // count
    rows = 16
    y = lax.rem(lax.broadcasted_iota(jnp.int32, (4, width), 1), NY)
    u = pl.program_id(0)
    source = u + chunk * pl.num_programs(0)

    def south(array):
        return pltpu.roll(array, 1, 1)

    def north(array):
        return pltpu.roll(array, width - 1, 1)

    for half in range(pairs):
        t = u * pairs + half
        lanes = slice(half * width, (half + 1) * width)

        def around(kind, first):
            faces = [
                before[source, kind, 1:2, lanes],
                winds[source, kind, 0:2, lanes],
                after[source, kind, 0:2, lanes],
            ]
            return jnp.concatenate(faces, axis=0)[first : first + 4]

        east = around(0, 0)
        east_next = around(0, 1)
        upward = around(1, 0)
        upward_next = jnp.where(y == NY - 1, 0.0, north(upward))
        upward = jnp.where(y == 0, 0.0, upward)
        here = (
            1.0
            + jnp.minimum(east, 0.0)
            - jnp.maximum(east_next, 0.0)
            + jnp.minimum(upward, 0.0)
            - jnp.maximum(upward_next, 0.0)
        )
        west_of = jnp.maximum(east, 0.0)
        east_of = -jnp.minimum(east_next, 0.0)
        south_of = jnp.maximum(upward, 0.0)
        north_of = -jnp.minimum(upward_next, 0.0)

        def step(q, at, west, east):
            row = slice(at, at + 1)
            return (
                here[row] * q
                + west_of[row] * west
                + east_of[row] * east
                + south_of[row] * south(q)
                + north_of[row] * north(q)
            )

        for first in range(0, count, rows):

            def column(ref, c):
                start = first * stride + 2 * pieces * t + c
                return jnp.concatenate(
                    [ref[pl.ds(start + 2 * m, rows, stride=stride), :] for m in range(pieces)], axis=1
                )

            q = [column(ref, c) for ref in (left, own, right) for c in range(2)]
            q = [step(q[i + 1], i, q[i], q[i + 2]) for i in range(4)]
            for c in range(2):
                out[half, first : first + rows, c * width : (c + 1) * width] = step(
                    q[c + 1], c + 1, q[c], q[c + 2]
                )


def transport(chunk, winds, left, own, right, shape):
    groups, count, twice = shape
    steps = groups // CHUNKS
    return pl.pallas_call(
        functools.partial(transport_kernel, chunk),
        grid=(steps,),
        in_specs=[VMEM] * 6,
        out_specs=pl.BlockSpec((groups // steps, count, twice), lambda u: (u, 0, 0)),
        out_shape=pltpu.HBM(shape, F32),
        compiler_params=pltpu.CompilerParams(vmem_limit_bytes=16 << 20),
        name="transport",
    )(*winds, left, own, right)


def join_kernel(y_ref, *refs):
    x_ref = refs[-1]
    groups, _, twice = y_ref.shape
    rows = x_ref.shape[0]
    at = pl.ds(pl.multiple_of(pl.program_id(0) * rows, rows), rows)
    width = twice // 2
    pieces = width // LANES
    stride = x_ref.shape[1]
    flat = x_ref.reshape(rows * stride, LANES)
    for t in range(groups):
        for c in range(2):
            for m in range(pieces):
                lane = c * width + m * LANES
                flat[pl.ds(2 * (t * pieces + m) + c, rows, stride=stride), :] = y_ref[t, at, lane : lane + LANES]


def join(blocks, so_far, chunk):
    groups, own, twice = blocks.shape
    length = groups * twice // LANES
    more = [] if so_far is None else [so_far]
    return pl.pallas_call(
        join_kernel,
        grid=(own // 8,),
        in_specs=[VMEM]
        + [pl.BlockSpec(memory_space=pl.ANY)] * len(more),
        out_specs=pl.BlockSpec((8, length, LANES), lambda i: (i, chunk, 0)),
        out_shape=jax.ShapeDtypeStruct((own, CHUNKS * length, LANES), F32),
        input_output_aliases={1: 0} if more else {},
        name="join",
    )(blocks, *more)


def split(values):
    high = values.astype(BF16)
    low = (values - high.astype(F32)).astype(BF16)
    return jnp.concatenate([high, low], axis=0)


def react_kernel(cells, pick1, pick2, change, rates, out):
    amounts = cells[...]
    rate = jnp.concatenate(
        [jnp.broadcast_to(rates[i : i + 1, :], (LANES, LANES)).T for i in range(rates.shape[0])], axis=0
    )
    rate = jnp.concatenate([rate] * (amounts.shape[1] // LANES), axis=1)
    for step in range(SUBSTEPS):
        parts = split(amounts)
        first = jnp.dot(pick1[...], parts, preferred_element_type=F32)
        second = jnp.dot(pick2[...], parts, preferred_element_type=F32)
        velocity = split(rate * first * second)
        amounts = amounts + jnp.dot(change[...], velocity, preferred_element_type=F32)
    out[...] = amounts


def react(cells, pick1, pick2, change, rates):
    return pl.pallas_call(
        react_kernel,
        in_specs=[VMEM] * 5,
        out_specs=VMEM,
        out_shape=jax.ShapeDtypeStruct(cells.shape, F32),
        compiler_params=pltpu.CompilerParams(vmem_limit_bytes=24 << 20),
        name="react",
    )(cells, pick1, pick2, change, rates)


def neighbours(array):
    count = lax.axis_size("region")
    left = lax.ppermute(array, "region", [(i, (i + 1) % count) for i in range(count)])
    right = lax.ppermute(array, "region", [((i + 1) % count, i) for i in range(count)])
    return left, right


def tables(first_reactant, second_reactant, product_species, rate_coeff):
    species = jnp.arange(2 * TRACERS, dtype=jnp.int32) % TRACERS
    pick1 = (first_reactant[:, None] == species[None, :]).astype(BF16)
    pick2 = (second_reactant[:, None] == species[None, :]).astype(BF16)
    kinds = jnp.arange(TRACERS, dtype=jnp.int32)[:, None]
    change = (
        (product_species[None, :] == kinds).astype(F32)
        - (first_reactant[None, :] == kinds).astype(F32)
        - (second_reactant[None, :] == kinds).astype(F32)
    ).astype(BF16)
    change = jnp.concatenate([change, change], axis=1)
    return pick1, pick2, change, rate_coeff.reshape(-1, LANES)


def exchange(blocks):
    return lax.all_to_all(blocks, "tracer", split_axis=0, concat_axis=0, tiled=True)


def body(tracers, fluxes, rate_coeff, first_reactant, second_reactant, product_species):
    groups = lax.axis_size("tracer")
    count, cols, length = tracers.shape
    width = length // groups // CHUNKS

    part = length // CHUNKS
    own = [as_tiles(lax.slice_in_dim(tracers, k * part, (k + 1) * part, axis=2)) for k in range(CHUNKS)]
    section = exchange(jnp.broadcast_to(fluxes, (groups, *fluxes.shape)))
    before, after = neighbours(section)
    winds = (before, section, after)
    sides = [neighbours(array) for array in own]
    table = tables(first_reactant, second_reactant, product_species, rate_coeff)
    winds, table = lax.optimization_barrier((winds, table))

    out = None
    for k in range(CHUNKS):
        left, right = sides[k]
        moved = transport(k, winds, left, own[k], right, (groups, count, cols * width))
        cells = exchange(moved).reshape(groups * count, cols * width)
        reacted = react(cells, *table)
        back = exchange(reacted.reshape(groups, count, cols * width))
        out = join(back, out, k)
    return from_tiles(out, tracers.shape)


def solution(mesh):
    in_specs = (P("tracer", "region", None), P(None, "region", "tracer"), P(), P(), P(), P())
    out_specs = P("tracer", "region", None)
    return jax.shard_map(body, mesh=mesh, in_specs=in_specs, out_specs=out_specs, check_vma=False)
```

time: 132 us -> 118 us (0.89)
  the two profiles are of different devices: /device:TPU:2 before, /device:TPU:1 now
where the time goes in v1:
time: 118 us; the launch traced here: 117 us
  starting transfers between devices  38.3 us (32%)
  Pallas kernels  37.7 us (32%)
  waiting for transfers between devices  33.7 us (29%)
  local copies, waits for them, and re-layouts  5.95 us (5%)
    all_to_all x5, waiting for transfers between devices, exchange(): lax.all_to_all(blocks, 'tracer', split_axis=0, concat_axis=0, tiled=True)  31.6 us
    pallas_call x2, Pallas kernels, react(): pl.pallas_call(react_kernel, in_specs=[VMEM] * 5, out_specs=VMEM, out_sha...  23 us
    all_to_all x5, starting transfers between devices, exchange(): lax.all_to_all(blocks, 'tracer', split_axis=0, concat_axis=0, tiled=True)  21.6 us
    ppermute x3, starting transfers between devices, neighbours(): lax.ppermute(array, 'region', [((i + 1) % count, i) for i in range(count)])  12.1 us
    pallas_call x2, Pallas kernels, transport(): pl.pallas_call(functools.partial(transport_kernel, chunk), grid=(steps,),...  9.37 us
    pallas_call x2, Pallas kernels, join(): pl.pallas_call(join_kernel, grid=(own // 8,), in_specs=[VMEM] + [pl.Block...  5.37 us
    ppermute x3, starting transfers between devices, neighbours(): lax.ppermute(array, 'region', [(i, (i + 1) % count) for i in range(count)])  4.56 us
    slice x1, local copies, waits for them, and re-layouts, body(): lax.slice_in_dim(tracers, k * part, (k + 1) * part, axis=2)  2.64 us
  transfers between devices with their start and end apart: 11, of which 7 were waited for; matrix products, arithmetic and copies ran while one was open for 2% of the time, Pallas kernels for 30%

profile of v1, /device:TPU:1, one launch (start us, length us, event | category | flops | bytes accessed | tf_op | source)
XLA Modules:
  0.0 116.9 jit_solution(15337106952135491501)
XLA Ops:
  0.0 2.6 %fusion.3 = (f32[32,2,3072]{2,1,0:T(2,128)}, f32[32,2,3072]{2,1,0:T(2,128)}) fusion(f32[32,2,6144]{2,1,0:T(2,128)} %param.6), kind=kLoop, calls=%fused_computation.12 | loop fusion | bytes 3145728 | tf_op jit(solution)/shard_map/slice | solution.py:212
  2.7 3.0 %collective-permute-start.2 = (f32[1536,128]{1,0:T(8,128)}, f32[1536,128]{1,0:T(8,128)}, u32[]{:S(2)}, u32[]{:S(2)}) collective-permute-start(f32[1536,128]{1,0:T(8,128)} %bitcast.3.own), channel_id=1, source_target_pairs={{0,8},{8,16},{16,24},{24,32},{32,40},{40,48},{48,56},{56,64},{64,7... | collective-permute-start | bytes 2359304 | tf_op jit(solution)/shard_map/ppermute | solution.py:183
  5.7 0.2 collective-permute-start.3
  5.9 1.5 %collective-permute-start.4 = (f32[1536,128]{1,0:T(8,128)}, f32[1536,128]{1,0:T(8,128)}, u32[]{:S(2)}, u32[]{:S(2)}) collective-permute-start(f32[1536,128]{1,0:T(8,128)} %bitcast.10.own), channel_id=1, source_target_pairs={{0,8},{8,16},{16,24},{24,32},{32,40},{40,48},{48,56},{56,64},{64,7... | collective-permute-start | bytes 2359304 | tf_op jit(solution)/shard_map/ppermute | solution.py:183
  7.4 4.7 %collective-permute-start.5 = (f32[1536,128]{1,0:T(8,128)}, f32[1536,128]{1,0:T(8,128)}, u32[]{:S(2)}, u32[]{:S(2)}) collective-permute-start(f32[1536,128]{1,0:T(8,128)} %bitcast.10.own), channel_id=1, source_target_pairs={{8,0},{16,8},{24,16},{32,24},{40,32},{48,40},{56,48},{64,56},{72,6... | collective-permute-start | bytes 2359304 | tf_op jit(solution)/shard_map/ppermute | solution.py:184
  12.1 0.7 broadcast_in_dim.2
  12.8 4.1 %all-to-all-start = ((f32[8,2,2,768]{3,2,1,0:T(2,128)}), f32[8,2,2,768]{3,2,1,0:T(2,128)S(1)}, u32[]{:S(2)}, u32[]{:S(2)}) async-start(f32[8,2,2,768]{3,2,1,0:T(2,128)} %broadcast_in_dim.2), calls=%async_computation | async-start | bytes 196608 | tf_op jit(solution)/shard_map/all_to_all | solution.py:203
  16.9 0.7 compare_convert_fusion
  17.6 11.8 %all-to-all-done.winds = f32[8,2,2,768]{3,2,1,0:T(2,128)S(1)} async-done(((f32[8,2,2,768]{3,2,1,0:T(2,128)}), f32[8,2,2,768]{3,2,1,0:T(2,128)S(1)}, u32[]{:S(2)}, u32[]{:S(2)}) %all-to-all-start) | async-done | bytes 98336 | tf_op jit(solution)/shard_map/all_to_all | solution.py:203
  29.4 0.0 collective-permute-start
  29.4 0.3 subtract_convert_fusion
  29.8 1.3 %collective-permute-done.before = f32[8,2,2,768]{3,2,1,0:T(2,128)S(1)} collective-permute-done((f32[8,2,2,768]{3,2,1,0:T(2,128)S(1)}, f32[8,2,2,768]{3,2,1,0:T(2,128)S(1)}, u32[]{:S(2)}, u32[]{:S(2)}) %collective-permute-start) | collective-permute-done | bytes 98336 | tf_op jit(solution)/shard_map/ppermute | solution.py:183
  31.1 7.3 %collective-permute-start.1 = (f32[8,2,2,768]{3,2,1,0:T(2,128)S(1)}, f32[8,2,2,768]{3,2,1,0:T(2,128)S(1)}, u32[]{:S(2)}, u32[]{:S(2)}) collective-permute-start(f32[8,2,2,768]{3,2,1,0:T(2,128)S(1)} %all-to-all-done.winds), channel_id=1, source_target_pairs={{8,0},{16,8},{24,16},{32,24},{40,32},{48,40},{56,48},{64,56},{72,6... | collective-permute-start | bytes 294920 | tf_op jit(solution)/shard_map/ppermute | solution.py:184
  38.3 0.1 pad_maximum_fusion.change
  38.5 0.8 collective-permute-done.1.after
  39.3 4.7 %transport.3 = f32[8,32,768]{2,1,0:T(8,128)} custom-call(f32[8,2,2,768]{3,2,1,0:T(2,128)S(1)} %collective-permute-done.before, f32[8,2,2,768]{3,2,1,0:T(2,128)S(1)} %all-to-all-done.winds, f32[8,2,2,768]{3,2,1,0:T(2,128)S(1)} %collective-permute-done.1.after, f32[1536,128]{1,0:T(8,128)} %collective-permute-done.4.left, f32[1536,128]{1,0:T(8,128)} %bitcast.10.own, ...), custom_call_target="tpu_custom_call" | custom-call | tf_op jit(solution)/shard_map/transport/pallas_call | solution.py:106
  44.0 4.2 %all-to-all-start.3 = ((f32[8,32,768]{2,1,0:T(8,128)}), f32[8,32,768]{2,1,0:T(8,128)}, u32[]{:S(2)}, u32[]{:S(2)}) async-start(f32[8,32,768]{2,1,0:T(8,128)} %transport.3), calls=%async_computation.3 | async-start | bytes 1572864 | tf_op jit(solution)/shard_map/all_to_all | solution.py:203
  48.2 4.7 %transport.2 = f32[8,32,768]{2,1,0:T(8,128)} custom-call(f32[8,2,2,768]{3,2,1,0:T(2,128)S(1)} %collective-permute-done.before, f32[8,2,2,768]{3,2,1,0:T(2,128)S(1)} %all-to-all-done.winds, f32[8,2,2,768]{3,2,1,0:T(2,128)S(1)} %collective-permute-done.1.after, f32[1536,128]{1,0:T(8,128)} %collective-permute-done.2.left, f32[1536,128]{1,0:T(8,128)} %bitcast.3.own, ...), custom_call_target="tpu_custom_call" | custom-call | tf_op jit(solution)/shard_map/transport/pallas_call | solution.py:106
  52.9 8.3 %all-to-all-done.3 = f32[8,32,768]{2,1,0:T(8,128)} async-done(((f32[8,32,768]{2,1,0:T(8,128)}), f32[8,32,768]{2,1,0:T(8,128)}, u32[]{:S(2)}, u32[]{:S(2)}) %all-to-all-start.3) | async-done | bytes 786464 | tf_op jit(solution)/shard_map/all_to_all | solution.py:203
  61.2 4.4 %all-to-all-start.1 = ((f32[8,32,768]{2,1,0:T(8,128)}), f32[8,32,768]{2,1,0:T(8,128)}, u32[]{:S(2)}, u32[]{:S(2)}) async-start(f32[8,32,768]{2,1,0:T(8,128)} %transport.2), calls=%async_computation.1 | async-start | bytes 1572864 | tf_op jit(solution)/shard_map/all_to_all | solution.py:203
  65.6 11.5 %react.3 = f32[256,768]{1,0:T(8,128)S(1)} custom-call(f32[256,768]{1,0:T(8,128)} %bitcast.13.cells, bf16[1024,512]{1,0:T(8,128)(2,1)S(1)} %get-tuple-element.15.pick1, bf16[1024,512]{1,0:T(8,128)(2,1)S(1)} %get-tuple-element.16.pick2, bf16[256,2048]{1,0:T(8,128)(2,1)S(1)} %pad_maximum_fusion.change, f32[8,128]{1,0:T(8,128)S(1)} %bitcast.22), custom_call_target="tpu_custom_call" | custom-call | tf_op jit(solution)/shard_map/react/pallas_call | solution.py:171
  77.1 0.9 copy-done
  78.0 0.5 all-to-all-done.1
  78.5 4.4 %all-to-all-start.4 = ((f32[8,32,768]{2,1,0:T(8,128)}), f32[8,32,768]{2,1,0:T(8,128)}, u32[]{:S(2)}, u32[]{:S(2)}) async-start(f32[8,32,768]{2,1,0:T(8,128)} %bitcast.20), calls=%async_computation.4 | async-start | bytes 1572864 | tf_op jit(solution)/shard_map/all_to_all | solution.py:203
  82.9 11.5 %react.2 = f32[256,768]{1,0:T(8,128)S(1)} custom-call(f32[256,768]{1,0:T(8,128)} %bitcast.6.cells, bf16[1024,512]{1,0:T(8,128)(2,1)S(1)} %get-tuple-element.15.pick1, bf16[1024,512]{1,0:T(8,128)(2,1)S(1)} %get-tuple-element.16.pick2, bf16[256,2048]{1,0:T(8,128)(2,1)S(1)} %pad_maximum_fusion.change, f32[8,128]{1,0:T(8,128)S(1)} %bitcast.23), custom_call_target="tpu_custom_call" | custom-call | tf_op jit(solution)/shard_map/react/pallas_call | solution.py:171
  94.4 0.9 copy-done.1
  95.3 0.7 all-to-all-done.4.y_ref
  96.0 4.4 %all-to-all-start.2 = ((f32[8,32,768]{2,1,0:T(8,128)}), f32[8,32,768]{2,1,0:T(8,128)S(1)}, u32[]{:S(2)}, u32[]{:S(2)}) async-start(f32[8,32,768]{2,1,0:T(8,128)} %bitcast.21), calls=%async_computation.2 | async-start | bytes 1572864 | tf_op jit(solution)/shard_map/all_to_all | solution.py:203
  100.4 2.7 %join.2.refs_0_ = f32[32,96,128]{2,1,0:T(8,128)} custom-call(f32[8,32,768]{2,1,0:T(8,128)} %all-to-all-done.4.y_ref), custom_call_target="tpu_custom_call" | custom-call | tf_op jit(solution)/shard_map/join/pallas_call | solution.py:137
  103.1 10.3 %all-to-all-done.2.y_ref = f32[8,32,768]{2,1,0:T(8,128)S(1)} async-done(((f32[8,32,768]{2,1,0:T(8,128)}), f32[8,32,768]{2,1,0:T(8,128)S(1)}, u32[]{:S(2)}, u32[]{:S(2)}) %all-to-all-start.2) | async-done | bytes 786464 | tf_op jit(solution)/shard_map/all_to_all | solution.py:203
  113.4 0.9 copy-done.3
  114.2 2.7 %join.3 = f32[32,96,128]{2,1,0:T(8,128)} custom-call(f32[8,32,768]{2,1,0:T(8,128)} %copy-done.3, f32[32,96,128]{2,1,0:T(8,128)} %join.2.refs_0_), custom_call_target="tpu_custom_call", output_to_operand_aliasing={{}: (1, {})} | custom-call | tf_op jit(solution)/shard_map/join/pallas_call | solution.py:137
  (18 shorter events, 0.0 us)
Async XLA Ops:
  0.0 12.1 %copy-start.6 = (f32[2,2,768]{2,1,0:T(2,128)S(1)}, f32[2,2,768]{2,1,0:T(2,128)}, u32[]{:S(2)}) copy-start(f32[2,2,768]{2,1,0:T(2,128)} %param.7) | copy-start | bytes 36868
  0.0 16.9 %copy-start.4 = (s32[1024]{0:T(1024)S(1)}, s32[1024]{0:T(1024)}, u32[]{:S(2)}) copy-start(s32[1024]{0:T(1024)} %param.10) | copy-start | bytes 12292
  0.0 16.9 %copy-start.5 = (s32[1024]{0:T(1024)S(1)}, s32[1024]{0:T(1024)}, u32[]{:S(2)}) copy-start(s32[1024]{0:T(1024)} %param.9) | copy-start | bytes 12292
  2.7 26.8 %copy-start.7 = (s32[1024]{0:T(1024)S(1)}, s32[1024]{0:T(1024)}, u32[]{:S(2)}) copy-start(s32[1024]{0:T(1024)} %param.11) | copy-start | bytes 12292
  2.7 45.6 %collective-permute-start.2 = (f32[1536,128]{1,0:T(8,128)}, f32[1536,128]{1,0:T(8,128)}, u32[]{:S(2)}, u32[]{:S(2)}) collective-permute-start(f32[1536,128]{1,0:T(8,128)} %bitcast.3.own), channel_id=1, source_target_pairs={{0,8},{8,16},{16,24},{24,32},{32,40},{40,48},{48,56},{56,64},{64,7... | collective-permute-start | bytes 2359304 | tf_op jit(solution)/shard_map/ppermute | solution.py:183
  5.7 42.5 %collective-permute-start.3 = (f32[1536,128]{1,0:T(8,128)}, f32[1536,128]{1,0:T(8,128)}, u32[]{:S(2)}, u32[]{:S(2)}) collective-permute-start(f32[1536,128]{1,0:T(8,128)} %bitcast.3.own), channel_id=1, source_target_pairs={{8,0},{16,8},{24,16},{32,24},{40,32},{48,40},{56,48},{64,56},{72,6... | collective-permute-start | bytes 2359304 | tf_op jit(solution)/shard_map/ppermute | solution.py:184
  5.9 33.4 %collective-permute-start.4 = (f32[1536,128]{1,0:T(8,128)}, f32[1536,128]{1,0:T(8,128)}, u32[]{:S(2)}, u32[]{:S(2)}) collective-permute-start(f32[1536,128]{1,0:T(8,128)} %bitcast.10.own), channel_id=1, source_target_pairs={{0,8},{8,16},{16,24},{24,32},{32,40},{40,48},{48,56},{56,64},{64,7... | collective-permute-start | bytes 2359304 | tf_op jit(solution)/shard_map/ppermute | solution.py:183
  7.4 31.9 %collective-permute-start.5 = (f32[1536,128]{1,0:T(8,128)}, f32[1536,128]{1,0:T(8,128)}, u32[]{:S(2)}, u32[]{:S(2)}) collective-permute-start(f32[1536,128]{1,0:T(8,128)} %bitcast.10.own), channel_id=1, source_target_pairs={{8,0},{16,8},{24,16},{32,24},{40,32},{48,40},{56,48},{64,56},{72,6... | collective-permute-start | bytes 2359304 | tf_op jit(solution)/shard_map/ppermute | solution.py:184
  12.8 16.7 %all-to-all-start = ((f32[8,2,2,768]{3,2,1,0:T(2,128)}), f32[8,2,2,768]{3,2,1,0:T(2,128)S(1)}, u32[]{:S(2)}, u32[]{:S(2)}) async-start(f32[8,2,2,768]{3,2,1,0:T(2,128)} %broadcast_in_dim.2), calls=%async_computation | async-start | bytes 196608 | tf_op jit(solution)/shard_map/all_to_all | solution.py:203
  29.4 1.6 %collective-permute-start = (f32[8,2,2,768]{3,2,1,0:T(2,128)S(1)}, f32[8,2,2,768]{3,2,1,0:T(2,128)S(1)}, u32[]{:S(2)}, u32[]{:S(2)}) collective-permute-start(f32[8,2,2,768]{3,2,1,0:T(2,128)S(1)} %all-to-all-done.winds), channel_id=1, source_target_pairs={{0,8},{8,16},{16,24},{24,32},{32,40},{40,48},{48,56},{56,64},{64,7... | collective-permute-start | bytes 294920 | tf_op jit(solution)/shard_map/ppermute | solution.py:183
  31.1 8.2 %collective-permute-start.1 = (f32[8,2,2,768]{3,2,1,0:T(2,128)S(1)}, f32[8,2,2,768]{3,2,1,0:T(2,128)S(1)}, u32[]{:S(2)}, u32[]{:S(2)}) collective-permute-start(f32[8,2,2,768]{3,2,1,0:T(2,128)S(1)} %all-to-all-done.winds), channel_id=1, source_target_pairs={{8,0},{16,8},{24,16},{32,24},{40,32},{48,40},{56,48},{64,56},{72,6... | collective-permute-start | bytes 294920 | tf_op jit(solution)/shard_map/ppermute | solution.py:184
  44.0 17.2 %all-to-all-start.3 = ((f32[8,32,768]{2,1,0:T(8,128)}), f32[8,32,768]{2,1,0:T(8,128)}, u32[]{:S(2)}, u32[]{:S(2)}) async-start(f32[8,32,768]{2,1,0:T(8,128)} %transport.3), calls=%async_computation.3 | async-start | bytes 1572864 | tf_op jit(solution)/shard_map/all_to_all | solution.py:203
  52.9 12.7 %copy-start.2 = (f32[1024]{0:T(1024)S(1)}, f32[1024]{0:T(1024)}, u32[]{:S(2)}) copy-start(f32[1024]{0:T(1024)} %param.8) | copy-start | bytes 12292
  61.2 17.3 %all-to-all-start.1 = ((f32[8,32,768]{2,1,0:T(8,128)}), f32[8,32,768]{2,1,0:T(8,128)}, u32[]{:S(2)}, u32[]{:S(2)}) async-start(f32[8,32,768]{2,1,0:T(8,128)} %transport.2), calls=%async_computation.1 | async-start | bytes 1572864 | tf_op jit(solution)/shard_map/all_to_all | solution.py:203
  77.1 0.9 copy-start
  78.5 17.5 %all-to-all-start.4 = ((f32[8,32,768]{2,1,0:T(8,128)}), f32[8,32,768]{2,1,0:T(8,128)}, u32[]{:S(2)}, u32[]{:S(2)}) async-start(f32[8,32,768]{2,1,0:T(8,128)} %bitcast.20), calls=%async_computation.4 | async-start | bytes 1572864 | tf_op jit(solution)/shard_map/all_to_all | solution.py:203
  94.4 0.9 copy-start.1
  96.0 17.4 %all-to-all-start.2 = ((f32[8,32,768]{2,1,0:T(8,128)}), f32[8,32,768]{2,1,0:T(8,128)S(1)}, u32[]{:S(2)}, u32[]{:S(2)}) async-start(f32[8,32,768]{2,1,0:T(8,128)} %bitcast.21), calls=%async_computation.2 | async-start | bytes 1572864 | tf_op jit(solution)/shard_map/all_to_all | solution.py:203
  113.4 0.9 copy-start.3

commit v2 on v1

--- a/solution.py
+++ b/solution.py
@@ -29,15 +29,17 @@
     return jnp.transpose(tiles, (0, 2, 1, 3)).reshape(shape)
 
 
-def transport_kernel(chunk, before, winds, after, left, own, right, out):
-    pairs, count, twice = out.shape
+def transport_kernel(chunk, winds, left, own, right, out):
+    ahead, count, twice = out.shape
     width = twice // 2
     pieces = width // LANES
-    stride = own.shape[0] // count
+    stride = own.shape[1]
+    pairs = winds.shape[4] // width
     rows = 16
     y = lax.rem(lax.broadcasted_iota(jnp.int32, (4, width), 1), NY)
-    u = pl.program_id(0)
-    source = u + chunk * pl.num_programs(0)
+    steps = pl.num_programs(0)
+    sources = ahead // pairs
+    left, own, right = (ref.reshape(count * stride, LANES) for ref in (left, own, right))
 
     def south(array):
         return pltpu.roll(array, 1, 1)
@@ -45,15 +47,15 @@
     def north(array):
         return pltpu.roll(array, width - 1, 1)
 
-    for half in range(pairs):
-        t = u * pairs + half
-        lanes = slice(half * width, (half + 1) * width)
+    for t in range(ahead):
+        source = (chunk * steps + pl.program_id(0)) * sources + t // pairs
+        lanes = slice(t % pairs * width, (t % pairs + 1) * width)
 
         def around(kind, first):
             faces = [
-                before[source, kind, 1:2, lanes],
-                winds[source, kind, 0:2, lanes],
-                after[source, kind, 0:2, lanes],
+                winds[source, 0, kind, 1:2, lanes],
+                winds[source, 1, kind, 0:2, lanes],
+                winds[source, 2, kind, 0:2, lanes],
             ]
             return jnp.concatenate(faces, axis=0)[first : first + 4]
 
@@ -95,30 +97,30 @@
             q = [column(ref, c) for ref in (left, own, right) for c in range(2)]
             q = [step(q[i + 1], i, q[i], q[i + 2]) for i in range(4)]
             for c in range(2):
-                out[half, first : first + rows, c * width : (c + 1) * width] = step(
+                out[t, first : first + rows, c * width : (c + 1) * width] = step(
                     q[c + 1], c + 1, q[c], q[c + 2]
                 )
 
 
 def transport(chunk, winds, left, own, right, shape):
     groups, count, twice = shape
-    steps = groups // CHUNKS
+    steps = 2
+    sides = [array.reshape(count, -1, LANES) for array in (left, own, right)]
+    part = sides[0].shape[1] // steps
     return pl.pallas_call(
         functools.partial(transport_kernel, chunk),
         grid=(steps,),
-        in_specs=[VMEM] * 6,
-        out_specs=pl.BlockSpec((groups // steps, count, twice), lambda u: (u, 0, 0)),
+        in_specs=[VMEM] + [pl.BlockSpec((count, part, LANES), lambda s: (0, s, 0))] * 3,
+        out_specs=pl.BlockSpec((groups // steps, count, twice), lambda s: (s, 0, 0)),
         out_shape=pltpu.HBM(shape, F32),
         compiler_params=pltpu.CompilerParams(vmem_limit_bytes=16 << 20),
         name="transport",
-    )(*winds, left, own, right)
+    )(winds, *sides)
 
 
 def join_kernel(y_ref, *refs):
     x_ref = refs[-1]
-    groups, _, twice = y_ref.shape
-    rows = x_ref.shape[0]
-    at = pl.ds(pl.multiple_of(pl.program_id(0) * rows, rows), rows)
+    groups, rows, twice = y_ref.shape
     width = twice // 2
     pieces = width // LANES
     stride = x_ref.shape[1]
@@ -127,7 +129,7 @@
         for c in range(2):
             for m in range(pieces):
                 lane = c * width + m * LANES
-                flat[pl.ds(2 * (t * pieces + m) + c, rows, stride=stride), :] = y_ref[t, at, lane : lane + LANES]
+                flat[pl.ds(2 * (t * pieces + m) + c, rows, stride=stride), :] = y_ref[t, :, lane : lane + LANES]
 
 
 def join(blocks, so_far, chunk):
@@ -137,7 +139,7 @@
     return pl.pallas_call(
         join_kernel,
         grid=(own // 8,),
-        in_specs=[VMEM]
+        in_specs=[pl.BlockSpec((groups, 8, twice), lambda i: (0, i, 0))]
         + [pl.BlockSpec(memory_space=pl.ANY)] * len(more),
         out_specs=pl.BlockSpec((8, length, LANES), lambda i: (i, chunk, 0)),
         out_shape=jax.ShapeDtypeStruct((own, CHUNKS * length, LANES), F32),
@@ -209,11 +211,15 @@
     width = length // groups // CHUNKS
 
     part = length // CHUNKS
-    own = [as_tiles(lax.slice_in_dim(tracers, k * part, (k + 1) * part, axis=2)) for k in range(CHUNKS)]
-    section = exchange(jnp.broadcast_to(fluxes, (groups, *fluxes.shape)))
-    before, after = neighbours(section)
-    winds = (before, section, after)
-    sides = [neighbours(array) for array in own]
+    before, after = neighbours(fluxes)
+    own, sides = [], []
+    for k in range(CHUNKS):
+        raw = lax.slice_in_dim(tracers, k * part, (k + 1) * part, axis=2)
+        raw, tracers = lax.optimization_barrier((raw, tracers))
+        own.append(as_tiles(raw))
+        sides.append(neighbours(own[k]))
+    section = jnp.stack([before, fluxes, after])
+    winds = exchange(jnp.broadcast_to(section, (groups, *section.shape)))
     table = tables(first_reactant, second_reactant, product_species, rate_coeff)
     winds, table = lax.optimization_barrier((winds, table))
 
@@ -225,7 +231,7 @@
         reacted = react(cells, *table)
         back = exchange(reacted.reshape(groups, count, cols * width))
         out = join(back, out, k)
-    return from_tiles(out, tracers.shape)
+    return from_tiles(out, (count, cols, length))
 
 
 def solution(mesh):

time: 118 us -> 115 us (0.975)
  the two profiles are of different devices: /device:TPU:1 before, /device:TPU:224 now
where the time goes in v2:
time: 115 us; the launch traced here: 114 us
  Pallas kernels  37.9 us (33%)
  waiting for transfers between devices  37.4 us (33%)
  starting transfers between devices  30.6 us (27%)
  local copies, waits for them, and re-layouts  6.43 us (6%)
    all_to_all x5, waiting for transfers between devices, exchange(): lax.all_to_all(blocks, 'tracer', split_axis=0, concat_axis=0, tiled=True)  37.4 us
    all_to_all x5, starting transfers between devices, exchange(): lax.all_to_all(blocks, 'tracer', split_axis=0, concat_axis=0, tiled=True)  25 us
    pallas_call x2, Pallas kernels, react(): pl.pallas_call(react_kernel, in_specs=[VMEM] * 5, out_specs=VMEM, out_sha...  22.9 us
    pallas_call x2, Pallas kernels, transport(): pl.pallas_call(functools.partial(transport_kernel, chunk), grid=(steps,),...  8.22 us
    pallas_call x2, Pallas kernels, join(): pl.pallas_call(join_kernel, grid=(own // 8,), in_specs=[pl.BlockSpec((gro...  6.69 us
    ppermute x3, starting transfers between devices, neighbours(): lax.ppermute(array, 'region', [((i + 1) % count, i) for i in range(count)])  3.48 us
    slice x2, local copies, waits for them, and re-layouts, body(): raw = lax.slice_in_dim(tracers, k * part, (k + 1) * part, axis=2)  3 us
    unnamed x18, local copies, waits for them, and re-layouts  2.64 us
  transfers between devices with their start and end apart: 11, of which 5 were waited for; matrix products, arithmetic and copies ran while one was open for 4% of the time, Pallas kernels for 30%

profile of v2, /device:TPU:224, one launch (start us, length us, event | category | flops | bytes accessed | tf_op | source)
XLA Modules:
  0.0 113.6 jit_solution(17428012257800414960)
XLA Ops:
  0.0 0.1 collective-permute-start
  0.1 1.7 %collective-permute-start.1 = (f32[2,2,768]{2,1,0:T(2,128)}, f32[2,2,768]{2,1,0:T(2,128)S(1)}, u32[]{:S(2)}, u32[]{:S(2)}) collective-permute-start(f32[2,2,768]{2,1,0:T(2,128)} %param.7), channel_id=1, source_target_pairs={{8,0},{16,8},{24,16},{32,24},{40,32},{48,40},{56,48},{64,56},{72,6... | collective-permute-start | bytes 36872 | tf_op jit(solution)/shard_map/ppermute | solution.py:186
  1.8 2.1 %slice.6 = f32[32,2,3072]{2,1,0:T(2,128)} slice(f32[32,2,6144]{2,1,0:T(2,128)} %param.6), slice={[0:32], [0:2], [0:3072]} | slice | bytes 1572864 | tf_op jit(solution)/shard_map/slice | solution.py:217
  3.9 1.7 %collective-permute-start.5 = (f32[1536,128]{1,0:T(8,128)}, f32[1536,128]{1,0:T(8,128)}, u32[]{:S(2)}, u32[]{:S(2)}) collective-permute-start(f32[1536,128]{1,0:T(8,128)} %bitcast.16), channel_id=1, source_target_pairs={{8,0},{16,8},{24,16},{32,24},{40,32},{48,40},{56,48},{64,56},{72,6... | collective-permute-start | bytes 2359304 | tf_op jit(solution)/shard_map/ppermute | solution.py:186
  5.7 0.9 slice.7
  6.6 0.0 collective-permute-start.3
  6.6 0.7 compare_convert_fusion
  7.3 0.0 collective-permute-done
  7.3 2.1 %collective-permute-start.2 = (f32[1536,128]{1,0:T(8,128)}, f32[1536,128]{1,0:T(8,128)}, u32[]{:S(2)}, u32[]{:S(2)}) collective-permute-start(f32[1536,128]{1,0:T(8,128)} %bitcast.6), channel_id=1, source_target_pairs={{0,8},{8,16},{16,24},{24,32},{32,40},{40,48},{48,56},{56,64},{64,7... | collective-permute-start | bytes 2359304 | tf_op jit(solution)/shard_map/ppermute | solution.py:185
  9.4 0.8 broadcast_in_dim.2
  10.2 5.1 %all-to-all-start = ((f32[8,3,2,2,768]{4,3,2,1,0:T(2,128)}), f32[8,3,2,2,768]{4,3,2,1,0:T(2,128)S(1)}, u32[]{:S(2)}, u32[]{:S(2)}) async-start(f32[8,3,2,2,768]{4,3,2,1,0:T(2,128)} %broadcast_in_dim.2), calls=%async_computation | async-start | bytes 589824 | tf_op jit(solution)/shard_map/all_to_all | solution.py:205
  15.3 0.3 subtract_convert_fusion
  15.6 0.1 pad_maximum_fusion.change
  15.8 18.9 %all-to-all-done.winds = f32[8,3,2,2,768]{4,3,2,1,0:T(2,128)S(1)} async-done(((f32[8,3,2,2,768]{4,3,2,1,0:T(2,128)}), f32[8,3,2,2,768]{4,3,2,1,0:T(2,128)S(1)}, u32[]{:S(2)}, u32[]{:S(2)}) %all-to-all-start) | async-done | bytes 294944 | tf_op jit(solution)/shard_map/all_to_all | solution.py:205
  34.7 4.1 %transport.3 = f32[8,32,768]{2,1,0:T(8,128)} custom-call(f32[8,3,2,2,768]{4,3,2,1,0:T(2,128)S(1)} %all-to-all-done.winds, f32[32,48,128]{2,1,0:T(8,128)} %bitcast.17.left, f32[32,48,128]{2,1,0:T(8,128)} %bitcast.19.own, f32[32,48,128]{2,1,0:T(8,128)} %bitcast.21.right), custom_call_target="tpu_custom_call" | custom-call | tf_op jit(solution)/shard_map/transport/pallas_call | solution.py:110
  38.8 5.1 %all-to-all-start.3 = ((f32[8,32,768]{2,1,0:T(8,128)}), f32[8,32,768]{2,1,0:T(8,128)}, u32[]{:S(2)}, u32[]{:S(2)}) async-start(f32[8,32,768]{2,1,0:T(8,128)} %transport.3), calls=%async_computation.3 | async-start | bytes 1572864 | tf_op jit(solution)/shard_map/all_to_all | solution.py:205
  43.9 4.1 %transport.2 = f32[8,32,768]{2,1,0:T(8,128)} custom-call(f32[8,3,2,2,768]{4,3,2,1,0:T(2,128)S(1)} %all-to-all-done.winds, f32[32,48,128]{2,1,0:T(8,128)} %bitcast.7.left, f32[32,48,128]{2,1,0:T(8,128)} %bitcast.9.own, f32[32,48,128]{2,1,0:T(8,128)} %bitcast.11.right), custom_call_target="tpu_custom_call" | custom-call | tf_op jit(solution)/shard_map/transport/pallas_call | solution.py:110
  48.0 9.1 %all-to-all-done.3 = f32[8,32,768]{2,1,0:T(8,128)} async-done(((f32[8,32,768]{2,1,0:T(8,128)}), f32[8,32,768]{2,1,0:T(8,128)}, u32[]{:S(2)}, u32[]{:S(2)}) %all-to-all-start.3) | async-done | bytes 786464 | tf_op jit(solution)/shard_map/all_to_all | solution.py:205
  57.2 4.4 %all-to-all-start.1 = ((f32[8,32,768]{2,1,0:T(8,128)}), f32[8,32,768]{2,1,0:T(8,128)}, u32[]{:S(2)}, u32[]{:S(2)}) async-start(f32[8,32,768]{2,1,0:T(8,128)} %transport.2), calls=%async_computation.1 | async-start | bytes 1572864 | tf_op jit(solution)/shard_map/all_to_all | solution.py:205
  61.6 11.5 %react.3 = f32[256,768]{1,0:T(8,128)S(1)} custom-call(f32[256,768]{1,0:T(8,128)} %bitcast.22.cells, bf16[1024,512]{1,0:T(8,128)(2,1)S(1)} %get-tuple-element.16.pick1, bf16[1024,512]{1,0:T(8,128)(2,1)S(1)} %get-tuple-element.17.pick2, bf16[256,2048]{1,0:T(8,128)(2,1)S(1)} %pad_maximum_fusion.change, f32[8,128]{1,0:T(8,128)S(1)} %bitcast.33), custom_call_target="tpu_custom_call" | custom-call | tf_op jit(solution)/shard_map/react/pallas_call | solution.py:173
  73.1 0.0 copy-start
  73.1 0.9 copy-done
  73.9 0.5 all-to-all-done.1
  74.5 4.9 %all-to-all-start.4 = ((f32[8,32,768]{2,1,0:T(8,128)}), f32[8,32,768]{2,1,0:T(8,128)}, u32[]{:S(2)}, u32[]{:S(2)}) async-start(f32[8,32,768]{2,1,0:T(8,128)} %bitcast.31), calls=%async_computation.4 | async-start | bytes 1572864 | tf_op jit(solution)/shard_map/all_to_all | solution.py:205
  79.4 11.5 %react.2 = f32[256,768]{1,0:T(8,128)S(1)} custom-call(f32[256,768]{1,0:T(8,128)} %bitcast.12.cells, bf16[1024,512]{1,0:T(8,128)(2,1)S(1)} %get-tuple-element.16.pick1, bf16[1024,512]{1,0:T(8,128)(2,1)S(1)} %get-tuple-element.17.pick2, bf16[256,2048]{1,0:T(8,128)(2,1)S(1)} %pad_maximum_fusion.change, f32[8,128]{1,0:T(8,128)S(1)} %bitcast.34), custom_call_target="tpu_custom_call" | custom-call | tf_op jit(solution)/shard_map/react/pallas_call | solution.py:173
  90.9 0.9 copy-done.1
  91.7 0.2 all-to-all-done.4.y_ref
  92.0 5.5 %all-to-all-start.2 = ((f32[8,32,768]{2,1,0:T(8,128)}), f32[8,32,768]{2,1,0:T(8,128)S(1)}, u32[]{:S(2)}, u32[]{:S(2)}) async-start(f32[8,32,768]{2,1,0:T(8,128)} %bitcast.32), calls=%async_computation.2 | async-start | bytes 1572864 | tf_op jit(solution)/shard_map/all_to_all | solution.py:205
  97.4 3.3 %join.2.refs_0_ = f32[32,96,128]{2,1,0:T(8,128)} custom-call(f32[8,32,768]{2,1,0:T(8,128)} %all-to-all-done.4.y_ref), custom_call_target="tpu_custom_call" | custom-call | tf_op jit(solution)/shard_map/join/pallas_call | solution.py:139
  100.8 8.6 %all-to-all-done.2.y_ref = f32[8,32,768]{2,1,0:T(8,128)S(1)} async-done(((f32[8,32,768]{2,1,0:T(8,128)}), f32[8,32,768]{2,1,0:T(8,128)S(1)}, u32[]{:S(2)}, u32[]{:S(2)}) %all-to-all-start.2) | async-done | bytes 786464 | tf_op jit(solution)/shard_map/all_to_all | solution.py:205
  109.4 0.9 copy-done.3
  110.2 3.3 %join.3 = f32[32,96,128]{2,1,0:T(8,128)} custom-call(f32[8,32,768]{2,1,0:T(8,128)} %copy-done.3, f32[32,96,128]{2,1,0:T(8,128)} %join.2.refs_0_), custom_call_target="tpu_custom_call", output_to_operand_aliasing={{}: (1, {})} | custom-call | tf_op jit(solution)/shard_map/join/pallas_call | solution.py:139
  (22 shorter events, 0.1 us)
Async XLA Ops:
  0.0 5.7 %copy-start.4 = (f32[32,2,6144]{2,1,0:T(2,128)S(1)}, f32[32,2,6144]{2,1,0:T(2,128)}, u32[]{:S(2)}) copy-start(f32[32,2,6144]{2,1,0:T(2,128)} %param.6) | copy-start | bytes 4718596
  0.0 6.6 %copy-start.5 = (s32[1024]{0:T(1024)S(1)}, s32[1024]{0:T(1024)}, u32[]{:S(2)}) copy-start(s32[1024]{0:T(1024)} %param.10) | copy-start | bytes 12292
  0.0 6.6 %copy-start.6 = (s32[1024]{0:T(1024)S(1)}, s32[1024]{0:T(1024)}, u32[]{:S(2)}) copy-start(s32[1024]{0:T(1024)} %param.9) | copy-start | bytes 12292
  0.0 7.3 %collective-permute-start = (f32[2,2,768]{2,1,0:T(2,128)}, f32[2,2,768]{2,1,0:T(2,128)S(1)}, u32[]{:S(2)}, u32[]{:S(2)}) collective-permute-start(f32[2,2,768]{2,1,0:T(2,128)} %param.7), channel_id=1, source_target_pairs={{0,8},{8,16},{16,24},{24,32},{32,40},{40,48},{48,56},{56,64},{64,7... | collective-permute-start | bytes 36872 | tf_op jit(solution)/shard_map/ppermute | solution.py:185
  0.1 9.3 %collective-permute-start.1 = (f32[2,2,768]{2,1,0:T(2,128)}, f32[2,2,768]{2,1,0:T(2,128)S(1)}, u32[]{:S(2)}, u32[]{:S(2)}) collective-permute-start(f32[2,2,768]{2,1,0:T(2,128)} %param.7), channel_id=1, source_target_pairs={{8,0},{16,8},{24,16},{32,24},{40,32},{48,40},{56,48},{64,56},{72,6... | collective-permute-start | bytes 36872 | tf_op jit(solution)/shard_map/ppermute | solution.py:186
  3.9 5.5 %copy-start.7 = (f32[2,2,768]{2,1,0:T(2,128)S(1)}, f32[2,2,768]{2,1,0:T(2,128)}, u32[]{:S(2)}) copy-start(f32[2,2,768]{2,1,0:T(2,128)} %param.7) | copy-start | bytes 36868
  3.9 30.8 %collective-permute-start.4 = (f32[1536,128]{1,0:T(8,128)}, f32[1536,128]{1,0:T(8,128)}, u32[]{:S(2)}, u32[]{:S(2)}) collective-permute-start(f32[1536,128]{1,0:T(8,128)} %bitcast.16), channel_id=1, source_target_pairs={{0,8},{8,16},{16,24},{24,32},{32,40},{40,48},{48,56},{56,64},{64,7... | collective-permute-start | bytes 2359304 | tf_op jit(solution)/shard_map/ppermute | solution.py:185
  3.9 30.8 %collective-permute-start.5 = (f32[1536,128]{1,0:T(8,128)}, f32[1536,128]{1,0:T(8,128)}, u32[]{:S(2)}, u32[]{:S(2)}) collective-permute-start(f32[1536,128]{1,0:T(8,128)} %bitcast.16), channel_id=1, source_target_pairs={{8,0},{16,8},{24,16},{32,24},{40,32},{48,40},{56,48},{64,56},{72,6... | collective-permute-start | bytes 2359304 | tf_op jit(solution)/shard_map/ppermute | solution.py:186
  6.6 8.7 %copy-start.8 = (s32[1024]{0:T(1024)S(1)}, s32[1024]{0:T(1024)}, u32[]{:S(2)}) copy-start(s32[1024]{0:T(1024)} %param.11) | copy-start | bytes 12292
  6.6 37.3 %collective-permute-start.3 = (f32[1536,128]{1,0:T(8,128)}, f32[1536,128]{1,0:T(8,128)}, u32[]{:S(2)}, u32[]{:S(2)}) collective-permute-start(f32[1536,128]{1,0:T(8,128)} %bitcast.6), channel_id=1, source_target_pairs={{8,0},{16,8},{24,16},{32,24},{40,32},{48,40},{56,48},{64,56},{72,6... | collective-permute-start | bytes 2359304 | tf_op jit(solution)/shard_map/ppermute | solution.py:186
  7.3 36.6 %collective-permute-start.2 = (f32[1536,128]{1,0:T(8,128)}, f32[1536,128]{1,0:T(8,128)}, u32[]{:S(2)}, u32[]{:S(2)}) collective-permute-start(f32[1536,128]{1,0:T(8,128)} %bitcast.6), channel_id=1, source_target_pairs={{0,8},{8,16},{16,24},{24,32},{32,40},{40,48},{48,56},{56,64},{64,7... | collective-permute-start | bytes 2359304 | tf_op jit(solution)/shard_map/ppermute | solution.py:185
  10.2 24.5 %all-to-all-start = ((f32[8,3,2,2,768]{4,3,2,1,0:T(2,128)}), f32[8,3,2,2,768]{4,3,2,1,0:T(2,128)S(1)}, u32[]{:S(2)}, u32[]{:S(2)}) async-start(f32[8,3,2,2,768]{4,3,2,1,0:T(2,128)} %broadcast_in_dim.2), calls=%async_computation | async-start | bytes 589824 | tf_op jit(solution)/shard_map/all_to_all | solution.py:205
  38.8 18.4 %all-to-all-start.3 = ((f32[8,32,768]{2,1,0:T(8,128)}), f32[8,32,768]{2,1,0:T(8,128)}, u32[]{:S(2)}, u32[]{:S(2)}) async-start(f32[8,32,768]{2,1,0:T(8,128)} %transport.3), calls=%async_computation.3 | async-start | bytes 1572864 | tf_op jit(solution)/shard_map/all_to_all | solution.py:205
  48.0 13.6 %copy-start.2 = (f32[1024]{0:T(1024)S(1)}, f32[1024]{0:T(1024)}, u32[]{:S(2)}) copy-start(f32[1024]{0:T(1024)} %param.8) | copy-start | bytes 12292
  57.2 17.3 %all-to-all-start.1 = ((f32[8,32,768]{2,1,0:T(8,128)}), f32[8,32,768]{2,1,0:T(8,128)}, u32[]{:S(2)}, u32[]{:S(2)}) async-start(f32[8,32,768]{2,1,0:T(8,128)} %transport.2), calls=%async_computation.1 | async-start | bytes 1572864 | tf_op jit(solution)/shard_map/all_to_all | solution.py:205
  73.1 0.9 copy-start
  74.5 17.5 %all-to-all-start.4 = ((f32[8,32,768]{2,1,0:T(8,128)}), f32[8,32,768]{2,1,0:T(8,128)}, u32[]{:S(2)}, u32[]{:S(2)}) async-start(f32[8,32,768]{2,1,0:T(8,128)} %bitcast.31), calls=%async_computation.4 | async-start | bytes 1572864 | tf_op jit(solution)/shard_map/all_to_all | solution.py:205
  90.9 0.9 copy-start.1
  92.0 17.4 %all-to-all-start.2 = ((f32[8,32,768]{2,1,0:T(8,128)}), f32[8,32,768]{2,1,0:T(8,128)S(1)}, u32[]{:S(2)}, u32[]{:S(2)}) async-start(f32[8,32,768]{2,1,0:T(8,128)} %bitcast.32), calls=%async_computation.2 | async-start | bytes 1572864 | tf_op jit(solution)/shard_map/all_to_all | solution.py:205
  109.4 0.9 copy-start.3

commit v3 on v1

v3 whole, which is shorter than its diff:
```python
import functools

import jax
import jax.numpy as jnp
from jax import lax
from jax.experimental import pallas as pl
from jax.experimental.pallas import tpu as pltpu
from jax.sharding import Mesh, PartitionSpec as P

TRACERS = 256
NY = 48
SUBSTEPS = 4
LANES = 128
CHUNKS = 2
F32 = jnp.float32
BF16 = jnp.bfloat16
VMEM = pl.BlockSpec(memory_space=pltpu.VMEM)
PLANE = ("yhi", "tracer")
RING = ("z", "core")
REGION = ("yhi", "z", "core")


def low_half(shape):
    return lax.broadcasted_iota(jnp.int32, shape, 1) < LANES // 2


def turned(tile):
    return pltpu.roll(tile, LANES // 2, 1)


def to_blocks_kernel(chunk, x_ref, o_ref):
    rows = o_ref.shape[2]
    stride = x_ref.shape[0] // rows
    low = low_half((rows, LANES))

    def tile(j, c):
        return x_ref[pl.ds(2 * j + c, rows, stride=stride), :]

    for t in range(o_ref.shape[1]):
        j = (t * CHUNKS + chunk) * 3
        a0, a1, a2 = (tile(j + m, 0) for m in range(3))
        b0, b1, b2 = (tile(j + m, 1) for m in range(3))
        o_ref[0, t, :, 0:128] = a0
        o_ref[0, t, :, 128:256] = jnp.where(low, a1, turned(b0))
        o_ref[0, t, :, 256:384] = jnp.where(low, turned(b0), turned(b1))
        o_ref[1, t, :, 0:128] = jnp.where(low, turned(a1), turned(a2))
        o_ref[1, t, :, 128:256] = jnp.where(low, turned(a2), b1)
        o_ref[1, t, :, 256:384] = b2


def from_blocks_kernel(*refs):
    *y_refs, x_ref = refs
    rows = y_refs[0].shape[2]
    stride = x_ref.shape[0] // rows
    low = low_half((rows, LANES))

    def put(j, c, value):
        x_ref[pl.ds(2 * j + c, rows, stride=stride), :] = value

    for t in range(y_refs[0].shape[1]):
        for chunk, y_ref in enumerate(y_refs):
            j = (t * CHUNKS + chunk) * 3
            s0, s1, s2 = (y_ref[0, t, :, m * 128 : m * 128 + 128] for m in range(3))
            n0, n1, n2 = (y_ref[1, t, :, m * 128 : m * 128 + 128] for m in range(3))
            put(j, 0, s0)
            put(j + 1, 0, jnp.where(low, s1, turned(n0)))
            put(j + 2, 0, jnp.where(low, turned(n0), turned(n1)))
            put(j, 1, jnp.where(low, turned(s1), turned(s2)))
            put(j + 1, 1, jnp.where(low, turned(s2), n1))
            put(j + 2, 1, n2)


def to_blocks(tracers, chunk, groups):
    own, cols, length = tracers.shape
    width = length // groups // CHUNKS
    tiles = tracers.reshape(own, cols, length // LANES, LANES)
    tiles = jnp.transpose(tiles, (0, 2, 1, 3)).reshape(-1, LANES)
    steps = own // 8
    return pl.pallas_call(
        functools.partial(to_blocks_kernel, chunk),
        grid=(steps,),
        in_specs=[pl.BlockSpec((tiles.shape[0] // steps, LANES), lambda i: (i, 0))],
        out_specs=pl.BlockSpec((2, groups, 8, width), lambda i: (0, 0, i, 0)),
        out_shape=pltpu.HBM((2, groups, own, width), F32),
        name="to_blocks",
    )(tiles)


def from_blocks(blocks, shape):
    own, cols, length = shape
    _, groups, _, width = blocks[0].shape
    steps = own // 8
    rows = own * cols * length // LANES
    tiles = pl.pallas_call(
        from_blocks_kernel,
        grid=(steps,),
        in_specs=[pl.BlockSpec((2, groups, 8, width), lambda i: (0, 0, i, 0))] * CHUNKS,
        out_specs=pl.BlockSpec((rows // steps, LANES), lambda i: (i, 0)),
        out_shape=jax.ShapeDtypeStruct((rows, LANES), F32),
        name="from_blocks",
    )(*blocks)
    tiles = tiles.reshape(own, length // LANES, cols, LANES)
    return jnp.transpose(tiles, (0, 2, 1, 3)).reshape(shape)


def transport_kernel(swap, winds, own, left, right, cells):
    width = own.shape[2]
    col = width // 2
    rows = 32
    row = lax.rem(lax.broadcasted_iota(jnp.int32, (1, 4 * col), 1), NY)

    for h in range(2):
        from_left = jnp.where(swap[0] == 1, 1 - h, h)
        from_right = jnp.where(swap[1] == 1, 1 - h, h)
        u = winds[h, 0:1, col : 5 * col]
        u_next = winds[h, 0:1, 2 * col : 6 * col]
        v = jnp.where(row == 0, 0.0, winds[h, 1:2, col : 5 * col])
        v_next = jnp.where(row == NY - 1, 0.0, winds[h, 1:2, col + 1 : 5 * col + 1])
        here = (
            1.0
            + jnp.minimum(u, 0.0)
            - jnp.maximum(u_next, 0.0)
            + jnp.minimum(v, 0.0)
            - jnp.maximum(v_next, 0.0)
        )
        wide = [
            here,
            jnp.maximum(u, 0.0),
            -jnp.minimum(u_next, 0.0),
            jnp.maximum(v, 0.0),
            -jnp.minimum(v_next, 0.0),
        ]
        narrow = [array[:, col : 3 * col] for array in wide]

        def step(q, weights):
            n = weights[0].shape[1]
            shifts = (col, 0, 2 * col, col - 1, col + 1)
            terms = [w * q[:, s : s + n] for w, s in zip(weights, shifts)]
            return terms[0] + terms[1] + terms[2] + terms[3] + terms[4]

        for first in range(0, own.shape[1], rows):
            at = slice(first, first + rows)
            q = jnp.concatenate([left[from_left, at, :], own[h, at, :], right[from_right, at, :]], axis=1)
            cells[at, h * width : (h + 1) * width] = step(step(q, wide), narrow)


def transport(swap, winds, own, left, right):
    _, count, width = own.shape
    steps = 4
    part = pl.BlockSpec((2, count // steps, width), lambda i: (0, i, 0))
    return pl.pallas_call(
        transport_kernel,
        grid=(steps,),
        in_specs=[pl.BlockSpec(memory_space=pltpu.SMEM), VMEM, part, part, part],
        out_specs=pl.BlockSpec((count // steps, 2 * width), lambda i: (i, 0)),
        out_shape=jax.ShapeDtypeStruct((count, 2 * width), F32),
        compiler_params=pltpu.CompilerParams(vmem_limit_bytes=16 << 20),
        name="transport",
    )(swap, winds, own, left, right)


def split(values):
    high = values.astype(BF16)
    low = (values - high.astype(F32)).astype(BF16)
    return jnp.concatenate([high, low], axis=0)


def react_kernel(cells, pick1, pick2, change, rates, out):
    amounts = cells[...]
    rate = jnp.concatenate(
        [jnp.broadcast_to(rates[i : i + 1, :], (LANES, LANES)).T for i in range(rates.shape[0])], axis=0
    )
    rate = jnp.concatenate([rate] * (amounts.shape[1] // LANES), axis=1)
    for step in range(SUBSTEPS):
        parts = split(amounts)
        first = jnp.dot(pick1[...], parts, preferred_element_type=F32)
        second = jnp.dot(pick2[...], parts, preferred_element_type=F32)
        velocity = split(rate * first * second)
        amounts = amounts + jnp.dot(change[...], velocity, preferred_element_type=F32)
    width = out.shape[2]
    for h in range(2):
        out[h] = amounts[:, h * width : (h + 1) * width]


def react(cells, pick1, pick2, change, rates):
    return pl.pallas_call(
        react_kernel,
        in_specs=[VMEM] * 5,
        out_specs=VMEM,
        out_shape=jax.ShapeDtypeStruct((2, cells.shape[0], cells.shape[1] // 2), F32),
        compiler_params=pltpu.CompilerParams(vmem_limit_bytes=24 << 20),
        name="react",
    )(cells, pick1, pick2, change, rates)


def neighbours(array):
    count = lax.axis_size(RING)
    left = lax.ppermute(array, RING, [(i, (i + 1) % count) for i in range(count)])
    right = lax.ppermute(array, RING, [((i + 1) % count, i) for i in range(count)])
    return left, right


def all_winds(fluxes):
    regions = lax.axis_size(REGION)
    half = lax.axis_index("yhi")

    def from_region(ahead):
        if ahead == 0:
            return fluxes
        return lax.ppermute(fluxes, REGION, [((i + ahead) % regions, i) for i in range(regions)])

    def mine(array):
        array = array.reshape(2, array.shape[1], CHUNKS, 2, -1)
        return jnp.where(half == 0, array[:, :, :, 0], array[:, :, :, 1])

    own = [mine(from_region(d)) for d in (-1, 0, 1)]
    other = [mine(from_region(regions // 2 + d)) for d in (-1, 0, 1)]
    parts = []
    for h in range(2):
        trio = [jnp.where(half == h, a, b) for a, b in zip(own, other)]
        parts.append(jnp.stack(trio))
    winds = jnp.stack(parts)
    winds = jnp.transpose(winds, (0, 4, 2, 1, 3, 5))
    return winds.reshape(2, CHUNKS, 2, -1)


def tables(first_reactant, second_reactant, product_species, rate_coeff):
    species = jnp.arange(2 * TRACERS, dtype=jnp.int32) % TRACERS
    pick1 = (first_reactant[:, None] == species[None, :]).astype(BF16)
    pick2 = (second_reactant[:, None] == species[None, :]).astype(BF16)
    kinds = jnp.arange(TRACERS, dtype=jnp.int32)[:, None]
    change = (
        (product_species[None, :] == kinds).astype(F32)
        - (first_reactant[None, :] == kinds).astype(F32)
        - (second_reactant[None, :] == kinds).astype(F32)
    ).astype(BF16)
    change = jnp.concatenate([change, change], axis=1)
    return pick1, pick2, change, rate_coeff.reshape(-1, LANES)


def exchange(blocks):
    return lax.all_to_all(blocks, PLANE, split_axis=0, concat_axis=0, tiled=True)


def body(tracers, fluxes, rate_coeff, first_reactant, second_reactant, product_species):
    groups = lax.axis_size("tracer")
    own = tracers.shape[0]
    count = lax.axis_size(RING)
    place = lax.axis_index(RING)
    swap = jnp.stack([place == 0, place == count - 1]).astype(jnp.int32)

    gathered = []
    for chunk in range(CHUNKS):
        blocks = to_blocks(tracers, chunk, groups)
        if chunk == 0:
            blocks, first_reactant, second_reactant, product_species = lax.optimization_barrier(
                (blocks, first_reactant, second_reactant, product_species)
            )
        gathered.append(exchange(blocks.reshape(2 * groups, own, -1)))
    table = tables(first_reactant, second_reactant, product_species, rate_coeff)
    winds = all_winds(fluxes)

    returned = []
    for chunk in range(CHUNKS):
        part = gathered[chunk]
        shape = (2, TRACERS, part.shape[-1])
        left, right = neighbours(part)
        cells = transport(
            swap, winds[:, chunk], part.reshape(shape), left.reshape(shape), right.reshape(shape)
        )
        reacted = react(cells, *table)
        back = exchange(reacted.reshape(part.shape))
        returned.append(back.reshape(2, groups, own, -1))
    return from_blocks(returned, tracers.shape)


def solution(mesh):
    regions, groups = mesh.devices.shape
    torus = Mesh(mesh.devices.reshape(2, regions // 4, 2, groups), ("yhi", "z", "core", "tracer"))
    in_specs = (P("tracer", REGION, None), P(None, REGION, "tracer"), P(), P(), P(), P())
    out_specs = P("tracer", REGION, None)
    return jax.shard_map(body, mesh=torus, in_specs=in_specs, out_specs=out_specs, check_vma=False)
```

time: 118 us -> 123 us (1.042)
  the two profiles are of different devices: /device:TPU:1 before, /device:TPU:96 now
where the time goes in v3:
time: 123 us; the launch traced here: 122 us
  Pallas kernels  46.9 us (38%)
  waiting for transfers between devices  25.4 us (21%)
  starting transfers between devices  23.3 us (19%)
  blocking collectives  22.8 us (19%)
  local copies, waits for them, and re-layouts  2.55 us (2%)
  other arithmetic  1.3 us (1%)
    all_to_all x3, waiting for transfers between devices, exchange(): lax.all_to_all(blocks, PLANE, split_axis=0, concat_axis=0, tiled=True)  25.4 us
    all_to_all x1, blocking collectives, exchange(): lax.all_to_all(blocks, PLANE, split_axis=0, concat_axis=0, tiled=True)  22.8 us
    pallas_call x2, Pallas kernels, react(): pl.pallas_call(react_kernel, in_specs=[VMEM] * 5, out_specs=VMEM, out_sha...  20.8 us
    pallas_call x2, Pallas kernels, transport(): pl.pallas_call(transport_kernel, grid=(steps,), in_specs=[pl.BlockSpec(me...  14.6 us
    all_to_all x3, starting transfers between devices, exchange(): lax.all_to_all(blocks, PLANE, split_axis=0, concat_axis=0, tiled=True)  14.2 us
    ppermute x5, starting transfers between devices, from_region(): lax.ppermute(fluxes, REGION, [((i + ahead) % regions, i) for i in range(r...  8.02 us
    pallas_call x2, Pallas kernels, to_blocks(): pl.pallas_call(functools.partial(to_blocks_kernel, chunk), grid=(steps,),...  7.4 us
    pallas_call x1, Pallas kernels, from_blocks(): pl.pallas_call(from_blocks_kernel, grid=(steps,), in_specs=[pl.BlockSpec(...  4.05 us
  transfers between devices with their start and end apart: 12, of which 2 were waited for; matrix products, arithmetic and copies ran while one was open for 2% of the time, Pallas kernels for 35%

profile of v3, /device:TPU:96, one launch (start us, length us, event | category | flops | bytes accessed | tf_op | source)
XLA Modules:
  0.0 122.5 jit_solution(1435517984313127017)
XLA Ops:
  0.0 3.2 %collective-permute-start.2 = (f32[2,2,768]{2,1,0:T(2,128)}, f32[2,2,768]{2,1,0:T(2,128)S(1)}, u32[]{:S(2)}, u32[]{:S(2)}) collective-permute-start(f32[2,2,768]{2,1,0:T(2,128)} %param.7), channel_id=1, source_target_pairs={{128,0},{136,8},{144,16},{152,24},{160,32},{168,40},{176,48},{184,... | collective-permute-start | bytes 36872 | tf_op jit(solution)/shard_map/ppermute | solution.py:210
  3.2 3.0 %collective-permute-start = (f32[2,2,768]{2,1,0:T(2,128)}, f32[2,2,768]{2,1,0:T(2,128)S(1)}, u32[]{:S(2)}, u32[]{:S(2)}) collective-permute-start(f32[2,2,768]{2,1,0:T(2,128)} %param.7), channel_id=1, source_target_pairs={{248,0},{0,8},{8,16},{16,24},{24,32},{32,40},{40,48},{48,56},{56,6... | collective-permute-start | bytes 36872 | tf_op jit(solution)/shard_map/ppermute | solution.py:210
  6.2 1.1 collective-permute-start.4
  7.3 0.7 collective-permute-start.3
  8.0 3.7 %to_blocks.3 = f32[2,8,32,384]{3,2,1,0:T(8,128)} custom-call(f32[3072,128]{1,0:T(8,128)} %bitcast.59), custom_call_target="tpu_custom_call" | custom-call | tf_op jit(solution)/shard_map/to_blocks/pallas_call | solution.py:79
  11.8 5.3 %all-to-all-start.2 = ((f32[16,32,384]{2,1,0:T(8,128)}), f32[16,32,384]{2,1,0:T(8,128)}, u32[]{:S(2)}, u32[]{:S(2)}) async-start(f32[16,32,384]{2,1,0:T(8,128)} %bitcast.62), calls=%async_computation.2 | async-start | bytes 1572864 | tf_op jit(solution)/shard_map/all_to_all | solution.py:242
  17.1 0.1 reshape.282
  17.2 3.7 %to_blocks.2 = f32[2,8,32,384]{3,2,1,0:T(8,128)} custom-call(f32[3072,128]{1,0:T(8,128)} %bitcast.60), custom_call_target="tpu_custom_call" | custom-call | tf_op jit(solution)/shard_map/to_blocks/pallas_call | solution.py:79
  20.9 0.3 subtract_convert_fusion
  21.2 0.1 pad_maximum_fusion.change
  21.4 0.7 compare_convert_fusion
  22.1 0.1 add_convert_fusion.swap
  22.1 0.1 reshape.283
  22.3 0.1 reshape.281
  22.4 0.1 reshape.280
  22.5 0.1 reshape.285
  22.6 0.1 reshape.284
  22.7 11.5 %all-to-all-done.2 = f32[16,32,384]{2,1,0:T(8,128)} async-done(((f32[16,32,384]{2,1,0:T(8,128)}), f32[16,32,384]{2,1,0:T(8,128)}, u32[]{:S(2)}, u32[]{:S(2)}) %all-to-all-start.2) | async-done | bytes 786464 | tf_op jit(solution)/shard_map/all_to_all | solution.py:242
  34.2 4.5 %all-to-all-start = ((f32[16,32,384]{2,1,0:T(8,128)}), f32[16,32,384]{2,1,0:T(8,128)}, u32[]{:S(2)}, u32[]{:S(2)}) async-start(f32[16,32,384]{2,1,0:T(8,128)} %bitcast.61), calls=%async_computation | async-start | bytes 1572864 | tf_op jit(solution)/shard_map/all_to_all | solution.py:242
  38.8 0.5 collective-permute-start.7
  39.3 0.1 reshape.286
  39.5 13.9 %all-to-all-done = f32[16,32,384]{2,1,0:T(8,128)} async-done(((f32[16,32,384]{2,1,0:T(8,128)}), f32[16,32,384]{2,1,0:T(8,128)}, u32[]{:S(2)}, u32[]{:S(2)}) %all-to-all-start) | async-done | bytes 786464 | tf_op jit(solution)/shard_map/all_to_all | solution.py:242
  53.3 0.5 collective-permute-start.5
  53.9 7.3 %transport.3.cells = f32[256,768]{1,0:T(8,128)S(1)} custom-call(s32[2]{0:T(128)S(1)} %add_convert_fusion.swap, f32[2,2,1152]{2,1,0:T(2,128)S(1)} %get-tuple-element.13.winds, f32[2,256,384]{2,1,0:T(8,128)} %bitcast.28.own, f32[2,256,384]{2,1,0:T(8,128)} %bitcast.29.left, f32[2,256,384]{2,1,0:T(8,128)} %bitcast.30.right), custom_call_target="tpu_custom_call" | custom-call | tf_op jit(solution)/shard_map/transport/pallas_call | solution.py:151
  61.2 10.4 %react.3 = f32[2,256,384]{2,1,0:T(8,128)S(1)} custom-call(f32[256,768]{1,0:T(8,128)S(1)} %transport.3.cells, bf16[1024,512]{1,0:T(8,128)(2,1)S(1)} %get-tuple-element.34.pick1, bf16[1024,512]{1,0:T(8,128)(2,1)S(1)} %get-tuple-element.33.pick2, bf16[256,2048]{1,0:T(8,128)(2,1)S(1)} %pad_maximum_fusion.change, f32[8,128]{1,0:T(8,128)S(1)} %bitcast.57), custom_call_target="tpu_custom_call" | custom-call | tf_op jit(solution)/shard_map/react/pallas_call | solution.py:186
  71.6 0.9 copy-done
  72.5 4.5 %all-to-all-start.3 = ((f32[16,32,384]{2,1,0:T(8,128)}), f32[16,32,384]{2,1,0:T(8,128)}, u32[]{:S(2)}, u32[]{:S(2)}) async-start(f32[16,32,384]{2,1,0:T(8,128)} %bitcast.55), calls=%async_computation.3 | async-start | bytes 1572864 | tf_op jit(solution)/shard_map/all_to_all | solution.py:242
  77.0 7.3 %transport.2.cells = f32[256,768]{1,0:T(8,128)S(1)} custom-call(s32[2]{0:T(128)S(1)} %add_convert_fusion.swap, f32[2,2,1152]{2,1,0:T(2,128)S(1)} %get-tuple-element.14.winds, f32[2,256,384]{2,1,0:T(8,128)} %bitcast.18.own, f32[2,256,384]{2,1,0:T(8,128)} %bitcast.19.left, f32[2,256,384]{2,1,0:T(8,128)} %bitcast.20.right), custom_call_target="tpu_custom_call" | custom-call | tf_op jit(solution)/shard_map/transport/pallas_call | solution.py:151
  84.3 10.4 %react.2 = f32[2,256,384]{2,1,0:T(8,128)S(1)} custom-call(f32[256,768]{1,0:T(8,128)S(1)} %transport.2.cells, bf16[1024,512]{1,0:T(8,128)(2,1)S(1)} %get-tuple-element.34.pick1, bf16[1024,512]{1,0:T(8,128)(2,1)S(1)} %get-tuple-element.33.pick2, bf16[256,2048]{1,0:T(8,128)(2,1)S(1)} %pad_maximum_fusion.change, f32[8,128]{1,0:T(8,128)S(1)} %bitcast.58), custom_call_target="tpu_custom_call" | custom-call | tf_op jit(solution)/shard_map/react/pallas_call | solution.py:186
  94.8 0.9 copy-done.1
  95.6 22.8 %all_to_all.20 = f32[16,32,384]{2,1,0:T(8,128)} all-to-all(f32[16,32,384]{2,1,0:T(8,128)} %bitcast.56), channel_id=1, replica_groups=mesh['yhi'=2,'z'=8,'core'=2,'tracer'=8] {'yhi','tracer'}, dimensions={0} | all-to-all | bytes 1572864 | tf_op jit(solution)/shard_map/all_to_all | solution.py:242
  118.4 4.1 %from_blocks.1 = f32[3072,128]{1,0:T(8,128)} custom-call(f32[2,8,32,384]{3,2,1,0:T(8,128)} %bitcast.63, f32[2,8,32,384]{3,2,1,0:T(8,128)} %bitcast.32.refs_1_), custom_call_target="tpu_custom_call" | custom-call | tf_op jit(solution)/shard_map/from_blocks/pallas_call | solution.py:94
  (37 shorter events, 0.3 us)
Async XLA Ops:
  0.0 22.1 %collective-permute-start.2 = (f32[2,2,768]{2,1,0:T(2,128)}, f32[2,2,768]{2,1,0:T(2,128)S(1)}, u32[]{:S(2)}, u32[]{:S(2)}) collective-permute-start(f32[2,2,768]{2,1,0:T(2,128)} %param.7), channel_id=1, source_target_pairs={{128,0},{136,8},{144,16},{152,24},{160,32},{168,40},{176,48},{184,... | collective-permute-start | bytes 36872 | tf_op jit(solution)/shard_map/ppermute | solution.py:210
  3.2 19.1 %collective-permute-start.1 = (f32[2,2,768]{2,1,0:T(2,128)}, f32[2,2,768]{2,1,0:T(2,128)S(1)}, u32[]{:S(2)}, u32[]{:S(2)}) collective-permute-start(f32[2,2,768]{2,1,0:T(2,128)} %param.7), channel_id=1, source_target_pairs={{120,0},{128,8},{136,16},{144,24},{152,32},{160,40},{168,48},{176,... | collective-permute-start | bytes 36872 | tf_op jit(solution)/shard_map/ppermute | solution.py:210
  3.2 19.2 %collective-permute-start = (f32[2,2,768]{2,1,0:T(2,128)}, f32[2,2,768]{2,1,0:T(2,128)S(1)}, u32[]{:S(2)}, u32[]{:S(2)}) collective-permute-start(f32[2,2,768]{2,1,0:T(2,128)} %param.7), channel_id=1, source_target_pairs={{248,0},{0,8},{8,16},{16,24},{24,32},{32,40},{40,48},{48,56},{56,6... | collective-permute-start | bytes 36872 | tf_op jit(solution)/shard_map/ppermute | solution.py:210
  6.2 16.2 %collective-permute-start.4 = (f32[2,2,768]{2,1,0:T(2,128)}, f32[2,2,768]{2,1,0:T(2,128)S(1)}, u32[]{:S(2)}, u32[]{:S(2)}) collective-permute-start(f32[2,2,768]{2,1,0:T(2,128)} %param.7), channel_id=1, source_target_pairs={{136,0},{144,8},{152,16},{160,24},{168,32},{176,40},{184,48},{192,... | collective-permute-start | bytes 36872 | tf_op jit(solution)/shard_map/ppermute | solution.py:210
  7.3 15.2 %collective-permute-start.3 = (f32[2,2,768]{2,1,0:T(2,128)}, f32[2,2,768]{2,1,0:T(2,128)S(1)}, u32[]{:S(2)}, u32[]{:S(2)}) collective-permute-start(f32[2,2,768]{2,1,0:T(2,128)} %param.7), channel_id=1, source_target_pairs={{8,0},{16,8},{24,16},{32,24},{40,32},{48,40},{56,48},{64,56},{72,6... | collective-permute-start | bytes 36872 | tf_op jit(solution)/shard_map/ppermute | solution.py:210
  8.0 9.1 %copy-start.5 = (f32[2,2,768]{2,1,0:T(2,128)S(1)}, f32[2,2,768]{2,1,0:T(2,128)}, u32[]{:S(2)}) copy-start(f32[2,2,768]{2,1,0:T(2,128)} %param.7) | copy-start | bytes 36868
  11.8 22.4 %all-to-all-start.2 = ((f32[16,32,384]{2,1,0:T(8,128)}), f32[16,32,384]{2,1,0:T(8,128)}, u32[]{:S(2)}, u32[]{:S(2)}) async-start(f32[16,32,384]{2,1,0:T(8,128)} %bitcast.62), calls=%async_computation.2 | async-start | bytes 1572864 | tf_op jit(solution)/shard_map/all_to_all | solution.py:242
  17.1 3.8 %copy-start.3 = (s32[1024]{0:T(1024)S(1)}, s32[1024]{0:T(1024)}, u32[]{:S(2)}) copy-start(s32[1024]{0:T(1024)} %param.10) | copy-start | bytes 12292
  17.1 3.8 %copy-start.4 = (s32[1024]{0:T(1024)S(1)}, s32[1024]{0:T(1024)}, u32[]{:S(2)}) copy-start(s32[1024]{0:T(1024)} %param.9) | copy-start | bytes 12292
  17.1 3.8 %copy-start.6 = (s32[1024]{0:T(1024)S(1)}, s32[1024]{0:T(1024)}, u32[]{:S(2)}) copy-start(s32[1024]{0:T(1024)} %param.11) | copy-start | bytes 12292
  34.2 19.1 %all-to-all-start = ((f32[16,32,384]{2,1,0:T(8,128)}), f32[16,32,384]{2,1,0:T(8,128)}, u32[]{:S(2)}, u32[]{:S(2)}) async-start(f32[16,32,384]{2,1,0:T(8,128)} %bitcast.61), calls=%async_computation | async-start | bytes 1572864 | tf_op jit(solution)/shard_map/all_to_all | solution.py:242
  38.7 15.1 %collective-permute-start.8 = (f32[16,32,384]{2,1,0:T(8,128)}, f32[16,32,384]{2,1,0:T(8,128)}, u32[]{:S(2)}, u32[]{:S(2)}) collective-permute-start(f32[16,32,384]{2,1,0:T(8,128)} %all-to-all-done.2), channel_id=1, source_target_pairs={{8,0},{16,8},{24,16},{32,24},{40,32},{48,40},{56,48},{64,56},{72,6... | collective-permute-start | bytes 2359304 | tf_op jit(solution)/shard_map/ppermute | solution.py:199
  38.8 15.1 %collective-permute-start.7 = (f32[16,32,384]{2,1,0:T(8,128)}, f32[16,32,384]{2,1,0:T(8,128)}, u32[]{:S(2)}, u32[]{:S(2)}) collective-permute-start(f32[16,32,384]{2,1,0:T(8,128)} %all-to-all-done.2), channel_id=1, source_target_pairs={{0,8},{8,16},{16,24},{24,32},{32,40},{40,48},{48,56},{56,64},{64,7... | collective-permute-start | bytes 2359304 | tf_op jit(solution)/shard_map/ppermute | solution.py:198
  53.3 23.7 %collective-permute-start.6 = (f32[16,32,384]{2,1,0:T(8,128)}, f32[16,32,384]{2,1,0:T(8,128)}, u32[]{:S(2)}, u32[]{:S(2)}) collective-permute-start(f32[16,32,384]{2,1,0:T(8,128)} %all-to-all-done), channel_id=1, source_target_pairs={{8,0},{16,8},{24,16},{32,24},{40,32},{48,40},{56,48},{64,56},{72,6... | collective-permute-start | bytes 2359304 | tf_op jit(solution)/shard_map/ppermute | solution.py:199
  53.3 23.7 %collective-permute-start.5 = (f32[16,32,384]{2,1,0:T(8,128)}, f32[16,32,384]{2,1,0:T(8,128)}, u32[]{:S(2)}, u32[]{:S(2)}) collective-permute-start(f32[16,32,384]{2,1,0:T(8,128)} %all-to-all-done), channel_id=1, source_target_pairs={{0,8},{8,16},{16,24},{24,32},{32,40},{40,48},{48,56},{56,64},{64,7... | collective-permute-start | bytes 2359304 | tf_op jit(solution)/shard_map/ppermute | solution.py:198
  53.9 7.3 %copy-start.2 = (f32[1024]{0:T(1024)S(1)}, f32[1024]{0:T(1024)}, u32[]{:S(2)}) copy-start(f32[1024]{0:T(1024)} %param.8) | copy-start | bytes 12292
  71.6 0.9 copy-start
  72.5 23.1 %all-to-all-start.3 = ((f32[16,32,384]{2,1,0:T(8,128)}), f32[16,32,384]{2,1,0:T(8,128)}, u32[]{:S(2)}, u32[]{:S(2)}) async-start(f32[16,32,384]{2,1,0:T(8,128)} %bitcast.55), calls=%async_computation.3 | async-start | bytes 1572864 | tf_op jit(solution)/shard_map/all_to_all | solution.py:242
  94.7 0.9 copy-start.1

commit v4 on v2

--- a/solution.py
+++ b/solution.py
@@ -120,7 +120,9 @@
 
 def join_kernel(y_ref, *refs):
     x_ref = refs[-1]
-    groups, rows, twice = y_ref.shape
+    groups, _, twice = y_ref.shape
+    rows = x_ref.shape[0]
+    at = pl.ds(pl.multiple_of(pl.program_id(0) * rows, rows), rows)
     width = twice // 2
     pieces = width // LANES
     stride = x_ref.shape[1]
@@ -129,7 +131,7 @@
         for c in range(2):
             for m in range(pieces):
                 lane = c * width + m * LANES
-                flat[pl.ds(2 * (t * pieces + m) + c, rows, stride=stride), :] = y_ref[t, :, lane : lane + LANES]
+                flat[pl.ds(2 * (t * pieces + m) + c, rows, stride=stride), :] = y_ref[t, at, lane : lane + LANES]
 
 
 def join(blocks, so_far, chunk):
@@ -139,13 +141,13 @@
     return pl.pallas_call(
         join_kernel,
         grid=(own // 8,),
-        in_specs=[pl.BlockSpec((groups, 8, twice), lambda i: (0, i, 0))]
+        in_specs=[VMEM]
         + [pl.BlockSpec(memory_space=pl.ANY)] * len(more),
         out_specs=pl.BlockSpec((8, length, LANES), lambda i: (i, chunk, 0)),
         out_shape=jax.ShapeDtypeStruct((own, CHUNKS * length, LANES), F32),
         input_output_aliases={1: 0} if more else {},
         name="join",
-    )(blocks, *more)
+    )(pltpu.with_memory_space_constraint(blocks, pltpu.VMEM), *more)
 
 
 def split(values):
@@ -154,30 +156,42 @@
     return jnp.concatenate([high, low], axis=0)
 
 
-def react_kernel(cells, pick1, pick2, change, rates, out):
+def react_kernel(cells, pick1, pick2, change, rates, out, done, sems):
     amounts = cells[...]
     rate = jnp.concatenate(
         [jnp.broadcast_to(rates[i : i + 1, :], (LANES, LANES)).T for i in range(rates.shape[0])], axis=0
     )
     rate = jnp.concatenate([rate] * (amounts.shape[1] // LANES), axis=1)
+    tile = 256
+    copies = []
     for step in range(SUBSTEPS):
         parts = split(amounts)
         first = jnp.dot(pick1[...], parts, preferred_element_type=F32)
         second = jnp.dot(pick2[...], parts, preferred_element_type=F32)
         velocity = split(rate * first * second)
-        amounts = amounts + jnp.dot(change[...], velocity, preferred_element_type=F32)
-    out[...] = amounts
+        if step < SUBSTEPS - 1:
+            amounts = amounts + jnp.dot(change[...], velocity, preferred_element_type=F32)
+            continue
+        for n in range(amounts.shape[1] // tile):
+            lanes = slice(n * tile, (n + 1) * tile)
+            moved = jnp.dot(change[...], velocity[:, lanes], preferred_element_type=F32)
+            done[:, lanes] = amounts[:, lanes] + moved
+            copies.append(pltpu.make_async_copy(done.at[:, lanes], out.at[:, lanes], sems.at[n]))
+            copies[-1].start()
+    for copy in copies:
+        copy.wait()
 
 
 def react(cells, pick1, pick2, change, rates):
     return pl.pallas_call(
         react_kernel,
         in_specs=[VMEM] * 5,
-        out_specs=VMEM,
-        out_shape=jax.ShapeDtypeStruct(cells.shape, F32),
+        out_specs=pl.BlockSpec(memory_space=pltpu.HBM),
+        out_shape=pltpu.HBM(cells.shape, F32),
+        scratch_shapes=[pltpu.VMEM(cells.shape, F32), pltpu.SemaphoreType.DMA((cells.shape[1] // 256,))],
         compiler_params=pltpu.CompilerParams(vmem_limit_bytes=24 << 20),
         name="react",
-    )(cells, pick1, pick2, change, rates)
+    )(pltpu.with_memory_space_constraint(cells, pltpu.VMEM), pick1, pick2, change, rates)
 
 
 def neighbours(array):
@@ -212,14 +226,16 @@
 
     part = length // CHUNKS
     before, after = neighbours(fluxes)
+    section = jnp.stack([before, fluxes, after])
+    winds = exchange(jnp.broadcast_to(section, (groups, *section.shape)))
     own, sides = [], []
     for k in range(CHUNKS):
         raw = lax.slice_in_dim(tracers, k * part, (k + 1) * part, axis=2)
         raw, tracers = lax.optimization_barrier((raw, tracers))
         own.append(as_tiles(raw))
+        if k > 0:
+            own[k], winds = lax.optimization_barrier((own[k], winds))
         sides.append(neighbours(own[k]))
-    section = jnp.stack([before, fluxes, after])
-    winds = exchange(jnp.broadcast_to(section, (groups, *section.shape)))
     table = tables(first_reactant, second_reactant, product_species, rate_coeff)
     winds, table = lax.optimization_barrier((winds, table))
 

time: 115 us -> 108 us (0.939)
  waiting for transfers between devices: 37.4 us -> 32.4 us
  other arithmetic: 1.15 us -> 3.07 us
  local copies, waits for them, and re-layouts: 6.43 us -> 4.81 us
    all_to_all x5, waiting for transfers between devices: 37.4 us -> 32.4 us  [exchange(): lax.all_to_all(blocks, 'tracer', split_axis=0, concat_axis=0, tiled=True)]
    unnamed x18 -> x10, local copies, waits for them, and re-layouts: 2.64 us -> 0.02 us
    ppermute x3, starting transfers between devices: 2.16 us -> 0.2 us  [neighbours(): lax.ppermute(array, 'region', [(i, (i + 1) % count) for i in range(count)])]
    ppermute x3, starting transfers between devices: 3.48 us -> 5.1 us  [neighbours(): lax.ppermute(array, 'region', [((i + 1) % count, i) for i in range(count)])]
    transpose x0 -> x1, local copies, waits for them, and re-layouts: none -> 1.28 us  [as_tiles(): return jnp.transpose(tiles, (0, 2, 1, 3)).reshape(-1, LANES)]
    slice x2 -> x3, local copies, waits for them, and re-layouts: 3 us -> 2.07 us  [body(): raw = lax.slice_in_dim(tracers, k * part, (k + 1) * part, axis=2)]
  transfers between devices with their start and end apart: 11 -> 11, of which waited for: 5 -> 5; matrix products, arithmetic and copies ran while one was open for 4% -> 7% of each run, Pallas kernels for 30% -> 33%
where the time goes in v4:
time: 108 us; the launch traced here: 107 us
  Pallas kernels  36.9 us (34%)
  waiting for transfers between devices  32.4 us (30%)
  starting transfers between devices  29.5 us (27%)
  local copies, waits for them, and re-layouts  4.81 us (4%)
  other arithmetic  3.07 us (3%)
    all_to_all x5, waiting for transfers between devices, exchange(): lax.all_to_all(blocks, 'tracer', split_axis=0, concat_axis=0, tiled=True)  32.4 us
    pallas_call x2, Pallas kernels, react(): pl.pallas_call(react_kernel, in_specs=[VMEM] * 5, out_specs=pl.BlockSpec(...  24.5 us
    all_to_all x5, starting transfers between devices, exchange(): lax.all_to_all(blocks, 'tracer', split_axis=0, concat_axis=0, tiled=True)  24.2 us
    pallas_call x2, Pallas kernels, transport(): pl.pallas_call(functools.partial(transport_kernel, chunk), grid=(steps,),...  8.22 us
    ppermute x3, starting transfers between devices, neighbours(): lax.ppermute(array, 'region', [((i + 1) % count, i) for i in range(count)])  5.1 us
    pallas_call x2, Pallas kernels, join(): pl.pallas_call(join_kernel, grid=(own // 8,), in_specs=[VMEM] + [pl.Block...  4.23 us
  transfers between devices with their start and end apart: 11, of which 5 were waited for; matrix products, arithmetic and copies ran while one was open for 7% of the time, Pallas kernels for 33%

profile of v4, /device:TPU:224, one launch (start us, length us, event | category | flops | bytes accessed | tf_op | source)
XLA Modules:
  0.0 106.8 jit_solution(1347409355484760171)
XLA Ops:
  0.0 0.1 collective-permute-start
  0.1 1.7 %collective-permute-start.1 = (f32[2,2,768]{2,1,0:T(2,128)}, f32[2,2,768]{2,1,0:T(2,128)S(1)}, u32[]{:S(2)}, u32[]{:S(2)}) collective-permute-start(f32[2,2,768]{2,1,0:T(2,128)} %param.7), channel_id=1, source_target_pairs={{8,0},{16,8},{24,16},{32,24},{40,32},{48,40},{56,48},{64,56},{72,6... | collective-permute-start | bytes 36872 | tf_op jit(solution)/shard_map/ppermute | solution.py:200
  1.8 2.1 %slice.6 = f32[32,2,3072]{2,1,0:T(2,128)} slice(f32[32,2,6144]{2,1,0:T(2,128)} %param.6), slice={[0:32], [0:2], [0:3072]} | slice | bytes 1572864 | tf_op jit(solution)/shard_map/slice | solution.py:233
  3.9 0.0 collective-permute-start.4
  3.9 1.7 %collective-permute-start.5 = (f32[1536,128]{1,0:T(8,128)}, f32[1536,128]{1,0:T(8,128)}, u32[]{:S(2)}, u32[]{:S(2)}) collective-permute-start(f32[1536,128]{1,0:T(8,128)} %bitcast.13), channel_id=1, source_target_pairs={{8,0},{16,8},{24,16},{32,24},{40,32},{48,40},{56,48},{64,56},{72,6... | collective-permute-start | bytes 2359304 | tf_op jit(solution)/shard_map/ppermute | solution.py:200
  5.7 1.1 %subtract_convert_fusion = bf16[256,1024]{1,0:T(8,128)(2,1)} fusion(s32[1024]{0:T(1024)S(1)} %copy-done.1, s32[1024]{0:T(1024)S(1)} %copy-done.2, s32[1024]{0:T(1024)S(1)} %copy-done.4), kind=kLoop, calls=%fused_computation.3 | loop fusion | flops 2359296 | bytes 536576 | tf_op jit(solution)/shard_map/convert_element_type | solution.py:213
  6.8 0.6 reshape.62
  7.4 1.3 %copy.8 = f32[32,24,2,128]{3,2,1,0:T(2,128)} copy(f32[32,24,2,128]{3,1,2,0:T(8,128)S(1)} %bitcast.29) | data formatting | bytes 1572864 | tf_op jit(solution)/shard_map/transpose | solution.py:23
  8.7 0.0 collective-permute-done
  8.7 0.0 collective-permute-done.1
  8.8 0.8 broadcast_in_dim.2
  9.6 5.3 %all-to-all-start = ((f32[8,3,2,2,768]{4,3,2,1,0:T(2,128)}), f32[8,3,2,2,768]{4,3,2,1,0:T(2,128)S(1)}, u32[]{:S(2)}, u32[]{:S(2)}) async-start(f32[8,3,2,2,768]{4,3,2,1,0:T(2,128)} %broadcast_in_dim.2), calls=%async_computation | async-start | bytes 589824 | tf_op jit(solution)/shard_map/all_to_all | solution.py:219
  14.9 0.7 compare_convert_fusion
  15.5 10.8 %all-to-all-done.winds = f32[8,3,2,2,768]{4,3,2,1,0:T(2,128)S(1)} async-done(((f32[8,3,2,2,768]{4,3,2,1,0:T(2,128)}), f32[8,3,2,2,768]{4,3,2,1,0:T(2,128)S(1)}, u32[]{:S(2)}, u32[]{:S(2)}) %all-to-all-start) | async-done | bytes 294944 | tf_op jit(solution)/shard_map/all_to_all | solution.py:219
  26.3 0.1 collective-permute-start.2
  26.4 1.6 %collective-permute-start.3 = (f32[1536,128]{1,0:T(8,128)}, f32[1536,128]{1,0:T(8,128)}, u32[]{:S(2)}, u32[]{:S(2)}) collective-permute-start(f32[1536,128]{1,0:T(8,128)} %bitcast.1), channel_id=1, source_target_pairs={{8,0},{16,8},{24,16},{32,24},{40,32},{48,40},{56,48},{64,56},{72,6... | collective-permute-start | bytes 2359304 | tf_op jit(solution)/shard_map/ppermute | solution.py:200
  28.1 1.3 %pad_maximum_fusion.change = bf16[256,2048]{1,0:T(8,128)(2,1)S(1)} fusion(bf16[256,1024]{1,0:T(8,128)(2,1)} %subtract_convert_fusion), kind=kLoop, calls=%fused_computation.2 | loop fusion | flops 2097152 | bytes 1572864 | tf_op jit(solution)/shard_map/concatenate | solution.py:214
  29.4 4.1 %transport.3 = f32[8,32,768]{2,1,0:T(8,128)} custom-call(f32[8,3,2,2,768]{4,3,2,1,0:T(2,128)S(1)} %all-to-all-done.winds, f32[32,48,128]{2,1,0:T(8,128)} %bitcast.14.left, f32[32,48,128]{2,1,0:T(8,128)} %bitcast.16.own, f32[32,48,128]{2,1,0:T(8,128)} %bitcast.18.right), custom_call_target="tpu_custom_call" | custom-call | tf_op jit(solution)/shard_map/transport/pallas_call | solution.py:110
  33.5 5.1 %all-to-all-start.3 = ((f32[8,32,768]{2,1,0:T(8,128)}), f32[8,32,768]{2,1,0:T(8,128)}, u32[]{:S(2)}, u32[]{:S(2)}) async-start(f32[8,32,768]{2,1,0:T(8,128)} %transport.3), calls=%async_computation.3 | async-start | bytes 1572864 | tf_op jit(solution)/shard_map/all_to_all | solution.py:219
  38.6 0.0 collective-permute-done.3
  38.6 4.1 %transport.2 = f32[8,32,768]{2,1,0:T(8,128)} custom-call(f32[8,3,2,2,768]{4,3,2,1,0:T(2,128)S(1)} %all-to-all-done.winds, f32[32,48,128]{2,1,0:T(8,128)} %bitcast.6.left, f32[32,48,128]{2,1,0:T(8,128)} %bitcast.7.own, f32[32,48,128]{2,1,0:T(8,128)} %bitcast.8.right), custom_call_target="tpu_custom_call" | custom-call | tf_op jit(solution)/shard_map/transport/pallas_call | solution.py:110
  42.7 10.2 %all-to-all-done.3 = f32[8,32,768]{2,1,0:T(8,128)} async-done(((f32[8,32,768]{2,1,0:T(8,128)}), f32[8,32,768]{2,1,0:T(8,128)}, u32[]{:S(2)}, u32[]{:S(2)}) %all-to-all-start.3) | async-done | bytes 786464 | tf_op jit(solution)/shard_map/all_to_all | solution.py:219
  52.9 4.4 %all-to-all-start.1 = ((f32[8,32,768]{2,1,0:T(8,128)}), f32[8,32,768]{2,1,0:T(8,128)}, u32[]{:S(2)}, u32[]{:S(2)}) async-start(f32[8,32,768]{2,1,0:T(8,128)} %transport.2), calls=%async_computation.1 | async-start | bytes 1572864 | tf_op jit(solution)/shard_map/all_to_all | solution.py:219
  57.3 12.2 %react.3 = f32[256,768]{1,0:T(8,128)} custom-call(f32[256,768]{1,0:T(8,128)} %bitcast.19.cells, bf16[1024,512]{1,0:T(8,128)(2,1)S(1)} %get-tuple-element.20.pick1, bf16[1024,512]{1,0:T(8,128)(2,1)S(1)} %get-tuple-element.21.pick2, bf16[256,2048]{1,0:T(8,128)(2,1)S(1)} %pad_maximum_fusion.change, f32[8,128]{1,0:T(8,128)S(1)} %bitcast.27), custom_call_target="tpu_custom_call" | custom-call | tf_op jit(solution)/shard_map/react/pallas_call | solution.py:186
  69.5 1.1 all-to-all-done.1
  70.6 4.4 %all-to-all-start.4 = ((f32[8,32,768]{2,1,0:T(8,128)}), f32[8,32,768]{2,1,0:T(8,128)}, u32[]{:S(2)}, u32[]{:S(2)}) async-start(f32[8,32,768]{2,1,0:T(8,128)} %bitcast.30), calls=%async_computation.4 | async-start | bytes 1572864 | tf_op jit(solution)/shard_map/all_to_all | solution.py:219
  75.0 12.2 %react.2 = f32[256,768]{1,0:T(8,128)} custom-call(f32[256,768]{1,0:T(8,128)} %bitcast.9.cells, bf16[1024,512]{1,0:T(8,128)(2,1)S(1)} %get-tuple-element.20.pick1, bf16[1024,512]{1,0:T(8,128)(2,1)S(1)} %get-tuple-element.21.pick2, bf16[256,2048]{1,0:T(8,128)(2,1)S(1)} %pad_maximum_fusion.change, f32[8,128]{1,0:T(8,128)S(1)} %bitcast.28), custom_call_target="tpu_custom_call" | custom-call | tf_op jit(solution)/shard_map/react/pallas_call | solution.py:186
  87.3 0.7 all-to-all-done.4.y_ref
  88.0 5.0 %all-to-all-start.2 = ((f32[8,32,768]{2,1,0:T(8,128)}), f32[8,32,768]{2,1,0:T(8,128)S(1)}, u32[]{:S(2)}, u32[]{:S(2)}) async-start(f32[8,32,768]{2,1,0:T(8,128)} %bitcast.31), calls=%async_computation.2 | async-start | bytes 1572864 | tf_op jit(solution)/shard_map/all_to_all | solution.py:219
  92.9 2.7 %join.2.refs_0_ = f32[32,96,128]{2,1,0:T(8,128)} custom-call(f32[8,32,768]{2,1,0:T(8,128)} %all-to-all-done.4.y_ref), custom_call_target="tpu_custom_call" | custom-call | tf_op jit(solution)/shard_map/join/pallas_call | solution.py:141
  95.6 9.6 %all-to-all-done.2.y_ref = f32[8,32,768]{2,1,0:T(8,128)S(1)} async-done(((f32[8,32,768]{2,1,0:T(8,128)}), f32[8,32,768]{2,1,0:T(8,128)S(1)}, u32[]{:S(2)}, u32[]{:S(2)}) %all-to-all-start.2) | async-done | bytes 786464 | tf_op jit(solution)/shard_map/all_to_all | solution.py:219
  105.3 1.5 %join.3 = f32[32,96,128]{2,1,0:T(8,128)} custom-call(f32[8,32,768]{2,1,0:T(8,128)S(1)} %all-to-all-done.2.y_ref, f32[32,96,128]{2,1,0:T(8,128)} %join.2.refs_0_), custom_call_target="tpu_custom_call", output_to_operand_aliasing={{}: (1, {})} | custom-call | tf_op jit(solution)/shard_map/join/pallas_call | solution.py:141
  (17 shorter events, 0.1 us)
Async XLA Ops:
  0.0 6.8 %slice-start = ((f32[32,2,6144]{2,1,0:T(2,128)}), f32[32,2,3072]{2,1,0:T(2,128)S(1)}, s32[]{:S(2)}) async-start(f32[32,2,6144]{2,1,0:T(2,128)} %param.6), calls=%async_computation.5 | async-start | bytes 1572864 | tf_op jit(solution)/shard_map/slice | solution.py:233
  0.0 5.7 %copy-start.1 = (s32[1024]{0:T(1024)S(1)}, s32[1024]{0:T(1024)}, u32[]{:S(2)}) copy-start(s32[1024]{0:T(1024)} %param.10) | copy-start | bytes 12292
  0.0 5.7 %copy-start.2 = (s32[1024]{0:T(1024)S(1)}, s32[1024]{0:T(1024)}, u32[]{:S(2)}) copy-start(s32[1024]{0:T(1024)} %param.9) | copy-start | bytes 12292
  0.0 5.7 %copy-start.4 = (s32[1024]{0:T(1024)S(1)}, s32[1024]{0:T(1024)}, u32[]{:S(2)}) copy-start(s32[1024]{0:T(1024)} %param.11) | copy-start | bytes 12292
  0.0 8.7 %collective-permute-start = (f32[2,2,768]{2,1,0:T(2,128)}, f32[2,2,768]{2,1,0:T(2,128)S(1)}, u32[]{:S(2)}, u32[]{:S(2)}) collective-permute-start(f32[2,2,768]{2,1,0:T(2,128)} %param.7), channel_id=1, source_target_pairs={{0,8},{8,16},{16,24},{24,32},{32,40},{40,48},{48,56},{56,64},{64,7... | collective-permute-start | bytes 36872 | tf_op jit(solution)/shard_map/ppermute | solution.py:199
  0.1 8.6 %collective-permute-start.1 = (f32[2,2,768]{2,1,0:T(2,128)}, f32[2,2,768]{2,1,0:T(2,128)S(1)}, u32[]{:S(2)}, u32[]{:S(2)}) collective-permute-start(f32[2,2,768]{2,1,0:T(2,128)} %param.7), channel_id=1, source_target_pairs={{8,0},{16,8},{24,16},{32,24},{40,32},{48,40},{56,48},{64,56},{72,6... | collective-permute-start | bytes 36872 | tf_op jit(solution)/shard_map/ppermute | solution.py:200
  3.9 25.4 %collective-permute-start.4 = (f32[1536,128]{1,0:T(8,128)}, f32[1536,128]{1,0:T(8,128)}, u32[]{:S(2)}, u32[]{:S(2)}) collective-permute-start(f32[1536,128]{1,0:T(8,128)} %bitcast.13), channel_id=1, source_target_pairs={{0,8},{8,16},{16,24},{24,32},{32,40},{40,48},{48,56},{56,64},{64,7... | collective-permute-start | bytes 2359304 | tf_op jit(solution)/shard_map/ppermute | solution.py:199
  3.9 25.4 %collective-permute-start.5 = (f32[1536,128]{1,0:T(8,128)}, f32[1536,128]{1,0:T(8,128)}, u32[]{:S(2)}, u32[]{:S(2)}) collective-permute-start(f32[1536,128]{1,0:T(8,128)} %bitcast.13), channel_id=1, source_target_pairs={{8,0},{16,8},{24,16},{32,24},{40,32},{48,40},{56,48},{64,56},{72,6... | collective-permute-start | bytes 2359304 | tf_op jit(solution)/shard_map/ppermute | solution.py:200
  6.8 1.9 %copy-start.3 = (f32[2,2,768]{2,1,0:T(2,128)S(1)}, f32[2,2,768]{2,1,0:T(2,128)}, u32[]{:S(2)}) copy-start(f32[2,2,768]{2,1,0:T(2,128)} %param.7) | copy-start | bytes 36868
  9.6 16.8 %all-to-all-start = ((f32[8,3,2,2,768]{4,3,2,1,0:T(2,128)}), f32[8,3,2,2,768]{4,3,2,1,0:T(2,128)S(1)}, u32[]{:S(2)}, u32[]{:S(2)}) async-start(f32[8,3,2,2,768]{4,3,2,1,0:T(2,128)} %broadcast_in_dim.2), calls=%async_computation | async-start | bytes 589824 | tf_op jit(solution)/shard_map/all_to_all | solution.py:219
  26.3 12.3 %collective-permute-start.2 = (f32[1536,128]{1,0:T(8,128)}, f32[1536,128]{1,0:T(8,128)}, u32[]{:S(2)}, u32[]{:S(2)}) collective-permute-start(f32[1536,128]{1,0:T(8,128)} %bitcast.1), channel_id=1, source_target_pairs={{0,8},{8,16},{16,24},{24,32},{32,40},{40,48},{48,56},{56,64},{64,7... | collective-permute-start | bytes 2359304 | tf_op jit(solution)/shard_map/ppermute | solution.py:199
  26.4 12.2 %collective-permute-start.3 = (f32[1536,128]{1,0:T(8,128)}, f32[1536,128]{1,0:T(8,128)}, u32[]{:S(2)}, u32[]{:S(2)}) collective-permute-start(f32[1536,128]{1,0:T(8,128)} %bitcast.1), channel_id=1, source_target_pairs={{8,0},{16,8},{24,16},{32,24},{40,32},{48,40},{56,48},{64,56},{72,6... | collective-permute-start | bytes 2359304 | tf_op jit(solution)/shard_map/ppermute | solution.py:200
  33.5 19.4 %all-to-all-start.3 = ((f32[8,32,768]{2,1,0:T(8,128)}), f32[8,32,768]{2,1,0:T(8,128)}, u32[]{:S(2)}, u32[]{:S(2)}) async-start(f32[8,32,768]{2,1,0:T(8,128)} %transport.3), calls=%async_computation.3 | async-start | bytes 1572864 | tf_op jit(solution)/shard_map/all_to_all | solution.py:219
  42.7 14.6 %copy-start = (f32[1024]{0:T(1024)S(1)}, f32[1024]{0:T(1024)}, u32[]{:S(2)}) copy-start(f32[1024]{0:T(1024)} %param.8) | copy-start | bytes 12292
  52.9 17.7 %all-to-all-start.1 = ((f32[8,32,768]{2,1,0:T(8,128)}), f32[8,32,768]{2,1,0:T(8,128)}, u32[]{:S(2)}, u32[]{:S(2)}) async-start(f32[8,32,768]{2,1,0:T(8,128)} %transport.2), calls=%async_computation.1 | async-start | bytes 1572864 | tf_op jit(solution)/shard_map/all_to_all | solution.py:219
  70.6 17.4 %all-to-all-start.4 = ((f32[8,32,768]{2,1,0:T(8,128)}), f32[8,32,768]{2,1,0:T(8,128)}, u32[]{:S(2)}, u32[]{:S(2)}) async-start(f32[8,32,768]{2,1,0:T(8,128)} %bitcast.30), calls=%async_computation.4 | async-start | bytes 1572864 | tf_op jit(solution)/shard_map/all_to_all | solution.py:219
  88.0 17.3 %all-to-all-start.2 = ((f32[8,32,768]{2,1,0:T(8,128)}), f32[8,32,768]{2,1,0:T(8,128)S(1)}, u32[]{:S(2)}, u32[]{:S(2)}) async-start(f32[8,32,768]{2,1,0:T(8,128)} %bitcast.31), calls=%async_computation.2 | async-start | bytes 1572864 | tf_op jit(solution)/shard_map/all_to_all | solution.py:219

commit v5 on v4

--- a/solution.py
+++ b/solution.py
@@ -206,12 +206,12 @@
     pick1 = (first_reactant[:, None] == species[None, :]).astype(BF16)
     pick2 = (second_reactant[:, None] == species[None, :]).astype(BF16)
     kinds = jnp.arange(TRACERS, dtype=jnp.int32)[:, None]
+    first, second, product = (
+        jnp.concatenate([array, array])[None, :] for array in (first_reactant, second_reactant, product_species)
+    )
     change = (
-        (product_species[None, :] == kinds).astype(F32)
-        - (first_reactant[None, :] == kinds).astype(F32)
-        - (second_reactant[None, :] == kinds).astype(F32)
+        (product == kinds).astype(F32) - (first == kinds).astype(F32) - (second == kinds).astype(F32)
     ).astype(BF16)
-    change = jnp.concatenate([change, change], axis=1)
     return pick1, pick2, change, rate_coeff.reshape(-1, LANES)
 
 
@@ -226,18 +226,23 @@
 
     part = length // CHUNKS
     before, after = neighbours(fluxes)
+    own, sides = [], []
+    raw = lax.slice_in_dim(tracers, 0, part, axis=2)
+    raw, tracers = lax.optimization_barrier((raw, tracers))
+    own.append(as_tiles(raw))
+    sides.append(neighbours(own[0]))
     section = jnp.stack([before, fluxes, after])
-    winds = exchange(jnp.broadcast_to(section, (groups, *section.shape)))
-    own, sides = [], []
-    for k in range(CHUNKS):
-        raw = lax.slice_in_dim(tracers, k * part, (k + 1) * part, axis=2)
-        raw, tracers = lax.optimization_barrier((raw, tracers))
-        own.append(as_tiles(raw))
-        if k > 0:
-            own[k], winds = lax.optimization_barrier((own[k], winds))
-        sides.append(neighbours(own[k]))
-    table = tables(first_reactant, second_reactant, product_species, rate_coeff)
-    winds, table = lax.optimization_barrier((winds, table))
+    copies = jnp.broadcast_to(section, (groups, *section.shape))
+    copies, tracers, reactions = lax.optimization_barrier(
+        (copies, tracers, (first_reactant, second_reactant, product_species))
+    )
+    winds = exchange(copies)
+    table = tables(*reactions, rate_coeff)
+    tracers, table = lax.optimization_barrier((tracers, table))
+    raw = lax.slice_in_dim(tracers, part, 2 * part, axis=2)
+    raw, winds, table = lax.optimization_barrier((raw, winds, table))
+    own.append(as_tiles(raw))
+    sides.append(neighbours(own[1]))
 
     out = None
     for k in range(CHUNKS):

time: 108 us -> 106 us (0.981)
  other arithmetic: 3.07 us -> 1.35 us
    ppermute x3, starting transfers between devices: 0.2 us -> 4.79 us  [neighbours(): lax.ppermute(array, 'region', [(i, (i + 1) % count) for i in range(count)])]
    ppermute x3, starting transfers between devices: 5.1 us -> 2.23 us  [neighbours(): lax.ppermute(array, 'region', [((i + 1) % count, i) for i in range(count)])]
    transpose x1 -> x0, local copies, waits for them, and re-layouts: 1.28 us -> none  [as_tiles(): return jnp.transpose(tiles, (0, 2, 1, 3)).reshape(-1, LANES)]
    concatenate x1 -> x2, other arithmetic: 1.27 us -> 0.01 us  [tables(): jnp.concatenate([array, array])[None, :]]
    unnamed x10 -> x14, local copies, waits for them, and re-layouts: 0.02 us -> 1.22 us
    slice x3 -> x2, local copies, waits for them, and re-layouts: 2.07 us -> 2.99 us  [the longest x1 2.06 us: body(): raw = lax.slice_in_dim(tracers, 0, part, axis=2)]
  transfers between devices with their start and end apart: 11 -> 11, of which waited for: 5 -> 6; matrix products, arithmetic and copies ran while one was open for 7% -> 5% of each run, Pallas kernels for 33% -> 33%
where the time goes in v5:
time: 106 us
  Pallas kernels  36.8 us (35%)
  waiting for transfers between devices  32.2 us (30%)
  starting transfers between devices  30.2 us (28%)
  local copies, waits for them, and re-layouts  5.02 us (5%)
  other arithmetic  1.35 us (1%)
    all_to_all x5, waiting for transfers between devices, exchange(): lax.all_to_all(blocks, 'tracer', split_axis=0, concat_axis=0, tiled=True)  31.4 us
    pallas_call x2, Pallas kernels, react(): pl.pallas_call(react_kernel, in_specs=[VMEM] * 5, out_specs=pl.BlockSpec(...  24.5 us
    all_to_all x5, starting transfers between devices, exchange(): lax.all_to_all(blocks, 'tracer', split_axis=0, concat_axis=0, tiled=True)  23.2 us
    pallas_call x2, Pallas kernels, transport(): pl.pallas_call(functools.partial(transport_kernel, chunk), grid=(steps,),...  8.09 us
    ppermute x3, starting transfers between devices, neighbours(): lax.ppermute(array, 'region', [(i, (i + 1) % count) for i in range(count)])  4.79 us
    pallas_call x2, Pallas kernels, join(): pl.pallas_call(join_kernel, grid=(own // 8,), in_specs=[VMEM] + [pl.Block...  4.23 us
    ppermute x3, starting transfers between devices, neighbours(): lax.ppermute(array, 'region', [((i + 1) % count, i) for i in range(count)])  2.23 us
  transfers between devices with their start and end apart: 11, of which 6 were waited for; matrix products, arithmetic and copies ran while one was open for 5% of the time, Pallas kernels for 33%

profile of v5, /device:TPU:224, one launch (start us, length us, event | category | flops | bytes accessed | tf_op | source)
XLA Modules:
  0.0 105.7 jit_solution(15854120013147421471)
XLA Ops:
  0.0 0.5 collective-permute-start.1
  0.5 0.1 collective-permute-start
  0.6 2.1 %slice.6 = f32[32,2,3072]{2,1,0:T(2,128)} slice(f32[32,2,6144]{2,1,0:T(2,128)} %param.6), slice={[0:32], [0:2], [0:3072]} | slice | bytes 1572864 | tf_op jit(solution)/shard_map/slice | solution.py:230
  2.7 4.7 %collective-permute-start.4 = (f32[1536,128]{1,0:T(8,128)}, f32[1536,128]{1,0:T(8,128)}, u32[]{:S(2)}, u32[]{:S(2)}) collective-permute-start(f32[1536,128]{1,0:T(8,128)} %bitcast.16), channel_id=1, source_target_pairs={{0,8},{8,16},{16,24},{24,32},{32,40},{40,48},{48,56},{56,64},{64,7... | collective-permute-start | bytes 2359304 | tf_op jit(solution)/shard_map/ppermute | solution.py:199
  7.4 0.0 collective-permute-done.1
  7.4 0.8 broadcast_in_dim.2
  8.2 5.3 %all-to-all-start = ((f32[8,3,2,2,768]{4,3,2,1,0:T(2,128)}), f32[8,3,2,2,768]{4,3,2,1,0:T(2,128)S(1)}, u32[]{:S(2)}, u32[]{:S(2)}) async-start(f32[8,3,2,2,768]{4,3,2,1,0:T(2,128)} %broadcast_in_dim.2), calls=%async_computation | async-start | bytes 589824 | tf_op jit(solution)/shard_map/all_to_all | solution.py:219
  13.6 0.0 copy-start.2
  13.6 0.6 subtract_convert_fusion.change
  14.2 0.7 compare_convert_fusion
  14.9 0.1 copy-done.2
  15.0 0.9 slice.7
  15.9 10.4 %all-to-all-done.winds = f32[8,3,2,2,768]{4,3,2,1,0:T(2,128)S(1)} async-done(((f32[8,3,2,2,768]{4,3,2,1,0:T(2,128)}), f32[8,3,2,2,768]{4,3,2,1,0:T(2,128)S(1)}, u32[]{:S(2)}, u32[]{:S(2)}) %all-to-all-start) | async-done | bytes 294944 | tf_op jit(solution)/shard_map/all_to_all | solution.py:219
  26.3 0.0 collective-permute-start.2
  26.3 1.7 %collective-permute-start.3 = (f32[1536,128]{1,0:T(8,128)}, f32[1536,128]{1,0:T(8,128)}, u32[]{:S(2)}, u32[]{:S(2)}) collective-permute-start(f32[1536,128]{1,0:T(8,128)} %bitcast.32), channel_id=1, source_target_pairs={{8,0},{16,8},{24,16},{32,24},{40,32},{48,40},{56,48},{64,56},{72,6... | collective-permute-start | bytes 2359304 | tf_op jit(solution)/shard_map/ppermute | solution.py:200
  28.0 0.0 collective-permute-done.4
  28.0 4.1 %transport.3 = f32[8,32,768]{2,1,0:T(8,128)} custom-call(f32[8,3,2,2,768]{4,3,2,1,0:T(2,128)S(1)} %all-to-all-done.winds, f32[32,48,128]{2,1,0:T(8,128)} %bitcast.17.left, f32[32,48,128]{2,1,0:T(8,128)} %bitcast.19.own, f32[32,48,128]{2,1,0:T(8,128)} %bitcast.21.right), custom_call_target="tpu_custom_call" | custom-call | tf_op jit(solution)/shard_map/transport/pallas_call | solution.py:110
  32.1 5.1 %all-to-all-start.3 = ((f32[8,32,768]{2,1,0:T(8,128)}), f32[8,32,768]{2,1,0:T(8,128)}, u32[]{:S(2)}, u32[]{:S(2)}) async-start(f32[8,32,768]{2,1,0:T(8,128)} %transport.3), calls=%async_computation.3 | async-start | bytes 1572864 | tf_op jit(solution)/shard_map/all_to_all | solution.py:219
  37.2 0.8 collective-permute-done.2
  38.0 1.1 %copy-done = f32[32,2,3072]{2,1,0:T(2,128)S(1)} copy-done((f32[32,2,3072]{2,1,0:T(2,128)S(1)}, f32[32,2,3072]{2,1,0:T(2,128)}, u32[]{:S(2)}) %copy-start) | copy-done | bytes 786456
  39.1 4.0 %transport.2 = f32[8,32,768]{2,1,0:T(8,128)} custom-call(f32[8,3,2,2,768]{4,3,2,1,0:T(2,128)S(1)} %all-to-all-done.winds, f32[32,48,128]{2,1,0:T(8,128)} %bitcast.7.left, f32[32,48,128]{2,1,0:T(8,128)S(1)} %bitcast.33, f32[32,48,128]{2,1,0:T(8,128)} %bitcast.11.right), custom_call_target="tpu_custom_call" | custom-call | tf_op jit(solution)/shard_map/transport/pallas_call | solution.py:110
  43.1 6.5 %all-to-all-done.3 = f32[8,32,768]{2,1,0:T(8,128)} async-done(((f32[8,32,768]{2,1,0:T(8,128)}), f32[8,32,768]{2,1,0:T(8,128)}, u32[]{:S(2)}, u32[]{:S(2)}) %all-to-all-start.3) | async-done | bytes 786464 | tf_op jit(solution)/shard_map/all_to_all | solution.py:219
  49.6 4.7 %all-to-all-start.1 = ((f32[8,32,768]{2,1,0:T(8,128)}), f32[8,32,768]{2,1,0:T(8,128)}, u32[]{:S(2)}, u32[]{:S(2)}) async-start(f32[8,32,768]{2,1,0:T(8,128)} %transport.2), calls=%async_computation.1 | async-start | bytes 1572864 | tf_op jit(solution)/shard_map/all_to_all | solution.py:219
  54.4 12.2 %react.3 = f32[256,768]{1,0:T(8,128)} custom-call(f32[256,768]{1,0:T(8,128)} %bitcast.22.cells, bf16[1024,512]{1,0:T(8,128)(2,1)S(1)} %get-tuple-element.36.pick1, bf16[1024,512]{1,0:T(8,128)(2,1)S(1)} %get-tuple-element.37.pick2, bf16[256,2048]{1,0:T(8,128)(2,1)S(1)} %subtract_convert_fusion.change, f32[8,128]{1,0:T(8,128)S(1)} %bitcast.34), custom_call_target="tpu_custom_call" | custom-call | tf_op jit(solution)/shard_map/react/pallas_call | solution.py:186
  66.6 1.8 %all-to-all-done.1 = f32[8,32,768]{2,1,0:T(8,128)} async-done(((f32[8,32,768]{2,1,0:T(8,128)}), f32[8,32,768]{2,1,0:T(8,128)}, u32[]{:S(2)}, u32[]{:S(2)}) %all-to-all-start.1) | async-done | bytes 786464 | tf_op jit(solution)/shard_map/all_to_all | solution.py:219
  68.4 4.4 %all-to-all-start.4 = ((f32[8,32,768]{2,1,0:T(8,128)}), f32[8,32,768]{2,1,0:T(8,128)}, u32[]{:S(2)}, u32[]{:S(2)}) async-start(f32[8,32,768]{2,1,0:T(8,128)} %bitcast.36), calls=%async_computation.4 | async-start | bytes 1572864 | tf_op jit(solution)/shard_map/all_to_all | solution.py:219
  72.9 12.3 %react.2 = f32[256,768]{1,0:T(8,128)} custom-call(f32[256,768]{1,0:T(8,128)} %bitcast.12.cells, bf16[1024,512]{1,0:T(8,128)(2,1)S(1)} %get-tuple-element.36.pick1, bf16[1024,512]{1,0:T(8,128)(2,1)S(1)} %get-tuple-element.37.pick2, bf16[256,2048]{1,0:T(8,128)(2,1)S(1)} %subtract_convert_fusion.change, f32[8,128]{1,0:T(8,128)S(1)} %bitcast.35), custom_call_target="tpu_custom_call" | custom-call | tf_op jit(solution)/shard_map/react/pallas_call | solution.py:186
  85.1 1.8 %all-to-all-done.4.y_ref = f32[8,32,768]{2,1,0:T(8,128)} async-done(((f32[8,32,768]{2,1,0:T(8,128)}), f32[8,32,768]{2,1,0:T(8,128)}, u32[]{:S(2)}, u32[]{:S(2)}) %all-to-all-start.4) | async-done | bytes 786464 | tf_op jit(solution)/shard_map/all_to_all | solution.py:219
  86.9 3.7 %all-to-all-start.2 = ((f32[8,32,768]{2,1,0:T(8,128)}), f32[8,32,768]{2,1,0:T(8,128)S(1)}, u32[]{:S(2)}, u32[]{:S(2)}) async-start(f32[8,32,768]{2,1,0:T(8,128)} %bitcast.37), calls=%async_computation.2 | async-start | bytes 1572864 | tf_op jit(solution)/shard_map/all_to_all | solution.py:219
  90.5 2.7 %join.2.refs_0_ = f32[32,96,128]{2,1,0:T(8,128)} custom-call(f32[8,32,768]{2,1,0:T(8,128)} %all-to-all-done.4.y_ref), custom_call_target="tpu_custom_call" | custom-call | tf_op jit(solution)/shard_map/join/pallas_call | solution.py:141
  93.2 11.0 %all-to-all-done.2.y_ref = f32[8,32,768]{2,1,0:T(8,128)S(1)} async-done(((f32[8,32,768]{2,1,0:T(8,128)}), f32[8,32,768]{2,1,0:T(8,128)S(1)}, u32[]{:S(2)}, u32[]{:S(2)}) %all-to-all-start.2) | async-done | bytes 786464 | tf_op jit(solution)/shard_map/all_to_all | solution.py:219
  104.2 1.5 %join.3 = f32[32,96,128]{2,1,0:T(8,128)} custom-call(f32[8,32,768]{2,1,0:T(8,128)S(1)} %all-to-all-done.2.y_ref, f32[32,96,128]{2,1,0:T(8,128)} %join.2.refs_0_), custom_call_target="tpu_custom_call", output_to_operand_aliasing={{}: (1, {})} | custom-call | tf_op jit(solution)/shard_map/join/pallas_call | solution.py:141
  (19 shorter events, 0.1 us)
Async XLA Ops:
  0.0 7.4 %copy-start.5 = (f32[2,2,768]{2,1,0:T(2,128)S(1)}, f32[2,2,768]{2,1,0:T(2,128)}, u32[]{:S(2)}) copy-start(f32[2,2,768]{2,1,0:T(2,128)} %param.7) | copy-start | bytes 36868
  0.0 13.5 %copy-start.4 = (s32[1024]{0:T(1024)S(1)}, s32[1024]{0:T(1024)}, u32[]{:S(2)}) copy-start(s32[1024]{0:T(1024)} %param.9) | copy-start | bytes 12292
  0.0 8.2 %copy-start.3 = (s32[1024]{0:T(1024)S(1)}, s32[1024]{0:T(1024)}, u32[]{:S(2)}) copy-start(s32[1024]{0:T(1024)} %param.10) | copy-start | bytes 12292
  0.0 13.5 %copy-start.6 = (s32[1024]{0:T(1024)S(1)}, s32[1024]{0:T(1024)}, u32[]{:S(2)}) copy-start(s32[1024]{0:T(1024)} %param.11) | copy-start | bytes 12292
  0.0 7.3 %collective-permute-start.1 = (f32[2,2,768]{2,1,0:T(2,128)}, f32[2,2,768]{2,1,0:T(2,128)S(1)}, u32[]{:S(2)}, u32[]{:S(2)}) collective-permute-start(f32[2,2,768]{2,1,0:T(2,128)} %param.7), channel_id=1, source_target_pairs={{8,0},{16,8},{24,16},{32,24},{40,32},{48,40},{56,48},{64,56},{72,6... | collective-permute-start | bytes 36872 | tf_op jit(solution)/shard_map/ppermute | solution.py:200
  0.5 6.8 %collective-permute-start = (f32[2,2,768]{2,1,0:T(2,128)}, f32[2,2,768]{2,1,0:T(2,128)S(1)}, u32[]{:S(2)}, u32[]{:S(2)}) collective-permute-start(f32[2,2,768]{2,1,0:T(2,128)} %param.7), channel_id=1, source_target_pairs={{0,8},{8,16},{16,24},{24,32},{32,40},{40,48},{48,56},{56,64},{64,7... | collective-permute-start | bytes 36872 | tf_op jit(solution)/shard_map/ppermute | solution.py:199
  2.7 25.4 %collective-permute-start.4 = (f32[1536,128]{1,0:T(8,128)}, f32[1536,128]{1,0:T(8,128)}, u32[]{:S(2)}, u32[]{:S(2)}) collective-permute-start(f32[1536,128]{1,0:T(8,128)} %bitcast.16), channel_id=1, source_target_pairs={{0,8},{8,16},{16,24},{24,32},{32,40},{40,48},{48,56},{56,64},{64,7... | collective-permute-start | bytes 2359304 | tf_op jit(solution)/shard_map/ppermute | solution.py:199
  7.4 20.7 %collective-permute-start.5 = (f32[1536,128]{1,0:T(8,128)}, f32[1536,128]{1,0:T(8,128)}, u32[]{:S(2)}, u32[]{:S(2)}) collective-permute-start(f32[1536,128]{1,0:T(8,128)} %bitcast.16), channel_id=1, source_target_pairs={{8,0},{16,8},{24,16},{32,24},{40,32},{48,40},{56,48},{64,56},{72,6... | collective-permute-start | bytes 2359304 | tf_op jit(solution)/shard_map/ppermute | solution.py:200
  8.2 18.1 %all-to-all-start = ((f32[8,3,2,2,768]{4,3,2,1,0:T(2,128)}), f32[8,3,2,2,768]{4,3,2,1,0:T(2,128)S(1)}, u32[]{:S(2)}, u32[]{:S(2)}) async-start(f32[8,3,2,2,768]{4,3,2,1,0:T(2,128)} %broadcast_in_dim.2), calls=%async_computation | async-start | bytes 589824 | tf_op jit(solution)/shard_map/all_to_all | solution.py:219
  13.6 1.4 %copy-start.2 = (f32[32,2,6144]{2,1,0:T(2,128)S(1)}, f32[32,2,6144]{2,1,0:T(2,128)}, u32[]{:S(2)}) copy-start(f32[32,2,6144]{2,1,0:T(2,128)} %param.6) | copy-start | bytes 4718596
  26.3 11.7 %collective-permute-start.2 = (f32[1536,128]{1,0:T(8,128)}, f32[1536,128]{1,0:T(8,128)}, u32[]{:S(2)}, u32[]{:S(2)}) collective-permute-start(f32[1536,128]{1,0:T(8,128)} %bitcast.31), channel_id=1, source_target_pairs={{0,8},{8,16},{16,24},{24,32},{32,40},{40,48},{48,56},{56,64},{64,7... | collective-permute-start | bytes 2359304 | tf_op jit(solution)/shard_map/ppermute | solution.py:199
  26.3 11.7 %collective-permute-start.3 = (f32[1536,128]{1,0:T(8,128)}, f32[1536,128]{1,0:T(8,128)}, u32[]{:S(2)}, u32[]{:S(2)}) collective-permute-start(f32[1536,128]{1,0:T(8,128)} %bitcast.32), channel_id=1, source_target_pairs={{8,0},{16,8},{24,16},{32,24},{40,32},{48,40},{56,48},{64,56},{72,6... | collective-permute-start | bytes 2359304 | tf_op jit(solution)/shard_map/ppermute | solution.py:200
  32.1 17.5 %all-to-all-start.3 = ((f32[8,32,768]{2,1,0:T(8,128)}), f32[8,32,768]{2,1,0:T(8,128)}, u32[]{:S(2)}, u32[]{:S(2)}) async-start(f32[8,32,768]{2,1,0:T(8,128)} %transport.3), calls=%async_computation.3 | async-start | bytes 1572864 | tf_op jit(solution)/shard_map/all_to_all | solution.py:219
  38.0 1.1 %copy-start = (f32[32,2,3072]{2,1,0:T(2,128)S(1)}, f32[32,2,3072]{2,1,0:T(2,128)}, u32[]{:S(2)}) copy-start(f32[32,2,3072]{2,1,0:T(2,128)} %slice.7) | copy-start | bytes 2359300
  43.1 11.2 %copy-start.1 = (f32[1024]{0:T(1024)S(1)}, f32[1024]{0:T(1024)}, u32[]{:S(2)}) copy-start(f32[1024]{0:T(1024)} %param.8) | copy-start | bytes 12292
  49.6 18.8 %all-to-all-start.1 = ((f32[8,32,768]{2,1,0:T(8,128)}), f32[8,32,768]{2,1,0:T(8,128)}, u32[]{:S(2)}, u32[]{:S(2)}) async-start(f32[8,32,768]{2,1,0:T(8,128)} %transport.2), calls=%async_computation.1 | async-start | bytes 1572864 | tf_op jit(solution)/shard_map/all_to_all | solution.py:219
  68.4 18.5 %all-to-all-start.4 = ((f32[8,32,768]{2,1,0:T(8,128)}), f32[8,32,768]{2,1,0:T(8,128)}, u32[]{:S(2)}, u32[]{:S(2)}) async-start(f32[8,32,768]{2,1,0:T(8,128)} %bitcast.36), calls=%async_computation.4 | async-start | bytes 1572864 | tf_op jit(solution)/shard_map/all_to_all | solution.py:219
  86.9 17.3 %all-to-all-start.2 = ((f32[8,32,768]{2,1,0:T(8,128)}), f32[8,32,768]{2,1,0:T(8,128)S(1)}, u32[]{:S(2)}, u32[]{:S(2)}) async-start(f32[8,32,768]{2,1,0:T(8,128)} %bitcast.37), calls=%async_computation.2 | async-start | bytes 1572864 | tf_op jit(solution)/shard_map/all_to_all | solution.py:219

commit v6 on v5

--- a/solution.py
+++ b/solution.py
@@ -240,7 +240,7 @@
     table = tables(*reactions, rate_coeff)
     tracers, table = lax.optimization_barrier((tracers, table))
     raw = lax.slice_in_dim(tracers, part, 2 * part, axis=2)
-    raw, winds, table = lax.optimization_barrier((raw, winds, table))
+    raw, table = lax.optimization_barrier((raw, table))
     own.append(as_tiles(raw))
     sides.append(neighbours(own[1]))
 

time: 106 us -> 103 us (0.972)
  waiting for transfers between devices: 32.2 us -> 28.1 us
  starting transfers between devices: 30.2 us -> 32 us
  local copies, waits for them, and re-layouts: 5.02 us -> 3.87 us
    all_to_all x5, waiting for transfers between devices: 31.4 us -> 28 us  [exchange(): lax.all_to_all(blocks, 'tracer', split_axis=0, concat_axis=0, tiled=True)]
    all_to_all x5, starting transfers between devices: 23.2 us -> 25 us  [exchange(): lax.all_to_all(blocks, 'tracer', split_axis=0, concat_axis=0, tiled=True)]
    unnamed x14 -> x12, local copies, waits for them, and re-layouts: 1.22 us -> 0.09 us
  transfers between devices with their start and end apart: 11 -> 11, of which waited for: 6 -> 5; matrix products, arithmetic and copies ran while one was open for 5% -> 5% of each run, Pallas kernels for 33% -> 35%
where the time goes in v6:
time: 103 us; the launch traced here: 102 us
  Pallas kernels  36.9 us (36%)
  starting transfers between devices  32 us (31%)
  waiting for transfers between devices  28.1 us (27%)
  local copies, waits for them, and re-layouts  3.87 us (4%)
  other arithmetic  1.35 us (1%)
    all_to_all x5, waiting for transfers between devices, exchange(): lax.all_to_all(blocks, 'tracer', split_axis=0, concat_axis=0, tiled=True)  28 us
    all_to_all x5, starting transfers between devices, exchange(): lax.all_to_all(blocks, 'tracer', split_axis=0, concat_axis=0, tiled=True)  25 us
    pallas_call x2, Pallas kernels, react(): pl.pallas_call(react_kernel, in_specs=[VMEM] * 5, out_specs=pl.BlockSpec(...  24.5 us
    pallas_call x2, Pallas kernels, transport(): pl.pallas_call(functools.partial(transport_kernel, chunk), grid=(steps,),...  8.22 us
    ppermute x3, starting transfers between devices, neighbours(): lax.ppermute(array, 'region', [(i, (i + 1) % count) for i in range(count)])  4.97 us
    pallas_call x2, Pallas kernels, join(): pl.pallas_call(join_kernel, grid=(own // 8,), in_specs=[VMEM] + [pl.Block...  4.23 us
    slice x1, local copies, waits for them, and re-layouts, body(): raw = lax.slice_in_dim(tracers, 0, part, axis=2)  2.06 us
  transfers between devices with their start and end apart: 11, of which 5 were waited for; matrix products, arithmetic and copies ran while one was open for 5% of the time, Pallas kernels for 35%

profile of v6, /device:TPU:224, one launch (start us, length us, event | category | flops | bytes accessed | tf_op | source)
XLA Modules:
  0.0 102.3 jit_solution(14968290231179853879)
XLA Ops:
  0.0 0.5 collective-permute-start.1
  0.5 0.1 collective-permute-start
  0.6 2.1 %slice.6 = f32[32,2,3072]{2,1,0:T(2,128)} slice(f32[32,2,6144]{2,1,0:T(2,128)} %param.6), slice={[0:32], [0:2], [0:3072]} | slice | bytes 1572864 | tf_op jit(solution)/shard_map/slice | solution.py:230
  2.7 4.7 %collective-permute-start.4 = (f32[1536,128]{1,0:T(8,128)}, f32[1536,128]{1,0:T(8,128)}, u32[]{:S(2)}, u32[]{:S(2)}) collective-permute-start(f32[1536,128]{1,0:T(8,128)} %bitcast.16), channel_id=1, source_target_pairs={{0,8},{8,16},{16,24},{24,32},{32,40},{40,48},{48,56},{56,64},{64,7... | collective-permute-start | bytes 2359304 | tf_op jit(solution)/shard_map/ppermute | solution.py:199
  7.4 0.0 collective-permute-start.5
  7.4 0.0 collective-permute-done.1
  7.4 0.0 collective-permute-done
  7.4 0.8 broadcast_in_dim.2
  8.2 5.3 %all-to-all-start = ((f32[8,3,2,2,768]{4,3,2,1,0:T(2,128)}), f32[8,3,2,2,768]{4,3,2,1,0:T(2,128)S(1)}, u32[]{:S(2)}, u32[]{:S(2)}) async-start(f32[8,3,2,2,768]{4,3,2,1,0:T(2,128)} %broadcast_in_dim.2), calls=%async_computation | async-start | bytes 589824 | tf_op jit(solution)/shard_map/all_to_all | solution.py:219
  13.6 0.0 copy-start.1
  13.6 0.6 subtract_convert_fusion.change
  14.2 0.7 compare_convert_fusion
  14.9 0.1 copy-done.1
  15.0 0.9 slice.7
  15.9 0.2 collective-permute-start.2
  16.1 1.5 %collective-permute-start.3 = (f32[1536,128]{1,0:T(8,128)}, f32[1536,128]{1,0:T(8,128)}, u32[]{:S(2)}, u32[]{:S(2)}) collective-permute-start(f32[1536,128]{1,0:T(8,128)} %bitcast.6), channel_id=1, source_target_pairs={{8,0},{16,8},{24,16},{32,24},{40,32},{48,40},{56,48},{64,56},{72,6... | collective-permute-start | bytes 2359304 | tf_op jit(solution)/shard_map/ppermute | solution.py:200
  17.6 8.6 %all-to-all-done.winds = f32[8,3,2,2,768]{4,3,2,1,0:T(2,128)S(1)} async-done(((f32[8,3,2,2,768]{4,3,2,1,0:T(2,128)}), f32[8,3,2,2,768]{4,3,2,1,0:T(2,128)S(1)}, u32[]{:S(2)}, u32[]{:S(2)}) %all-to-all-start) | async-done | bytes 294944 | tf_op jit(solution)/shard_map/all_to_all | solution.py:219
  26.3 0.0 collective-permute-done.4
  26.3 4.1 %transport.3 = f32[8,32,768]{2,1,0:T(8,128)} custom-call(f32[8,3,2,2,768]{4,3,2,1,0:T(2,128)S(1)} %all-to-all-done.winds, f32[32,48,128]{2,1,0:T(8,128)} %bitcast.17.left, f32[32,48,128]{2,1,0:T(8,128)} %bitcast.19.own, f32[32,48,128]{2,1,0:T(8,128)} %bitcast.21.right), custom_call_target="tpu_custom_call" | custom-call | tf_op jit(solution)/shard_map/transport/pallas_call | solution.py:110
  30.4 5.1 %all-to-all-start.3 = ((f32[8,32,768]{2,1,0:T(8,128)}), f32[8,32,768]{2,1,0:T(8,128)}, u32[]{:S(2)}, u32[]{:S(2)}) async-start(f32[8,32,768]{2,1,0:T(8,128)} %transport.3), calls=%async_computation.3 | async-start | bytes 1572864 | tf_op jit(solution)/shard_map/all_to_all | solution.py:219
  35.5 4.1 %transport.2 = f32[8,32,768]{2,1,0:T(8,128)} custom-call(f32[8,3,2,2,768]{4,3,2,1,0:T(2,128)S(1)} %all-to-all-done.winds, f32[32,48,128]{2,1,0:T(8,128)} %bitcast.7.left, f32[32,48,128]{2,1,0:T(8,128)} %bitcast.9.own, f32[32,48,128]{2,1,0:T(8,128)} %bitcast.11.right), custom_call_target="tpu_custom_call" | custom-call | tf_op jit(solution)/shard_map/transport/pallas_call | solution.py:110
  39.6 9.2 %all-to-all-done.3 = f32[8,32,768]{2,1,0:T(8,128)} async-done(((f32[8,32,768]{2,1,0:T(8,128)}), f32[8,32,768]{2,1,0:T(8,128)}, u32[]{:S(2)}, u32[]{:S(2)}) %all-to-all-start.3) | async-done | bytes 786464 | tf_op jit(solution)/shard_map/all_to_all | solution.py:219
  48.8 4.4 %all-to-all-start.1 = ((f32[8,32,768]{2,1,0:T(8,128)}), f32[8,32,768]{2,1,0:T(8,128)}, u32[]{:S(2)}, u32[]{:S(2)}) async-start(f32[8,32,768]{2,1,0:T(8,128)} %transport.2), calls=%async_computation.1 | async-start | bytes 1572864 | tf_op jit(solution)/shard_map/all_to_all | solution.py:219
  53.2 12.2 %react.3 = f32[256,768]{1,0:T(8,128)} custom-call(f32[256,768]{1,0:T(8,128)} %bitcast.22.cells, bf16[1024,512]{1,0:T(8,128)(2,1)S(1)} %get-tuple-element.34.pick1, bf16[1024,512]{1,0:T(8,128)(2,1)S(1)} %get-tuple-element.35.pick2, bf16[256,2048]{1,0:T(8,128)(2,1)S(1)} %subtract_convert_fusion.change, f32[8,128]{1,0:T(8,128)S(1)} %bitcast.31), custom_call_target="tpu_custom_call" | custom-call | tf_op jit(solution)/shard_map/react/pallas_call | solution.py:186
  65.4 0.7 all-to-all-done.1
  66.1 4.8 %all-to-all-start.4 = ((f32[8,32,768]{2,1,0:T(8,128)}), f32[8,32,768]{2,1,0:T(8,128)}, u32[]{:S(2)}, u32[]{:S(2)}) async-start(f32[8,32,768]{2,1,0:T(8,128)} %bitcast.33), calls=%async_computation.4 | async-start | bytes 1572864 | tf_op jit(solution)/shard_map/all_to_all | solution.py:219
  70.9 12.2 %react.2 = f32[256,768]{1,0:T(8,128)} custom-call(f32[256,768]{1,0:T(8,128)} %bitcast.12.cells, bf16[1024,512]{1,0:T(8,128)(2,1)S(1)} %get-tuple-element.34.pick1, bf16[1024,512]{1,0:T(8,128)(2,1)S(1)} %get-tuple-element.35.pick2, bf16[256,2048]{1,0:T(8,128)(2,1)S(1)} %subtract_convert_fusion.change, f32[8,128]{1,0:T(8,128)S(1)} %bitcast.32), custom_call_target="tpu_custom_call" | custom-call | tf_op jit(solution)/shard_map/react/pallas_call | solution.py:186
  83.1 0.3 all-to-all-done.4.y_ref
  83.5 5.4 %all-to-all-start.2 = ((f32[8,32,768]{2,1,0:T(8,128)}), f32[8,32,768]{2,1,0:T(8,128)S(1)}, u32[]{:S(2)}, u32[]{:S(2)}) async-start(f32[8,32,768]{2,1,0:T(8,128)} %bitcast.34), calls=%async_computation.2 | async-start | bytes 1572864 | tf_op jit(solution)/shard_map/all_to_all | solution.py:219
  88.9 2.7 %join.2.refs_0_ = f32[32,96,128]{2,1,0:T(8,128)} custom-call(f32[8,32,768]{2,1,0:T(8,128)} %all-to-all-done.4.y_ref), custom_call_target="tpu_custom_call" | custom-call | tf_op jit(solution)/shard_map/join/pallas_call | solution.py:141
  91.5 9.2 %all-to-all-done.2.y_ref = f32[8,32,768]{2,1,0:T(8,128)S(1)} async-done(((f32[8,32,768]{2,1,0:T(8,128)}), f32[8,32,768]{2,1,0:T(8,128)S(1)}, u32[]{:S(2)}, u32[]{:S(2)}) %all-to-all-start.2) | async-done | bytes 786464 | tf_op jit(solution)/shard_map/all_to_all | solution.py:219
  100.8 1.5 %join.3 = f32[32,96,128]{2,1,0:T(8,128)} custom-call(f32[8,32,768]{2,1,0:T(8,128)S(1)} %all-to-all-done.2.y_ref, f32[32,96,128]{2,1,0:T(8,128)} %join.2.refs_0_), custom_call_target="tpu_custom_call", output_to_operand_aliasing={{}: (1, {})} | custom-call | tf_op jit(solution)/shard_map/join/pallas_call | solution.py:141
  (17 shorter events, 0.1 us)
Async XLA Ops:
  0.0 7.4 %copy-start.4 = (f32[2,2,768]{2,1,0:T(2,128)S(1)}, f32[2,2,768]{2,1,0:T(2,128)}, u32[]{:S(2)}) copy-start(f32[2,2,768]{2,1,0:T(2,128)} %param.7) | copy-start | bytes 36868
  0.0 13.5 %copy-start.3 = (s32[1024]{0:T(1024)S(1)}, s32[1024]{0:T(1024)}, u32[]{:S(2)}) copy-start(s32[1024]{0:T(1024)} %param.9) | copy-start | bytes 12292
  0.0 13.5 %copy-start.2 = (s32[1024]{0:T(1024)S(1)}, s32[1024]{0:T(1024)}, u32[]{:S(2)}) copy-start(s32[1024]{0:T(1024)} %param.10) | copy-start | bytes 12292
  0.0 13.5 %copy-start.5 = (s32[1024]{0:T(1024)S(1)}, s32[1024]{0:T(1024)}, u32[]{:S(2)}) copy-start(s32[1024]{0:T(1024)} %param.11) | copy-start | bytes 12292
  0.0 7.3 %collective-permute-start.1 = (f32[2,2,768]{2,1,0:T(2,128)}, f32[2,2,768]{2,1,0:T(2,128)S(1)}, u32[]{:S(2)}, u32[]{:S(2)}) collective-permute-start(f32[2,2,768]{2,1,0:T(2,128)} %param.7), channel_id=1, source_target_pairs={{8,0},{16,8},{24,16},{32,24},{40,32},{48,40},{56,48},{64,56},{72,6... | collective-permute-start | bytes 36872 | tf_op jit(solution)/shard_map/ppermute | solution.py:200
  0.5 6.8 %collective-permute-start = (f32[2,2,768]{2,1,0:T(2,128)}, f32[2,2,768]{2,1,0:T(2,128)S(1)}, u32[]{:S(2)}, u32[]{:S(2)}) collective-permute-start(f32[2,2,768]{2,1,0:T(2,128)} %param.7), channel_id=1, source_target_pairs={{0,8},{8,16},{16,24},{24,32},{32,40},{40,48},{48,56},{56,64},{64,7... | collective-permute-start | bytes 36872 | tf_op jit(solution)/shard_map/ppermute | solution.py:199
  2.7 23.6 %collective-permute-start.4 = (f32[1536,128]{1,0:T(8,128)}, f32[1536,128]{1,0:T(8,128)}, u32[]{:S(2)}, u32[]{:S(2)}) collective-permute-start(f32[1536,128]{1,0:T(8,128)} %bitcast.16), channel_id=1, source_target_pairs={{0,8},{8,16},{16,24},{24,32},{32,40},{40,48},{48,56},{56,64},{64,7... | collective-permute-start | bytes 2359304 | tf_op jit(solution)/shard_map/ppermute | solution.py:199
  7.4 18.9 %collective-permute-start.5 = (f32[1536,128]{1,0:T(8,128)}, f32[1536,128]{1,0:T(8,128)}, u32[]{:S(2)}, u32[]{:S(2)}) collective-permute-start(f32[1536,128]{1,0:T(8,128)} %bitcast.16), channel_id=1, source_target_pairs={{8,0},{16,8},{24,16},{32,24},{40,32},{48,40},{56,48},{64,56},{72,6... | collective-permute-start | bytes 2359304 | tf_op jit(solution)/shard_map/ppermute | solution.py:200
  8.2 18.1 %all-to-all-start = ((f32[8,3,2,2,768]{4,3,2,1,0:T(2,128)}), f32[8,3,2,2,768]{4,3,2,1,0:T(2,128)S(1)}, u32[]{:S(2)}, u32[]{:S(2)}) async-start(f32[8,3,2,2,768]{4,3,2,1,0:T(2,128)} %broadcast_in_dim.2), calls=%async_computation | async-start | bytes 589824 | tf_op jit(solution)/shard_map/all_to_all | solution.py:219
  13.6 1.4 %copy-start.1 = (f32[32,2,6144]{2,1,0:T(2,128)S(1)}, f32[32,2,6144]{2,1,0:T(2,128)}, u32[]{:S(2)}) copy-start(f32[32,2,6144]{2,1,0:T(2,128)} %param.6) | copy-start | bytes 4718596
  15.9 19.6 %collective-permute-start.2 = (f32[1536,128]{1,0:T(8,128)}, f32[1536,128]{1,0:T(8,128)}, u32[]{:S(2)}, u32[]{:S(2)}) collective-permute-start(f32[1536,128]{1,0:T(8,128)} %bitcast.6), channel_id=1, source_target_pairs={{0,8},{8,16},{16,24},{24,32},{32,40},{40,48},{48,56},{56,64},{64,7... | collective-permute-start | bytes 2359304 | tf_op jit(solution)/shard_map/ppermute | solution.py:199
  16.1 19.4 %collective-permute-start.3 = (f32[1536,128]{1,0:T(8,128)}, f32[1536,128]{1,0:T(8,128)}, u32[]{:S(2)}, u32[]{:S(2)}) collective-permute-start(f32[1536,128]{1,0:T(8,128)} %bitcast.6), channel_id=1, source_target_pairs={{8,0},{16,8},{24,16},{32,24},{40,32},{48,40},{56,48},{64,56},{72,6... | collective-permute-start | bytes 2359304 | tf_op jit(solution)/shard_map/ppermute | solution.py:200
  30.4 18.4 %all-to-all-start.3 = ((f32[8,32,768]{2,1,0:T(8,128)}), f32[8,32,768]{2,1,0:T(8,128)}, u32[]{:S(2)}, u32[]{:S(2)}) async-start(f32[8,32,768]{2,1,0:T(8,128)} %transport.3), calls=%async_computation.3 | async-start | bytes 1572864 | tf_op jit(solution)/shard_map/all_to_all | solution.py:219
  39.6 13.6 %copy-start = (f32[1024]{0:T(1024)S(1)}, f32[1024]{0:T(1024)}, u32[]{:S(2)}) copy-start(f32[1024]{0:T(1024)} %param.8) | copy-start | bytes 12292
  48.8 17.3 %all-to-all-start.1 = ((f32[8,32,768]{2,1,0:T(8,128)}), f32[8,32,768]{2,1,0:T(8,128)}, u32[]{:S(2)}, u32[]{:S(2)}) async-start(f32[8,32,768]{2,1,0:T(8,128)} %transport.2), calls=%async_computation.1 | async-start | bytes 1572864 | tf_op jit(solution)/shard_map/all_to_all | solution.py:219
  66.1 17.4 %all-to-all-start.4 = ((f32[8,32,768]{2,1,0:T(8,128)}), f32[8,32,768]{2,1,0:T(8,128)}, u32[]{:S(2)}, u32[]{:S(2)}) async-start(f32[8,32,768]{2,1,0:T(8,128)} %bitcast.33), calls=%async_computation.4 | async-start | bytes 1572864 | tf_op jit(solution)/shard_map/all_to_all | solution.py:219
  83.5 17.3 %all-to-all-start.2 = ((f32[8,32,768]{2,1,0:T(8,128)}), f32[8,32,768]{2,1,0:T(8,128)S(1)}, u32[]{:S(2)}, u32[]{:S(2)}) async-start(f32[8,32,768]{2,1,0:T(8,128)} %bitcast.34), calls=%async_computation.2 | async-start | bytes 1572864 | tf_op jit(solution)/shard_map/all_to_all | solution.py:219

commit v7 on v6

--- a/solution.py
+++ b/solution.py
@@ -156,42 +156,54 @@
     return jnp.concatenate([high, low], axis=0)
 
 
-def react_kernel(cells, pick1, pick2, change, rates, out, done, sems):
-    amounts = cells[...]
+def react_kernel(cells, pick1, pick2, change, rates, out, held, sems):
+    tile = 256
+    count = cells.shape[1] // tile
     rate = jnp.concatenate(
         [jnp.broadcast_to(rates[i : i + 1, :], (LANES, LANES)).T for i in range(rates.shape[0])], axis=0
     )
-    rate = jnp.concatenate([rate] * (amounts.shape[1] // LANES), axis=1)
-    tile = 256
-    copies = []
+    rate = jnp.concatenate([rate] * (tile // LANES), axis=1)
+    lanes = [slice(n * tile, (n + 1) * tile) for n in range(count)]
+    loads = [pltpu.make_async_copy(cells.at[:, at], held.at[:, at], sems.at[0, n]) for n, at in enumerate(lanes)]
+    stores = [pltpu.make_async_copy(held.at[:, at], out.at[:, at], sems.at[1, n]) for n, at in enumerate(lanes)]
+    for load in loads:
+        load.start()
+    amounts = [None] * count
+
+    def finish(step, n, first, second):
+        velocity = split(rate * first * second)
+        amounts[n] = amounts[n] + jnp.dot(change[...], velocity, preferred_element_type=F32)
+        if step == SUBSTEPS - 1:
+            held[:, lanes[n]] = amounts[n]
+            stores[n].start()
+
+    pending = None
     for step in range(SUBSTEPS):
-        parts = split(amounts)
-        first = jnp.dot(pick1[...], parts, preferred_element_type=F32)
-        second = jnp.dot(pick2[...], parts, preferred_element_type=F32)
-        velocity = split(rate * first * second)
-        if step < SUBSTEPS - 1:
-            amounts = amounts + jnp.dot(change[...], velocity, preferred_element_type=F32)
-            continue
-        for n in range(amounts.shape[1] // tile):
-            lanes = slice(n * tile, (n + 1) * tile)
-            moved = jnp.dot(change[...], velocity[:, lanes], preferred_element_type=F32)
-            done[:, lanes] = amounts[:, lanes] + moved
-            copies.append(pltpu.make_async_copy(done.at[:, lanes], out.at[:, lanes], sems.at[n]))
-            copies[-1].start()
-    for copy in copies:
-        copy.wait()
+        for n in range(count):
+            if step == 0:
+                loads[n].wait()
+                amounts[n] = held[:, lanes[n]]
+            parts = split(amounts[n])
+            first = jnp.dot(pick1[...], parts, preferred_element_type=F32)
+            second = jnp.dot(pick2[...], parts, preferred_element_type=F32)
+            if pending is not None:
+                finish(*pending)
+            pending = (step, n, first, second)
+    finish(*pending)
+    for store in stores:
+        store.wait()
 
 
 def react(cells, pick1, pick2, change, rates):
     return pl.pallas_call(
         react_kernel,
-        in_specs=[VMEM] * 5,
+        in_specs=[pl.BlockSpec(memory_space=pl.ANY)] + [VMEM] * 4,
         out_specs=pl.BlockSpec(memory_space=pltpu.HBM),
         out_shape=pltpu.HBM(cells.shape, F32),
-        scratch_shapes=[pltpu.VMEM(cells.shape, F32), pltpu.SemaphoreType.DMA((cells.shape[1] // 256,))],
+        scratch_shapes=[pltpu.VMEM(cells.shape, F32), pltpu.SemaphoreType.DMA((2, cells.shape[1] // 256))],
         compiler_params=pltpu.CompilerParams(vmem_limit_bytes=24 << 20),
         name="react",
-    )(pltpu.with_memory_space_constraint(cells, pltpu.VMEM), pick1, pick2, change, rates)
+    )(cells, pick1, pick2, change, rates)
 
 
 def neighbours(array):

time: 103 us -> 104 us (level)
  transfers between devices with their start and end apart: 11 -> 11, of which waited for: 5 -> 4; matrix products, arithmetic and copies ran while one was open for 5% -> 5% of each run, Pallas kernels for 35% -> 35%
where the time goes in v7:
time: 104 us; the launch traced here: 103 us
  Pallas kernels  37.7 us (36%)
  starting transfers between devices  32.7 us (31%)
  waiting for transfers between devices  27.3 us (26%)
  local copies, waits for them, and re-layouts  3.87 us (4%)
  other arithmetic  1.35 us (1%)
    all_to_all x5, waiting for transfers between devices, exchange(): lax.all_to_all(blocks, 'tracer', split_axis=0, concat_axis=0, tiled=True)  27.3 us
    all_to_all x5, starting transfers between devices, exchange(): lax.all_to_all(blocks, 'tracer', split_axis=0, concat_axis=0, tiled=True)  25.7 us
    pallas_call x2, Pallas kernels, react(): pl.pallas_call(react_kernel, in_specs=[pl.BlockSpec(memory_space=pl.ANY)]...  25.3 us
    pallas_call x2, Pallas kernels, transport(): pl.pallas_call(functools.partial(transport_kernel, chunk), grid=(steps,),...  8.22 us
    ppermute x3, starting transfers between devices, neighbours(): lax.ppermute(array, 'region', [(i, (i + 1) % count) for i in range(count)])  4.97 us
    pallas_call x2, Pallas kernels, join(): pl.pallas_call(join_kernel, grid=(own // 8,), in_specs=[VMEM] + [pl.Block...  4.23 us
  transfers between devices with their start and end apart: 11, of which 4 were waited for; matrix products, arithmetic and copies ran while one was open for 5% of the time, Pallas kernels for 35%

profile of v7, /device:TPU:224, one launch (start us, length us, event | category | flops | bytes accessed | tf_op | source)
XLA Modules:
  0.0 103.1 jit_solution(10857506504749239596)
XLA Ops:
  0.0 0.5 collective-permute-start.1
  0.5 0.1 collective-permute-start
  0.6 2.1 %slice.6 = f32[32,2,3072]{2,1,0:T(2,128)} slice(f32[32,2,6144]{2,1,0:T(2,128)} %param.6), slice={[0:32], [0:2], [0:3072]} | slice | bytes 1572864 | tf_op jit(solution)/shard_map/slice | solution.py:242
  2.7 4.7 %collective-permute-start.4 = (f32[1536,128]{1,0:T(8,128)}, f32[1536,128]{1,0:T(8,128)}, u32[]{:S(2)}, u32[]{:S(2)}) collective-permute-start(f32[1536,128]{1,0:T(8,128)} %bitcast.16), channel_id=1, source_target_pairs={{0,8},{8,16},{16,24},{24,32},{32,40},{40,48},{48,56},{56,64},{64,7... | collective-permute-start | bytes 2359304 | tf_op jit(solution)/shard_map/ppermute | solution.py:211
  7.4 0.0 collective-permute-start.5
  7.4 0.0 collective-permute-done.1
  7.4 0.0 collective-permute-done
  7.4 0.8 broadcast_in_dim.2
  8.2 5.3 %all-to-all-start = ((f32[8,3,2,2,768]{4,3,2,1,0:T(2,128)}), f32[8,3,2,2,768]{4,3,2,1,0:T(2,128)S(1)}, u32[]{:S(2)}, u32[]{:S(2)}) async-start(f32[8,3,2,2,768]{4,3,2,1,0:T(2,128)} %broadcast_in_dim.2), calls=%async_computation | async-start | bytes 589824 | tf_op jit(solution)/shard_map/all_to_all | solution.py:231
  13.6 0.0 copy-start.1
  13.6 0.6 subtract_convert_fusion.change
  14.2 0.7 compare_convert_fusion
  14.9 0.1 copy-done.1
  15.0 0.9 slice.7
  15.9 0.2 collective-permute-start.2
  16.1 1.5 %collective-permute-start.3 = (f32[1536,128]{1,0:T(8,128)}, f32[1536,128]{1,0:T(8,128)}, u32[]{:S(2)}, u32[]{:S(2)}) collective-permute-start(f32[1536,128]{1,0:T(8,128)} %bitcast.6), channel_id=1, source_target_pairs={{8,0},{16,8},{24,16},{32,24},{40,32},{48,40},{56,48},{64,56},{72,6... | collective-permute-start | bytes 2359304 | tf_op jit(solution)/shard_map/ppermute | solution.py:212
  17.6 8.6 %all-to-all-done.winds = f32[8,3,2,2,768]{4,3,2,1,0:T(2,128)S(1)} async-done(((f32[8,3,2,2,768]{4,3,2,1,0:T(2,128)}), f32[8,3,2,2,768]{4,3,2,1,0:T(2,128)S(1)}, u32[]{:S(2)}, u32[]{:S(2)}) %all-to-all-start) | async-done | bytes 294944 | tf_op jit(solution)/shard_map/all_to_all | solution.py:231
  26.3 0.0 collective-permute-done.4
  26.3 0.0 collective-permute-done.5
  26.3 4.1 %transport.3 = f32[8,32,768]{2,1,0:T(8,128)} custom-call(f32[8,3,2,2,768]{4,3,2,1,0:T(2,128)S(1)} %all-to-all-done.winds, f32[32,48,128]{2,1,0:T(8,128)} %bitcast.17.left, f32[32,48,128]{2,1,0:T(8,128)} %bitcast.19.own, f32[32,48,128]{2,1,0:T(8,128)} %bitcast.21.right), custom_call_target="tpu_custom_call" | custom-call | tf_op jit(solution)/shard_map/transport/pallas_call | solution.py:110
  30.4 5.1 %all-to-all-start.3 = ((f32[8,32,768]{2,1,0:T(8,128)}), f32[8,32,768]{2,1,0:T(8,128)}, u32[]{:S(2)}, u32[]{:S(2)}) async-start(f32[8,32,768]{2,1,0:T(8,128)} %transport.3), calls=%async_computation.3 | async-start | bytes 1572864 | tf_op jit(solution)/shard_map/all_to_all | solution.py:231
  35.5 4.1 %transport.2 = f32[8,32,768]{2,1,0:T(8,128)} custom-call(f32[8,3,2,2,768]{4,3,2,1,0:T(2,128)S(1)} %all-to-all-done.winds, f32[32,48,128]{2,1,0:T(8,128)} %bitcast.7.left, f32[32,48,128]{2,1,0:T(8,128)} %bitcast.9.own, f32[32,48,128]{2,1,0:T(8,128)} %bitcast.11.right), custom_call_target="tpu_custom_call" | custom-call | tf_op jit(solution)/shard_map/transport/pallas_call | solution.py:110
  39.6 9.2 %all-to-all-done.3 = f32[8,32,768]{2,1,0:T(8,128)} async-done(((f32[8,32,768]{2,1,0:T(8,128)}), f32[8,32,768]{2,1,0:T(8,128)}, u32[]{:S(2)}, u32[]{:S(2)}) %all-to-all-start.3) | async-done | bytes 786464 | tf_op jit(solution)/shard_map/all_to_all | solution.py:231
  48.8 4.4 %all-to-all-start.1 = ((f32[8,32,768]{2,1,0:T(8,128)}), f32[8,32,768]{2,1,0:T(8,128)}, u32[]{:S(2)}, u32[]{:S(2)}) async-start(f32[8,32,768]{2,1,0:T(8,128)} %transport.2), calls=%async_computation.1 | async-start | bytes 1572864 | tf_op jit(solution)/shard_map/all_to_all | solution.py:231
  53.2 12.6 %react.3 = f32[256,768]{1,0:T(8,128)} custom-call(f32[256,768]{1,0:T(8,128)} %bitcast.22.cells, bf16[1024,512]{1,0:T(8,128)(2,1)S(1)} %get-tuple-element.34.pick1, bf16[1024,512]{1,0:T(8,128)(2,1)S(1)} %get-tuple-element.35.pick2, bf16[256,2048]{1,0:T(8,128)(2,1)S(1)} %subtract_convert_fusion.change, f32[8,128]{1,0:T(8,128)S(1)} %bitcast.31), custom_call_target="tpu_custom_call" | custom-call | tf_op jit(solution)/shard_map/react/pallas_call | solution.py:198
  65.8 0.3 all-to-all-done.1
  66.1 5.2 %all-to-all-start.4 = ((f32[8,32,768]{2,1,0:T(8,128)}), f32[8,32,768]{2,1,0:T(8,128)}, u32[]{:S(2)}, u32[]{:S(2)}) async-start(f32[8,32,768]{2,1,0:T(8,128)} %bitcast.33), calls=%async_computation.4 | async-start | bytes 1572864 | tf_op jit(solution)/shard_map/all_to_all | solution.py:231
  71.3 12.6 %react.2 = f32[256,768]{1,0:T(8,128)} custom-call(f32[256,768]{1,0:T(8,128)} %bitcast.12.cells, bf16[1024,512]{1,0:T(8,128)(2,1)S(1)} %get-tuple-element.34.pick1, bf16[1024,512]{1,0:T(8,128)(2,1)S(1)} %get-tuple-element.35.pick2, bf16[256,2048]{1,0:T(8,128)(2,1)S(1)} %subtract_convert_fusion.change, f32[8,128]{1,0:T(8,128)S(1)} %bitcast.32), custom_call_target="tpu_custom_call" | custom-call | tf_op jit(solution)/shard_map/react/pallas_call | solution.py:198
  83.9 5.7 %all-to-all-start.2 = ((f32[8,32,768]{2,1,0:T(8,128)}), f32[8,32,768]{2,1,0:T(8,128)S(1)}, u32[]{:S(2)}, u32[]{:S(2)}) async-start(f32[8,32,768]{2,1,0:T(8,128)} %bitcast.34), calls=%async_computation.2 | async-start | bytes 1572864 | tf_op jit(solution)/shard_map/all_to_all | solution.py:231
  89.6 2.7 %join.2.refs_0_ = f32[32,96,128]{2,1,0:T(8,128)} custom-call(f32[8,32,768]{2,1,0:T(8,128)} %all-to-all-done.4.y_ref), custom_call_target="tpu_custom_call" | custom-call | tf_op jit(solution)/shard_map/join/pallas_call | solution.py:141
  92.3 9.2 %all-to-all-done.2.y_ref = f32[8,32,768]{2,1,0:T(8,128)S(1)} async-done(((f32[8,32,768]{2,1,0:T(8,128)}), f32[8,32,768]{2,1,0:T(8,128)S(1)}, u32[]{:S(2)}, u32[]{:S(2)}) %all-to-all-start.2) | async-done | bytes 786464 | tf_op jit(solution)/shard_map/all_to_all | solution.py:231
  101.6 1.5 %join.3 = f32[32,96,128]{2,1,0:T(8,128)} custom-call(f32[8,32,768]{2,1,0:T(8,128)S(1)} %all-to-all-done.2.y_ref, f32[32,96,128]{2,1,0:T(8,128)} %join.2.refs_0_), custom_call_target="tpu_custom_call", output_to_operand_aliasing={{}: (1, {})} | custom-call | tf_op jit(solution)/shard_map/join/pallas_call | solution.py:141
  (17 shorter events, 0.1 us)
Async XLA Ops:
  0.0 7.4 %copy-start.4 = (f32[2,2,768]{2,1,0:T(2,128)S(1)}, f32[2,2,768]{2,1,0:T(2,128)}, u32[]{:S(2)}) copy-start(f32[2,2,768]{2,1,0:T(2,128)} %param.7) | copy-start | bytes 36868
  0.0 13.5 %copy-start.3 = (s32[1024]{0:T(1024)S(1)}, s32[1024]{0:T(1024)}, u32[]{:S(2)}) copy-start(s32[1024]{0:T(1024)} %param.9) | copy-start | bytes 12292
  0.0 13.5 %copy-start.2 = (s32[1024]{0:T(1024)S(1)}, s32[1024]{0:T(1024)}, u32[]{:S(2)}) copy-start(s32[1024]{0:T(1024)} %param.10) | copy-start | bytes 12292
  0.0 13.5 %copy-start.5 = (s32[1024]{0:T(1024)S(1)}, s32[1024]{0:T(1024)}, u32[]{:S(2)}) copy-start(s32[1024]{0:T(1024)} %param.11) | copy-start | bytes 12292
  0.0 7.3 %collective-permute-start.1 = (f32[2,2,768]{2,1,0:T(2,128)}, f32[2,2,768]{2,1,0:T(2,128)S(1)}, u32[]{:S(2)}, u32[]{:S(2)}) collective-permute-start(f32[2,2,768]{2,1,0:T(2,128)} %param.7), channel_id=1, source_target_pairs={{8,0},{16,8},{24,16},{32,24},{40,32},{48,40},{56,48},{64,56},{72,6... | collective-permute-start | bytes 36872 | tf_op jit(solution)/shard_map/ppermute | solution.py:212
  0.5 6.8 %collective-permute-start = (f32[2,2,768]{2,1,0:T(2,128)}, f32[2,2,768]{2,1,0:T(2,128)S(1)}, u32[]{:S(2)}, u32[]{:S(2)}) collective-permute-start(f32[2,2,768]{2,1,0:T(2,128)} %param.7), channel_id=1, source_target_pairs={{0,8},{8,16},{16,24},{24,32},{32,40},{40,48},{48,56},{56,64},{64,7... | collective-permute-start | bytes 36872 | tf_op jit(solution)/shard_map/ppermute | solution.py:211
  2.7 23.6 %collective-permute-start.4 = (f32[1536,128]{1,0:T(8,128)}, f32[1536,128]{1,0:T(8,128)}, u32[]{:S(2)}, u32[]{:S(2)}) collective-permute-start(f32[1536,128]{1,0:T(8,128)} %bitcast.16), channel_id=1, source_target_pairs={{0,8},{8,16},{16,24},{24,32},{32,40},{40,48},{48,56},{56,64},{64,7... | collective-permute-start | bytes 2359304 | tf_op jit(solution)/shard_map/ppermute | solution.py:211
  7.4 18.9 %collective-permute-start.5 = (f32[1536,128]{1,0:T(8,128)}, f32[1536,128]{1,0:T(8,128)}, u32[]{:S(2)}, u32[]{:S(2)}) collective-permute-start(f32[1536,128]{1,0:T(8,128)} %bitcast.16), channel_id=1, source_target_pairs={{8,0},{16,8},{24,16},{32,24},{40,32},{48,40},{56,48},{64,56},{72,6... | collective-permute-start | bytes 2359304 | tf_op jit(solution)/shard_map/ppermute | solution.py:212
  8.2 18.1 %all-to-all-start = ((f32[8,3,2,2,768]{4,3,2,1,0:T(2,128)}), f32[8,3,2,2,768]{4,3,2,1,0:T(2,128)S(1)}, u32[]{:S(2)}, u32[]{:S(2)}) async-start(f32[8,3,2,2,768]{4,3,2,1,0:T(2,128)} %broadcast_in_dim.2), calls=%async_computation | async-start | bytes 589824 | tf_op jit(solution)/shard_map/all_to_all | solution.py:231
  13.6 1.4 %copy-start.1 = (f32[32,2,6144]{2,1,0:T(2,128)S(1)}, f32[32,2,6144]{2,1,0:T(2,128)}, u32[]{:S(2)}) copy-start(f32[32,2,6144]{2,1,0:T(2,128)} %param.6) | copy-start | bytes 4718596
  15.9 19.6 %collective-permute-start.2 = (f32[1536,128]{1,0:T(8,128)}, f32[1536,128]{1,0:T(8,128)}, u32[]{:S(2)}, u32[]{:S(2)}) collective-permute-start(f32[1536,128]{1,0:T(8,128)} %bitcast.6), channel_id=1, source_target_pairs={{0,8},{8,16},{16,24},{24,32},{32,40},{40,48},{48,56},{56,64},{64,7... | collective-permute-start | bytes 2359304 | tf_op jit(solution)/shard_map/ppermute | solution.py:211
  16.1 19.4 %collective-permute-start.3 = (f32[1536,128]{1,0:T(8,128)}, f32[1536,128]{1,0:T(8,128)}, u32[]{:S(2)}, u32[]{:S(2)}) collective-permute-start(f32[1536,128]{1,0:T(8,128)} %bitcast.6), channel_id=1, source_target_pairs={{8,0},{16,8},{24,16},{32,24},{40,32},{48,40},{56,48},{64,56},{72,6... | collective-permute-start | bytes 2359304 | tf_op jit(solution)/shard_map/ppermute | solution.py:212
  30.4 18.4 %all-to-all-start.3 = ((f32[8,32,768]{2,1,0:T(8,128)}), f32[8,32,768]{2,1,0:T(8,128)}, u32[]{:S(2)}, u32[]{:S(2)}) async-start(f32[8,32,768]{2,1,0:T(8,128)} %transport.3), calls=%async_computation.3 | async-start | bytes 1572864 | tf_op jit(solution)/shard_map/all_to_all | solution.py:231
  39.6 13.6 %copy-start = (f32[1024]{0:T(1024)S(1)}, f32[1024]{0:T(1024)}, u32[]{:S(2)}) copy-start(f32[1024]{0:T(1024)} %param.8) | copy-start | bytes 12292
  48.8 17.3 %all-to-all-start.1 = ((f32[8,32,768]{2,1,0:T(8,128)}), f32[8,32,768]{2,1,0:T(8,128)}, u32[]{:S(2)}, u32[]{:S(2)}) async-start(f32[8,32,768]{2,1,0:T(8,128)} %transport.2), calls=%async_computation.1 | async-start | bytes 1572864 | tf_op jit(solution)/shard_map/all_to_all | solution.py:231
  66.1 17.8 %all-to-all-start.4 = ((f32[8,32,768]{2,1,0:T(8,128)}), f32[8,32,768]{2,1,0:T(8,128)}, u32[]{:S(2)}, u32[]{:S(2)}) async-start(f32[8,32,768]{2,1,0:T(8,128)} %bitcast.33), calls=%async_computation.4 | async-start | bytes 1572864 | tf_op jit(solution)/shard_map/all_to_all | solution.py:231
  83.9 17.7 %all-to-all-start.2 = ((f32[8,32,768]{2,1,0:T(8,128)}), f32[8,32,768]{2,1,0:T(8,128)S(1)}, u32[]{:S(2)}, u32[]{:S(2)}) async-start(f32[8,32,768]{2,1,0:T(8,128)} %bitcast.34), calls=%async_computation.2 | async-start | bytes 1572864 | tf_op jit(solution)/shard_map/all_to_all | solution.py:231

commit v8 on v6

--- a/solution.py
+++ b/solution.py
@@ -30,16 +30,12 @@
 
 
 def transport_kernel(chunk, winds, left, own, right, out):
-    ahead, count, twice = out.shape
+    groups, rows, twice = out.shape
     width = twice // 2
     pieces = width // LANES
-    stride = own.shape[1]
+    stride = own.shape[0] // rows
     pairs = winds.shape[4] // width
-    rows = 16
     y = lax.rem(lax.broadcasted_iota(jnp.int32, (4, width), 1), NY)
-    steps = pl.num_programs(0)
-    sources = ahead // pairs
-    left, own, right = (ref.reshape(count * stride, LANES) for ref in (left, own, right))
 
     def south(array):
         return pltpu.roll(array, 1, 1)
@@ -47,8 +43,8 @@
     def north(array):
         return pltpu.roll(array, width - 1, 1)
 
-    for t in range(ahead):
-        source = (chunk * steps + pl.program_id(0)) * sources + t // pairs
+    for t in range(groups):
+        source = chunk * (groups // pairs) + t // pairs
         lanes = slice(t % pairs * width, (t % pairs + 1) * width)
 
         def around(kind, first):
@@ -86,36 +82,31 @@
                 + north_of[row] * north(q)
             )
 
-        for first in range(0, count, rows):
-
-            def column(ref, c):
-                start = first * stride + 2 * pieces * t + c
-                return jnp.concatenate(
-                    [ref[pl.ds(start + 2 * m, rows, stride=stride), :] for m in range(pieces)], axis=1
-                )
-
-            q = [column(ref, c) for ref in (left, own, right) for c in range(2)]
-            q = [step(q[i + 1], i, q[i], q[i + 2]) for i in range(4)]
-            for c in range(2):
-                out[t, first : first + rows, c * width : (c + 1) * width] = step(
-                    q[c + 1], c + 1, q[c], q[c + 2]
-                )
+        def column(ref, c):
+            start = 2 * pieces * t + c
+            return jnp.concatenate(
+                [ref[pl.ds(start + 2 * m, rows, stride=stride), :] for m in range(pieces)], axis=1
+            )
+
+        q = [column(ref, c) for ref in (left, own, right) for c in range(2)]
+        q = [step(q[i + 1], i, q[i], q[i + 2]) for i in range(4)]
+        for c in range(2):
+            out[t, :, c * width : (c + 1) * width] = step(q[c + 1], c + 1, q[c], q[c + 2])
 
 
 def transport(chunk, winds, left, own, right, shape):
     groups, count, twice = shape
-    steps = 2
-    sides = [array.reshape(count, -1, LANES) for array in (left, own, right)]
-    part = sides[0].shape[1] // steps
+    steps = count // 8
+    part = own.shape[0] // steps
     return pl.pallas_call(
         functools.partial(transport_kernel, chunk),
         grid=(steps,),
-        in_specs=[VMEM] + [pl.BlockSpec((count, part, LANES), lambda s: (0, s, 0))] * 3,
-        out_specs=pl.BlockSpec((groups // steps, count, twice), lambda s: (s, 0, 0)),
+        in_specs=[VMEM] + [pl.BlockSpec((part, LANES), lambda i: (i, 0))] * 3,
+        out_specs=pl.BlockSpec((groups, 8, twice), lambda i: (0, i, 0)),
         out_shape=pltpu.HBM(shape, F32),
         compiler_params=pltpu.CompilerParams(vmem_limit_bytes=16 << 20),
         name="transport",
-    )(winds, *sides)
+    )(winds, left, own, right)
 
 
 def join_kernel(y_ref, *refs):
@@ -156,28 +147,37 @@
     return jnp.concatenate([high, low], axis=0)
 
 
-def react_kernel(cells, pick1, pick2, change, rates, out, done, sems):
-    amounts = cells[...]
+def react_kernel(cells, pick1, pick2, change, rates, out, held, done, sems):
+    tile = 256
+    lanes = [slice(n * tile, (n + 1) * tile) for n in range(cells.shape[1] // tile)]
+    loads = [pltpu.make_async_copy(cells.at[:, at], held.at[:, at], sems.at[0, n]) for n, at in enumerate(lanes)]
+    for load in loads:
+        load.start()
     rate = jnp.concatenate(
         [jnp.broadcast_to(rates[i : i + 1, :], (LANES, LANES)).T for i in range(rates.shape[0])], axis=0
     )
-    rate = jnp.concatenate([rate] * (amounts.shape[1] // LANES), axis=1)
-    tile = 256
-    copies = []
-    for step in range(SUBSTEPS):
+
+    def velocity_of(amounts):
         parts = split(amounts)
         first = jnp.dot(pick1[...], parts, preferred_element_type=F32)
         second = jnp.dot(pick2[...], parts, preferred_element_type=F32)
-        velocity = split(rate * first * second)
-        if step < SUBSTEPS - 1:
-            amounts = amounts + jnp.dot(change[...], velocity, preferred_element_type=F32)
-            continue
-        for n in range(amounts.shape[1] // tile):
-            lanes = slice(n * tile, (n + 1) * tile)
-            moved = jnp.dot(change[...], velocity[:, lanes], preferred_element_type=F32)
-            done[:, lanes] = amounts[:, lanes] + moved
-            copies.append(pltpu.make_async_copy(done.at[:, lanes], out.at[:, lanes], sems.at[n]))
-            copies[-1].start()
+        return split(jnp.concatenate([rate] * (amounts.shape[1] // LANES), axis=1) * first * second)
+
+    pieces = []
+    for load, at in zip(loads, lanes):
+        load.wait()
+        pieces.append(velocity_of(held[:, at]))
+    velocity = jnp.concatenate(pieces, axis=1)
+    amounts = held[...]
+    for step in range(SUBSTEPS - 1):
+        amounts = amounts + jnp.dot(change[...], velocity, preferred_element_type=F32)
+        velocity = velocity_of(amounts)
+    copies = []
+    for n, at in enumerate(lanes):
+        moved = jnp.dot(change[...], velocity[:, at], preferred_element_type=F32)
+        done[:, at] = amounts[:, at] + moved
+        copies.append(pltpu.make_async_copy(done.at[:, at], out.at[:, at], sems.at[1, n]))
+        copies[-1].start()
     for copy in copies:
         copy.wait()
 
@@ -185,13 +185,13 @@
 def react(cells, pick1, pick2, change, rates):
     return pl.pallas_call(
         react_kernel,
-        in_specs=[VMEM] * 5,
+        in_specs=[pl.BlockSpec(memory_space=pl.ANY)] + [VMEM] * 4,
         out_specs=pl.BlockSpec(memory_space=pltpu.HBM),
         out_shape=pltpu.HBM(cells.shape, F32),
-        scratch_shapes=[pltpu.VMEM(cells.shape, F32), pltpu.SemaphoreType.DMA((cells.shape[1] // 256,))],
+        scratch_shapes=[pltpu.VMEM(cells.shape, F32)] * 2 + [pltpu.SemaphoreType.DMA((2, cells.shape[1] // 256))],
         compiler_params=pltpu.CompilerParams(vmem_limit_bytes=24 << 20),
         name="react",
-    )(pltpu.with_memory_space_constraint(cells, pltpu.VMEM), pick1, pick2, change, rates)
+    )(cells, pick1, pick2, change, rates)
 
 
 def neighbours(array):

time: 103 us -> 104 us (level)
  Pallas kernels: 36.9 us -> 39.2 us
  waiting for transfers between devices: 28.1 us -> 26.8 us
    pallas_call x2, Pallas kernels: 8.22 us -> 10.4 us  [transport(): pl.pallas_call(functools.partial(transport_kernel, chunk), grid=(steps,),...]
    all_to_all x5, waiting for transfers between devices: 28 us -> 26.8 us  [exchange(): lax.all_to_all(blocks, 'tracer', split_axis=0, concat_axis=0, tiled=True)]
  transfers between devices with their start and end apart: 11 -> 11, of which waited for: 5 -> 5; matrix products, arithmetic and copies ran while one was open for 5% -> 5% of each run, Pallas kernels for 35% -> 36%
where the time goes in v8:
time: 104 us
  Pallas kernels  39.2 us (38%)
  starting transfers between devices  32.2 us (31%)
  waiting for transfers between devices  26.8 us (26%)
  local copies, waits for them, and re-layouts  3.87 us (4%)
  other arithmetic  1.35 us (1%)
    all_to_all x5, waiting for transfers between devices, exchange(): lax.all_to_all(blocks, 'tracer', split_axis=0, concat_axis=0, tiled=True)  26.8 us
    all_to_all x5, starting transfers between devices, exchange(): lax.all_to_all(blocks, 'tracer', split_axis=0, concat_axis=0, tiled=True)  25.1 us
    pallas_call x2, Pallas kernels, react(): pl.pallas_call(react_kernel, in_specs=[pl.BlockSpec(memory_space=pl.ANY)]...  24.6 us
    pallas_call x2, Pallas kernels, transport(): pl.pallas_call(functools.partial(transport_kernel, chunk), grid=(steps,),...  10.4 us
    ppermute x3, starting transfers between devices, neighbours(): lax.ppermute(array, 'region', [(i, (i + 1) % count) for i in range(count)])  4.97 us
    pallas_call x2, Pallas kernels, join(): pl.pallas_call(join_kernel, grid=(own // 8,), in_specs=[VMEM] + [pl.Block...  4.23 us
  transfers between devices with their start and end apart: 11, of which 5 were waited for; matrix products, arithmetic and copies ran while one was open for 5% of the time, Pallas kernels for 36%

profile of v8, /device:TPU:224, one launch (start us, length us, event | category | flops | bytes accessed | tf_op | source)
XLA Modules:
  0.0 103.6 jit_solution(335303279377908063)
XLA Ops:
  0.0 0.5 collective-permute-start.1
  0.5 0.1 collective-permute-start
  0.6 2.1 %slice.6 = f32[32,2,3072]{2,1,0:T(2,128)} slice(f32[32,2,6144]{2,1,0:T(2,128)} %param.6), slice={[0:32], [0:2], [0:3072]} | slice | bytes 1572864 | tf_op jit(solution)/shard_map/slice | solution.py:230
  2.7 4.7 %collective-permute-start.4 = (f32[1536,128]{1,0:T(8,128)}, f32[1536,128]{1,0:T(8,128)}, u32[]{:S(2)}, u32[]{:S(2)}) collective-permute-start(f32[1536,128]{1,0:T(8,128)} %bitcast.13.own), channel_id=1, source_target_pairs={{0,8},{8,16},{16,24},{24,32},{32,40},{40,48},{48,56},{56,64},{64,7... | collective-permute-start | bytes 2359304 | tf_op jit(solution)/shard_map/ppermute | solution.py:199
  7.4 0.0 collective-permute-start.5
  7.4 0.0 collective-permute-done.1
  7.4 0.0 collective-permute-done
  7.4 0.8 broadcast_in_dim.2
  8.2 5.3 %all-to-all-start = ((f32[8,3,2,2,768]{4,3,2,1,0:T(2,128)}), f32[8,3,2,2,768]{4,3,2,1,0:T(2,128)S(1)}, u32[]{:S(2)}, u32[]{:S(2)}) async-start(f32[8,3,2,2,768]{4,3,2,1,0:T(2,128)} %broadcast_in_dim.2), calls=%async_computation | async-start | bytes 589824 | tf_op jit(solution)/shard_map/all_to_all | solution.py:219
  13.6 0.0 copy-start.1
  13.6 0.6 subtract_convert_fusion.change
  14.2 0.7 compare_convert_fusion
  14.9 0.1 copy-done.1
  15.0 0.9 slice.7
  15.9 0.2 collective-permute-start.2
  16.1 1.5 %collective-permute-start.3 = (f32[1536,128]{1,0:T(8,128)}, f32[1536,128]{1,0:T(8,128)}, u32[]{:S(2)}, u32[]{:S(2)}) collective-permute-start(f32[1536,128]{1,0:T(8,128)} %bitcast.6.own), channel_id=1, source_target_pairs={{8,0},{16,8},{24,16},{32,24},{40,32},{48,40},{56,48},{64,56},{72,6... | collective-permute-start | bytes 2359304 | tf_op jit(solution)/shard_map/ppermute | solution.py:200
  17.6 8.6 %all-to-all-done.winds = f32[8,3,2,2,768]{4,3,2,1,0:T(2,128)S(1)} async-done(((f32[8,3,2,2,768]{4,3,2,1,0:T(2,128)}), f32[8,3,2,2,768]{4,3,2,1,0:T(2,128)S(1)}, u32[]{:S(2)}, u32[]{:S(2)}) %all-to-all-start) | async-done | bytes 294944 | tf_op jit(solution)/shard_map/all_to_all | solution.py:219
  26.3 0.0 collective-permute-done.4.left
  26.3 5.2 %transport.3 = f32[8,32,768]{2,1,0:T(8,128)} custom-call(f32[8,3,2,2,768]{4,3,2,1,0:T(2,128)S(1)} %all-to-all-done.winds, f32[1536,128]{1,0:T(8,128)} %collective-permute-done.4.left, f32[1536,128]{1,0:T(8,128)} %bitcast.13.own, f32[1536,128]{1,0:T(8,128)} %collective-permute-done.5.right), custom_call_target="tpu_custom_call" | custom-call | tf_op jit(solution)/shard_map/transport/pallas_call | solution.py:101
  31.5 5.1 %all-to-all-start.3 = ((f32[8,32,768]{2,1,0:T(8,128)}), f32[8,32,768]{2,1,0:T(8,128)}, u32[]{:S(2)}, u32[]{:S(2)}) async-start(f32[8,32,768]{2,1,0:T(8,128)} %transport.3), calls=%async_computation.3 | async-start | bytes 1572864 | tf_op jit(solution)/shard_map/all_to_all | solution.py:219
  36.6 5.2 %transport.2 = f32[8,32,768]{2,1,0:T(8,128)} custom-call(f32[8,3,2,2,768]{4,3,2,1,0:T(2,128)S(1)} %all-to-all-done.winds, f32[1536,128]{1,0:T(8,128)} %collective-permute-done.2.left, f32[1536,128]{1,0:T(8,128)} %bitcast.6.own, f32[1536,128]{1,0:T(8,128)} %collective-permute-done.3.right), custom_call_target="tpu_custom_call" | custom-call | tf_op jit(solution)/shard_map/transport/pallas_call | solution.py:101
  41.8 8.1 %all-to-all-done.3 = f32[8,32,768]{2,1,0:T(8,128)} async-done(((f32[8,32,768]{2,1,0:T(8,128)}), f32[8,32,768]{2,1,0:T(8,128)}, u32[]{:S(2)}, u32[]{:S(2)}) %all-to-all-start.3) | async-done | bytes 786464 | tf_op jit(solution)/shard_map/all_to_all | solution.py:219
  49.9 4.4 %all-to-all-start.1 = ((f32[8,32,768]{2,1,0:T(8,128)}), f32[8,32,768]{2,1,0:T(8,128)}, u32[]{:S(2)}, u32[]{:S(2)}) async-start(f32[8,32,768]{2,1,0:T(8,128)} %transport.2), calls=%async_computation.1 | async-start | bytes 1572864 | tf_op jit(solution)/shard_map/all_to_all | solution.py:219
  54.3 12.3 %react.3 = f32[256,768]{1,0:T(8,128)} custom-call(f32[256,768]{1,0:T(8,128)} %bitcast.16.cells, bf16[1024,512]{1,0:T(8,128)(2,1)S(1)} %get-tuple-element.34.pick1, bf16[1024,512]{1,0:T(8,128)(2,1)S(1)} %get-tuple-element.35.pick2, bf16[256,2048]{1,0:T(8,128)(2,1)S(1)} %subtract_convert_fusion.change, f32[8,128]{1,0:T(8,128)S(1)} %bitcast.23), custom_call_target="tpu_custom_call" | custom-call | tf_op jit(solution)/shard_map/react/pallas_call | solution.py:186
  66.6 0.6 all-to-all-done.1
  67.2 4.9 %all-to-all-start.4 = ((f32[8,32,768]{2,1,0:T(8,128)}), f32[8,32,768]{2,1,0:T(8,128)}, u32[]{:S(2)}, u32[]{:S(2)}) async-start(f32[8,32,768]{2,1,0:T(8,128)} %bitcast.25), calls=%async_computation.4 | async-start | bytes 1572864 | tf_op jit(solution)/shard_map/all_to_all | solution.py:219
  72.0 12.3 %react.2 = f32[256,768]{1,0:T(8,128)} custom-call(f32[256,768]{1,0:T(8,128)} %bitcast.9.cells, bf16[1024,512]{1,0:T(8,128)(2,1)S(1)} %get-tuple-element.34.pick1, bf16[1024,512]{1,0:T(8,128)(2,1)S(1)} %get-tuple-element.35.pick2, bf16[256,2048]{1,0:T(8,128)(2,1)S(1)} %subtract_convert_fusion.change, f32[8,128]{1,0:T(8,128)S(1)} %bitcast.24), custom_call_target="tpu_custom_call" | custom-call | tf_op jit(solution)/shard_map/react/pallas_call | solution.py:186
  84.4 0.3 all-to-all-done.4.y_ref
  84.6 5.5 %all-to-all-start.2 = ((f32[8,32,768]{2,1,0:T(8,128)}), f32[8,32,768]{2,1,0:T(8,128)S(1)}, u32[]{:S(2)}, u32[]{:S(2)}) async-start(f32[8,32,768]{2,1,0:T(8,128)} %bitcast.26), calls=%async_computation.2 | async-start | bytes 1572864 | tf_op jit(solution)/shard_map/all_to_all | solution.py:219
  90.1 2.7 %join.2.refs_0_ = f32[32,96,128]{2,1,0:T(8,128)} custom-call(f32[8,32,768]{2,1,0:T(8,128)} %all-to-all-done.4.y_ref), custom_call_target="tpu_custom_call" | custom-call | tf_op jit(solution)/shard_map/join/pallas_call | solution.py:132
  92.8 9.2 %all-to-all-done.2.y_ref = f32[8,32,768]{2,1,0:T(8,128)S(1)} async-done(((f32[8,32,768]{2,1,0:T(8,128)}), f32[8,32,768]{2,1,0:T(8,128)S(1)}, u32[]{:S(2)}, u32[]{:S(2)}) %all-to-all-start.2) | async-done | bytes 786464 | tf_op jit(solution)/shard_map/all_to_all | solution.py:219
  102.0 1.5 %join.3 = f32[32,96,128]{2,1,0:T(8,128)} custom-call(f32[8,32,768]{2,1,0:T(8,128)S(1)} %all-to-all-done.2.y_ref, f32[32,96,128]{2,1,0:T(8,128)} %join.2.refs_0_), custom_call_target="tpu_custom_call", output_to_operand_aliasing={{}: (1, {})} | custom-call | tf_op jit(solution)/shard_map/join/pallas_call | solution.py:132
  (17 shorter events, 0.1 us)
Async XLA Ops:
  0.0 7.4 %copy-start.4 = (f32[2,2,768]{2,1,0:T(2,128)S(1)}, f32[2,2,768]{2,1,0:T(2,128)}, u32[]{:S(2)}) copy-start(f32[2,2,768]{2,1,0:T(2,128)} %param.7) | copy-start | bytes 36868
  0.0 13.5 %copy-start.3 = (s32[1024]{0:T(1024)S(1)}, s32[1024]{0:T(1024)}, u32[]{:S(2)}) copy-start(s32[1024]{0:T(1024)} %param.9) | copy-start | bytes 12292
  0.0 13.5 %copy-start.2 = (s32[1024]{0:T(1024)S(1)}, s32[1024]{0:T(1024)}, u32[]{:S(2)}) copy-start(s32[1024]{0:T(1024)} %param.10) | copy-start | bytes 12292
  0.0 13.5 %copy-start.5 = (s32[1024]{0:T(1024)S(1)}, s32[1024]{0:T(1024)}, u32[]{:S(2)}) copy-start(s32[1024]{0:T(1024)} %param.11) | copy-start | bytes 12292
  0.0 7.3 %collective-permute-start.1 = (f32[2,2,768]{2,1,0:T(2,128)}, f32[2,2,768]{2,1,0:T(2,128)S(1)}, u32[]{:S(2)}, u32[]{:S(2)}) collective-permute-start(f32[2,2,768]{2,1,0:T(2,128)} %param.7), channel_id=1, source_target_pairs={{8,0},{16,8},{24,16},{32,24},{40,32},{48,40},{56,48},{64,56},{72,6... | collective-permute-start | bytes 36872 | tf_op jit(solution)/shard_map/ppermute | solution.py:200
  0.5 6.8 %collective-permute-start = (f32[2,2,768]{2,1,0:T(2,128)}, f32[2,2,768]{2,1,0:T(2,128)S(1)}, u32[]{:S(2)}, u32[]{:S(2)}) collective-permute-start(f32[2,2,768]{2,1,0:T(2,128)} %param.7), channel_id=1, source_target_pairs={{0,8},{8,16},{16,24},{24,32},{32,40},{40,48},{48,56},{56,64},{64,7... | collective-permute-start | bytes 36872 | tf_op jit(solution)/shard_map/ppermute | solution.py:199
  2.7 23.6 %collective-permute-start.4 = (f32[1536,128]{1,0:T(8,128)}, f32[1536,128]{1,0:T(8,128)}, u32[]{:S(2)}, u32[]{:S(2)}) collective-permute-start(f32[1536,128]{1,0:T(8,128)} %bitcast.13.own), channel_id=1, source_target_pairs={{0,8},{8,16},{16,24},{24,32},{32,40},{40,48},{48,56},{56,64},{64,7... | collective-permute-start | bytes 2359304 | tf_op jit(solution)/shard_map/ppermute | solution.py:199
  7.4 18.9 %collective-permute-start.5 = (f32[1536,128]{1,0:T(8,128)}, f32[1536,128]{1,0:T(8,128)}, u32[]{:S(2)}, u32[]{:S(2)}) collective-permute-start(f32[1536,128]{1,0:T(8,128)} %bitcast.13.own), channel_id=1, source_target_pairs={{8,0},{16,8},{24,16},{32,24},{40,32},{48,40},{56,48},{64,56},{72,6... | collective-permute-start | bytes 2359304 | tf_op jit(solution)/shard_map/ppermute | solution.py:200
  8.2 18.1 %all-to-all-start = ((f32[8,3,2,2,768]{4,3,2,1,0:T(2,128)}), f32[8,3,2,2,768]{4,3,2,1,0:T(2,128)S(1)}, u32[]{:S(2)}, u32[]{:S(2)}) async-start(f32[8,3,2,2,768]{4,3,2,1,0:T(2,128)} %broadcast_in_dim.2), calls=%async_computation | async-start | bytes 589824 | tf_op jit(solution)/shard_map/all_to_all | solution.py:219
  13.6 1.4 %copy-start.1 = (f32[32,2,6144]{2,1,0:T(2,128)S(1)}, f32[32,2,6144]{2,1,0:T(2,128)}, u32[]{:S(2)}) copy-start(f32[32,2,6144]{2,1,0:T(2,128)} %param.6) | copy-start | bytes 4718596
  15.9 20.7 %collective-permute-start.2 = (f32[1536,128]{1,0:T(8,128)}, f32[1536,128]{1,0:T(8,128)}, u32[]{:S(2)}, u32[]{:S(2)}) collective-permute-start(f32[1536,128]{1,0:T(8,128)} %bitcast.6.own), channel_id=1, source_target_pairs={{0,8},{8,16},{16,24},{24,32},{32,40},{40,48},{48,56},{56,64},{64,7... | collective-permute-start | bytes 2359304 | tf_op jit(solution)/shard_map/ppermute | solution.py:199
  16.1 20.4 %collective-permute-start.3 = (f32[1536,128]{1,0:T(8,128)}, f32[1536,128]{1,0:T(8,128)}, u32[]{:S(2)}, u32[]{:S(2)}) collective-permute-start(f32[1536,128]{1,0:T(8,128)} %bitcast.6.own), channel_id=1, source_target_pairs={{8,0},{16,8},{24,16},{32,24},{40,32},{48,40},{56,48},{64,56},{72,6... | collective-permute-start | bytes 2359304 | tf_op jit(solution)/shard_map/ppermute | solution.py:200
  31.5 18.4 %all-to-all-start.3 = ((f32[8,32,768]{2,1,0:T(8,128)}), f32[8,32,768]{2,1,0:T(8,128)}, u32[]{:S(2)}, u32[]{:S(2)}) async-start(f32[8,32,768]{2,1,0:T(8,128)} %transport.3), calls=%async_computation.3 | async-start | bytes 1572864 | tf_op jit(solution)/shard_map/all_to_all | solution.py:219
  41.8 12.5 %copy-start = (f32[1024]{0:T(1024)S(1)}, f32[1024]{0:T(1024)}, u32[]{:S(2)}) copy-start(f32[1024]{0:T(1024)} %param.8) | copy-start | bytes 12292
  49.9 17.3 %all-to-all-start.1 = ((f32[8,32,768]{2,1,0:T(8,128)}), f32[8,32,768]{2,1,0:T(8,128)}, u32[]{:S(2)}, u32[]{:S(2)}) async-start(f32[8,32,768]{2,1,0:T(8,128)} %transport.2), calls=%async_computation.1 | async-start | bytes 1572864 | tf_op jit(solution)/shard_map/all_to_all | solution.py:219
  67.2 17.5 %all-to-all-start.4 = ((f32[8,32,768]{2,1,0:T(8,128)}), f32[8,32,768]{2,1,0:T(8,128)}, u32[]{:S(2)}, u32[]{:S(2)}) async-start(f32[8,32,768]{2,1,0:T(8,128)} %bitcast.25), calls=%async_computation.4 | async-start | bytes 1572864 | tf_op jit(solution)/shard_map/all_to_all | solution.py:219
  84.6 17.4 %all-to-all-start.2 = ((f32[8,32,768]{2,1,0:T(8,128)}), f32[8,32,768]{2,1,0:T(8,128)S(1)}, u32[]{:S(2)}, u32[]{:S(2)}) async-start(f32[8,32,768]{2,1,0:T(8,128)} %bitcast.26), calls=%async_computation.2 | async-start | bytes 1572864 | tf_op jit(solution)/shard_map/all_to_all | solution.py:219

commit v9 on v6

--- a/solution.py
+++ b/solution.py
@@ -30,12 +30,14 @@
 
 
 def transport_kernel(chunk, winds, left, own, right, out):
+    if chunk % 2 == 1:
+        left, right = right, left
     ahead, count, twice = out.shape
     width = twice // 2
     pieces = width // LANES
     stride = own.shape[1]
     pairs = winds.shape[4] // width
-    rows = 16
+    rows = 32
     y = lax.rem(lax.broadcasted_iota(jnp.int32, (4, width), 1), NY)
     steps = pl.num_programs(0)
     sources = ahead // pairs
@@ -105,7 +107,7 @@
 def transport(chunk, winds, left, own, right, shape):
     groups, count, twice = shape
     steps = 2
-    sides = [array.reshape(count, -1, LANES) for array in (left, own, right)]
+    sides = [array.reshape(count, -1, LANES) for array in ((right, own, left) if chunk % 2 == 1 else (left, own, right))]
     part = sides[0].shape[1] // steps
     return pl.pallas_call(
         functools.partial(transport_kernel, chunk),

time: 103 us -> 111 us (1.078)
  waiting for transfers between devices: 28.1 us -> 37.9 us
  starting transfers between devices: 32 us -> 30.8 us
    all_to_all x5, waiting for transfers between devices: 28 us -> 37.9 us  [exchange(): lax.all_to_all(blocks, 'tracer', split_axis=0, concat_axis=0, tiled=True)]
    ppermute x3, starting transfers between devices: 2.05 us -> 0.53 us  [neighbours(): lax.ppermute(array, 'region', [((i + 1) % count, i) for i in range(count)])]
  transfers between devices with their start and end apart: 11 -> 11, of which waited for: 5 -> 5; matrix products, arithmetic and copies ran while one was open for 5% -> 5% of each run, Pallas kernels for 35% -> 31%
where the time goes in v9:
time: 111 us; the launch traced here: 110 us
  waiting for transfers between devices  37.9 us (34%)
  Pallas kernels  36.1 us (33%)
  starting transfers between devices  30.8 us (28%)
  local copies, waits for them, and re-layouts  3.87 us (3%)
  other arithmetic  1.35 us (1%)
    all_to_all x5, waiting for transfers between devices, exchange(): lax.all_to_all(blocks, 'tracer', split_axis=0, concat_axis=0, tiled=True)  37.9 us
    all_to_all x5, starting transfers between devices, exchange(): lax.all_to_all(blocks, 'tracer', split_axis=0, concat_axis=0, tiled=True)  25 us
    pallas_call x2, Pallas kernels, react(): pl.pallas_call(react_kernel, in_specs=[VMEM] * 5, out_specs=pl.BlockSpec(...  24.5 us
    pallas_call x2, Pallas kernels, transport(): pl.pallas_call(functools.partial(transport_kernel, chunk), grid=(steps,),...  7.46 us
    ppermute x3, starting transfers between devices, neighbours(): lax.ppermute(array, 'region', [(i, (i + 1) % count) for i in range(count)])  5.25 us
    pallas_call x2, Pallas kernels, join(): pl.pallas_call(join_kernel, grid=(own // 8,), in_specs=[VMEM] + [pl.Block...  4.23 us
  transfers between devices with their start and end apart: 11, of which 5 were waited for; matrix products, arithmetic and copies ran while one was open for 5% of the time, Pallas kernels for 31%

profile of v9, /device:TPU:224, one launch (start us, length us, event | category | flops | bytes accessed | tf_op | source)
XLA Modules:
  0.0 110.2 jit_solution(13053686596711785189)
XLA Ops:
  0.0 0.5 collective-permute-start.1
  0.5 0.1 collective-permute-start
  0.6 2.1 %slice.6 = f32[32,2,3072]{2,1,0:T(2,128)} slice(f32[32,2,6144]{2,1,0:T(2,128)} %param.6), slice={[0:32], [0:2], [0:3072]} | slice | bytes 1572864 | tf_op jit(solution)/shard_map/slice | solution.py:232
  2.7 4.7 %collective-permute-start.4 = (f32[1536,128]{1,0:T(8,128)}, f32[1536,128]{1,0:T(8,128)}, u32[]{:S(2)}, u32[]{:S(2)}) collective-permute-start(f32[1536,128]{1,0:T(8,128)} %bitcast.16), channel_id=1, source_target_pairs={{0,8},{8,16},{16,24},{24,32},{32,40},{40,48},{48,56},{56,64},{64,7... | collective-permute-start | bytes 2359304 | tf_op jit(solution)/shard_map/ppermute | solution.py:201
  7.4 0.0 collective-permute-start.5
  7.4 0.0 collective-permute-done.1
  7.4 0.0 collective-permute-done
  7.4 0.8 broadcast_in_dim.2
  8.2 5.3 %all-to-all-start = ((f32[8,3,2,2,768]{4,3,2,1,0:T(2,128)}), f32[8,3,2,2,768]{4,3,2,1,0:T(2,128)S(1)}, u32[]{:S(2)}, u32[]{:S(2)}) async-start(f32[8,3,2,2,768]{4,3,2,1,0:T(2,128)} %broadcast_in_dim.2), calls=%async_computation | async-start | bytes 589824 | tf_op jit(solution)/shard_map/all_to_all | solution.py:221
  13.6 0.0 copy-start.1
  13.6 0.6 subtract_convert_fusion.change
  14.2 0.7 compare_convert_fusion
  14.9 0.1 copy-done.1
  15.0 0.9 slice.7
  15.9 0.5 collective-permute-start.3
  16.4 18.3 %all-to-all-done.winds = f32[8,3,2,2,768]{4,3,2,1,0:T(2,128)S(1)} async-done(((f32[8,3,2,2,768]{4,3,2,1,0:T(2,128)}), f32[8,3,2,2,768]{4,3,2,1,0:T(2,128)S(1)}, u32[]{:S(2)}, u32[]{:S(2)}) %all-to-all-start) | async-done | bytes 294944 | tf_op jit(solution)/shard_map/all_to_all | solution.py:221
  34.7 0.0 collective-permute-done.4
  34.7 0.0 collective-permute-done.5
  34.7 3.7 %transport.3 = f32[8,32,768]{2,1,0:T(8,128)} custom-call(f32[8,3,2,2,768]{4,3,2,1,0:T(2,128)S(1)} %all-to-all-done.winds, f32[32,48,128]{2,1,0:T(8,128)} %bitcast.17.left, f32[32,48,128]{2,1,0:T(8,128)} %bitcast.19.own, f32[32,48,128]{2,1,0:T(8,128)} %bitcast.21.right), custom_call_target="tpu_custom_call" | custom-call | tf_op jit(solution)/shard_map/transport/pallas_call | solution.py:112
  38.4 5.1 %all-to-all-start.3 = ((f32[8,32,768]{2,1,0:T(8,128)}), f32[8,32,768]{2,1,0:T(8,128)}, u32[]{:S(2)}, u32[]{:S(2)}) async-start(f32[8,32,768]{2,1,0:T(8,128)} %transport.3), calls=%async_computation.3 | async-start | bytes 1572864 | tf_op jit(solution)/shard_map/all_to_all | solution.py:221
  43.6 3.7 %transport.2 = f32[8,32,768]{2,1,0:T(8,128)} custom-call(f32[8,3,2,2,768]{4,3,2,1,0:T(2,128)S(1)} %all-to-all-done.winds, f32[32,48,128]{2,1,0:T(8,128)} %bitcast.7.left, f32[32,48,128]{2,1,0:T(8,128)} %bitcast.9.own, f32[32,48,128]{2,1,0:T(8,128)} %bitcast.11.right), custom_call_target="tpu_custom_call" | custom-call | tf_op jit(solution)/shard_map/transport/pallas_call | solution.py:112
  47.3 9.5 %all-to-all-done.3 = f32[8,32,768]{2,1,0:T(8,128)} async-done(((f32[8,32,768]{2,1,0:T(8,128)}), f32[8,32,768]{2,1,0:T(8,128)}, u32[]{:S(2)}, u32[]{:S(2)}) %all-to-all-start.3) | async-done | bytes 786464 | tf_op jit(solution)/shard_map/all_to_all | solution.py:221
  56.7 4.4 %all-to-all-start.1 = ((f32[8,32,768]{2,1,0:T(8,128)}), f32[8,32,768]{2,1,0:T(8,128)}, u32[]{:S(2)}, u32[]{:S(2)}) async-start(f32[8,32,768]{2,1,0:T(8,128)} %transport.2), calls=%async_computation.1 | async-start | bytes 1572864 | tf_op jit(solution)/shard_map/all_to_all | solution.py:221
  61.1 12.2 %react.3 = f32[256,768]{1,0:T(8,128)} custom-call(f32[256,768]{1,0:T(8,128)} %bitcast.22.cells, bf16[1024,512]{1,0:T(8,128)(2,1)S(1)} %get-tuple-element.34.pick1, bf16[1024,512]{1,0:T(8,128)(2,1)S(1)} %get-tuple-element.35.pick2, bf16[256,2048]{1,0:T(8,128)(2,1)S(1)} %subtract_convert_fusion.change, f32[8,128]{1,0:T(8,128)S(1)} %bitcast.31), custom_call_target="tpu_custom_call" | custom-call | tf_op jit(solution)/shard_map/react/pallas_call | solution.py:188
  73.4 0.6 all-to-all-done.1
  74.0 4.8 %all-to-all-start.4 = ((f32[8,32,768]{2,1,0:T(8,128)}), f32[8,32,768]{2,1,0:T(8,128)}, u32[]{:S(2)}, u32[]{:S(2)}) async-start(f32[8,32,768]{2,1,0:T(8,128)} %bitcast.33), calls=%async_computation.4 | async-start | bytes 1572864 | tf_op jit(solution)/shard_map/all_to_all | solution.py:221
  78.8 12.2 %react.2 = f32[256,768]{1,0:T(8,128)} custom-call(f32[256,768]{1,0:T(8,128)} %bitcast.12.cells, bf16[1024,512]{1,0:T(8,128)(2,1)S(1)} %get-tuple-element.34.pick1, bf16[1024,512]{1,0:T(8,128)(2,1)S(1)} %get-tuple-element.35.pick2, bf16[256,2048]{1,0:T(8,128)(2,1)S(1)} %subtract_convert_fusion.change, f32[8,128]{1,0:T(8,128)S(1)} %bitcast.32), custom_call_target="tpu_custom_call" | custom-call | tf_op jit(solution)/shard_map/react/pallas_call | solution.py:188
  91.1 0.3 all-to-all-done.4.y_ref
  91.4 5.4 %all-to-all-start.2 = ((f32[8,32,768]{2,1,0:T(8,128)}), f32[8,32,768]{2,1,0:T(8,128)S(1)}, u32[]{:S(2)}, u32[]{:S(2)}) async-start(f32[8,32,768]{2,1,0:T(8,128)} %bitcast.34), calls=%async_computation.2 | async-start | bytes 1572864 | tf_op jit(solution)/shard_map/all_to_all | solution.py:221
  96.8 2.7 %join.2.refs_0_ = f32[32,96,128]{2,1,0:T(8,128)} custom-call(f32[8,32,768]{2,1,0:T(8,128)} %all-to-all-done.4.y_ref), custom_call_target="tpu_custom_call" | custom-call | tf_op jit(solution)/shard_map/join/pallas_call | solution.py:143
  99.5 9.2 %all-to-all-done.2.y_ref = f32[8,32,768]{2,1,0:T(8,128)S(1)} async-done(((f32[8,32,768]{2,1,0:T(8,128)}), f32[8,32,768]{2,1,0:T(8,128)S(1)}, u32[]{:S(2)}, u32[]{:S(2)}) %all-to-all-start.2) | async-done | bytes 786464 | tf_op jit(solution)/shard_map/all_to_all | solution.py:221
  108.7 1.5 %join.3 = f32[32,96,128]{2,1,0:T(8,128)} custom-call(f32[8,32,768]{2,1,0:T(8,128)S(1)} %all-to-all-done.2.y_ref, f32[32,96,128]{2,1,0:T(8,128)} %join.2.refs_0_), custom_call_target="tpu_custom_call", output_to_operand_aliasing={{}: (1, {})} | custom-call | tf_op jit(solution)/shard_map/join/pallas_call | solution.py:143
  (17 shorter events, 0.1 us)
Async XLA Ops:
  0.0 7.4 %copy-start.4 = (f32[2,2,768]{2,1,0:T(2,128)S(1)}, f32[2,2,768]{2,1,0:T(2,128)}, u32[]{:S(2)}) copy-start(f32[2,2,768]{2,1,0:T(2,128)} %param.7) | copy-start | bytes 36868
  0.0 13.5 %copy-start.3 = (s32[1024]{0:T(1024)S(1)}, s32[1024]{0:T(1024)}, u32[]{:S(2)}) copy-start(s32[1024]{0:T(1024)} %param.9) | copy-start | bytes 12292
  0.0 13.5 %copy-start.2 = (s32[1024]{0:T(1024)S(1)}, s32[1024]{0:T(1024)}, u32[]{:S(2)}) copy-start(s32[1024]{0:T(1024)} %param.10) | copy-start | bytes 12292
  0.0 13.5 %copy-start.5 = (s32[1024]{0:T(1024)S(1)}, s32[1024]{0:T(1024)}, u32[]{:S(2)}) copy-start(s32[1024]{0:T(1024)} %param.11) | copy-start | bytes 12292
  0.0 7.3 %collective-permute-start.1 = (f32[2,2,768]{2,1,0:T(2,128)}, f32[2,2,768]{2,1,0:T(2,128)S(1)}, u32[]{:S(2)}, u32[]{:S(2)}) collective-permute-start(f32[2,2,768]{2,1,0:T(2,128)} %param.7), channel_id=1, source_target_pairs={{8,0},{16,8},{24,16},{32,24},{40,32},{48,40},{56,48},{64,56},{72,6... | collective-permute-start | bytes 36872 | tf_op jit(solution)/shard_map/ppermute | solution.py:202
  0.5 6.8 %collective-permute-start = (f32[2,2,768]{2,1,0:T(2,128)}, f32[2,2,768]{2,1,0:T(2,128)S(1)}, u32[]{:S(2)}, u32[]{:S(2)}) collective-permute-start(f32[2,2,768]{2,1,0:T(2,128)} %param.7), channel_id=1, source_target_pairs={{0,8},{8,16},{16,24},{24,32},{32,40},{40,48},{48,56},{56,64},{64,7... | collective-permute-start | bytes 36872 | tf_op jit(solution)/shard_map/ppermute | solution.py:201
  2.7 32.0 %collective-permute-start.4 = (f32[1536,128]{1,0:T(8,128)}, f32[1536,128]{1,0:T(8,128)}, u32[]{:S(2)}, u32[]{:S(2)}) collective-permute-start(f32[1536,128]{1,0:T(8,128)} %bitcast.16), channel_id=1, source_target_pairs={{0,8},{8,16},{16,24},{24,32},{32,40},{40,48},{48,56},{56,64},{64,7... | collective-permute-start | bytes 2359304 | tf_op jit(solution)/shard_map/ppermute | solution.py:201
  7.4 27.4 %collective-permute-start.5 = (f32[1536,128]{1,0:T(8,128)}, f32[1536,128]{1,0:T(8,128)}, u32[]{:S(2)}, u32[]{:S(2)}) collective-permute-start(f32[1536,128]{1,0:T(8,128)} %bitcast.16), channel_id=1, source_target_pairs={{8,0},{16,8},{24,16},{32,24},{40,32},{48,40},{56,48},{64,56},{72,6... | collective-permute-start | bytes 2359304 | tf_op jit(solution)/shard_map/ppermute | solution.py:202
  8.2 26.5 %all-to-all-start = ((f32[8,3,2,2,768]{4,3,2,1,0:T(2,128)}), f32[8,3,2,2,768]{4,3,2,1,0:T(2,128)S(1)}, u32[]{:S(2)}, u32[]{:S(2)}) async-start(f32[8,3,2,2,768]{4,3,2,1,0:T(2,128)} %broadcast_in_dim.2), calls=%async_computation | async-start | bytes 589824 | tf_op jit(solution)/shard_map/all_to_all | solution.py:221
  13.6 1.4 %copy-start.1 = (f32[32,2,6144]{2,1,0:T(2,128)S(1)}, f32[32,2,6144]{2,1,0:T(2,128)}, u32[]{:S(2)}) copy-start(f32[32,2,6144]{2,1,0:T(2,128)} %param.6) | copy-start | bytes 4718596
  15.9 27.6 %collective-permute-start.2 = (f32[1536,128]{1,0:T(8,128)}, f32[1536,128]{1,0:T(8,128)}, u32[]{:S(2)}, u32[]{:S(2)}) collective-permute-start(f32[1536,128]{1,0:T(8,128)} %bitcast.6), channel_id=1, source_target_pairs={{8,0},{16,8},{24,16},{32,24},{40,32},{48,40},{56,48},{64,56},{72,6... | collective-permute-start | bytes 2359304 | tf_op jit(solution)/shard_map/ppermute | solution.py:202
  15.9 27.6 %collective-permute-start.3 = (f32[1536,128]{1,0:T(8,128)}, f32[1536,128]{1,0:T(8,128)}, u32[]{:S(2)}, u32[]{:S(2)}) collective-permute-start(f32[1536,128]{1,0:T(8,128)} %bitcast.6), channel_id=1, source_target_pairs={{0,8},{8,16},{16,24},{24,32},{32,40},{40,48},{48,56},{56,64},{64,7... | collective-permute-start | bytes 2359304 | tf_op jit(solution)/shard_map/ppermute | solution.py:201
  38.4 18.3 %all-to-all-start.3 = ((f32[8,32,768]{2,1,0:T(8,128)}), f32[8,32,768]{2,1,0:T(8,128)}, u32[]{:S(2)}, u32[]{:S(2)}) async-start(f32[8,32,768]{2,1,0:T(8,128)} %transport.3), calls=%async_computation.3 | async-start | bytes 1572864 | tf_op jit(solution)/shard_map/all_to_all | solution.py:221
  47.3 13.9 %copy-start = (f32[1024]{0:T(1024)S(1)}, f32[1024]{0:T(1024)}, u32[]{:S(2)}) copy-start(f32[1024]{0:T(1024)} %param.8) | copy-start | bytes 12292
  56.7 17.3 %all-to-all-start.1 = ((f32[8,32,768]{2,1,0:T(8,128)}), f32[8,32,768]{2,1,0:T(8,128)}, u32[]{:S(2)}, u32[]{:S(2)}) async-start(f32[8,32,768]{2,1,0:T(8,128)} %transport.2), calls=%async_computation.1 | async-start | bytes 1572864 | tf_op jit(solution)/shard_map/all_to_all | solution.py:221
  74.0 17.4 %all-to-all-start.4 = ((f32[8,32,768]{2,1,0:T(8,128)}), f32[8,32,768]{2,1,0:T(8,128)}, u32[]{:S(2)}, u32[]{:S(2)}) async-start(f32[8,32,768]{2,1,0:T(8,128)} %bitcast.33), calls=%async_computation.4 | async-start | bytes 1572864 | tf_op jit(solution)/shard_map/all_to_all | solution.py:221
  91.4 17.3 %all-to-all-start.2 = ((f32[8,32,768]{2,1,0:T(8,128)}), f32[8,32,768]{2,1,0:T(8,128)S(1)}, u32[]{:S(2)}, u32[]{:S(2)}) async-start(f32[8,32,768]{2,1,0:T(8,128)} %bitcast.34), calls=%async_computation.2 | async-start | bytes 1572864 | tf_op jit(solution)/shard_map/all_to_all | solution.py:221

commit v10 on v6

--- a/solution.py
+++ b/solution.py
@@ -35,7 +35,7 @@
     pieces = width // LANES
     stride = own.shape[1]
     pairs = winds.shape[4] // width
-    rows = 16
+    rows = 32
     y = lax.rem(lax.broadcasted_iota(jnp.int32, (4, width), 1), NY)
     steps = pl.num_programs(0)
     sources = ahead // pairs

time: 103 us -> 103 us (level)
  transfers between devices with their start and end apart: 11 -> 11, of which waited for: 5 -> 5; matrix products, arithmetic and copies ran while one was open for 5% -> 5% of each run, Pallas kernels for 35% -> 34%
where the time goes in v10:
time: 103 us; the launch traced here: 102 us
  Pallas kernels  36.1 us (35%)
  starting transfers between devices  32 us (31%)
  waiting for transfers between devices  28.4 us (28%)
  local copies, waits for them, and re-layouts  3.87 us (4%)
  other arithmetic  1.35 us (1%)
    all_to_all x5, waiting for transfers between devices, exchange(): lax.all_to_all(blocks, 'tracer', split_axis=0, concat_axis=0, tiled=True)  28.4 us
    all_to_all x5, starting transfers between devices, exchange(): lax.all_to_all(blocks, 'tracer', split_axis=0, concat_axis=0, tiled=True)  25 us
    pallas_call x2, Pallas kernels, react(): pl.pallas_call(react_kernel, in_specs=[VMEM] * 5, out_specs=pl.BlockSpec(...  24.5 us
    pallas_call x2, Pallas kernels, transport(): pl.pallas_call(functools.partial(transport_kernel, chunk), grid=(steps,),...  7.46 us
    ppermute x3, starting transfers between devices, neighbours(): lax.ppermute(array, 'region', [(i, (i + 1) % count) for i in range(count)])  4.97 us
    pallas_call x2, Pallas kernels, join(): pl.pallas_call(join_kernel, grid=(own // 8,), in_specs=[VMEM] + [pl.Block...  4.23 us
    slice x1, local copies, waits for them, and re-layouts, body(): raw = lax.slice_in_dim(tracers, 0, part, axis=2)  2.06 us
  transfers between devices with their start and end apart: 11, of which 5 were waited for; matrix products, arithmetic and copies ran while one was open for 5% of the time, Pallas kernels for 34%

profile of v10, /device:TPU:224, one launch (start us, length us, event | category | flops | bytes accessed | tf_op | source)
XLA Modules:
  0.0 101.9 jit_solution(13743407477005803639)
XLA Ops:
  0.0 0.5 collective-permute-start.1
  0.5 0.1 collective-permute-start
  0.6 2.1 %slice.6 = f32[32,2,3072]{2,1,0:T(2,128)} slice(f32[32,2,6144]{2,1,0:T(2,128)} %param.6), slice={[0:32], [0:2], [0:3072]} | slice | bytes 1572864 | tf_op jit(solution)/shard_map/slice | solution.py:230
  2.7 4.7 %collective-permute-start.4 = (f32[1536,128]{1,0:T(8,128)}, f32[1536,128]{1,0:T(8,128)}, u32[]{:S(2)}, u32[]{:S(2)}) collective-permute-start(f32[1536,128]{1,0:T(8,128)} %bitcast.16), channel_id=1, source_target_pairs={{0,8},{8,16},{16,24},{24,32},{32,40},{40,48},{48,56},{56,64},{64,7... | collective-permute-start | bytes 2359304 | tf_op jit(solution)/shard_map/ppermute | solution.py:199
  7.4 0.0 collective-permute-start.5
  7.4 0.0 collective-permute-done.1
  7.4 0.0 collective-permute-done
  7.4 0.8 broadcast_in_dim.2
  8.2 5.3 %all-to-all-start = ((f32[8,3,2,2,768]{4,3,2,1,0:T(2,128)}), f32[8,3,2,2,768]{4,3,2,1,0:T(2,128)S(1)}, u32[]{:S(2)}, u32[]{:S(2)}) async-start(f32[8,3,2,2,768]{4,3,2,1,0:T(2,128)} %broadcast_in_dim.2), calls=%async_computation | async-start | bytes 589824 | tf_op jit(solution)/shard_map/all_to_all | solution.py:219
  13.6 0.0 copy-start.1
  13.6 0.6 subtract_convert_fusion.change
  14.2 0.7 compare_convert_fusion
  14.9 0.1 copy-done.1
  15.0 0.9 slice.7
  15.9 0.2 collective-permute-start.2
  16.1 1.5 %collective-permute-start.3 = (f32[1536,128]{1,0:T(8,128)}, f32[1536,128]{1,0:T(8,128)}, u32[]{:S(2)}, u32[]{:S(2)}) collective-permute-start(f32[1536,128]{1,0:T(8,128)} %bitcast.6), channel_id=1, source_target_pairs={{8,0},{16,8},{24,16},{32,24},{40,32},{48,40},{56,48},{64,56},{72,6... | collective-permute-start | bytes 2359304 | tf_op jit(solution)/shard_map/ppermute | solution.py:200
  17.6 8.6 %all-to-all-done.winds = f32[8,3,2,2,768]{4,3,2,1,0:T(2,128)S(1)} async-done(((f32[8,3,2,2,768]{4,3,2,1,0:T(2,128)}), f32[8,3,2,2,768]{4,3,2,1,0:T(2,128)S(1)}, u32[]{:S(2)}, u32[]{:S(2)}) %all-to-all-start) | async-done | bytes 294944 | tf_op jit(solution)/shard_map/all_to_all | solution.py:219
  26.3 0.0 collective-permute-done.4
  26.3 3.7 %transport.3 = f32[8,32,768]{2,1,0:T(8,128)} custom-call(f32[8,3,2,2,768]{4,3,2,1,0:T(2,128)S(1)} %all-to-all-done.winds, f32[32,48,128]{2,1,0:T(8,128)} %bitcast.17.left, f32[32,48,128]{2,1,0:T(8,128)} %bitcast.19.own, f32[32,48,128]{2,1,0:T(8,128)} %bitcast.21.right), custom_call_target="tpu_custom_call" | custom-call | tf_op jit(solution)/shard_map/transport/pallas_call | solution.py:110
  30.0 5.1 %all-to-all-start.3 = ((f32[8,32,768]{2,1,0:T(8,128)}), f32[8,32,768]{2,1,0:T(8,128)}, u32[]{:S(2)}, u32[]{:S(2)}) async-start(f32[8,32,768]{2,1,0:T(8,128)} %transport.3), calls=%async_computation.3 | async-start | bytes 1572864 | tf_op jit(solution)/shard_map/all_to_all | solution.py:219
  35.1 3.7 %transport.2 = f32[8,32,768]{2,1,0:T(8,128)} custom-call(f32[8,3,2,2,768]{4,3,2,1,0:T(2,128)S(1)} %all-to-all-done.winds, f32[32,48,128]{2,1,0:T(8,128)} %bitcast.7.left, f32[32,48,128]{2,1,0:T(8,128)} %bitcast.9.own, f32[32,48,128]{2,1,0:T(8,128)} %bitcast.11.right), custom_call_target="tpu_custom_call" | custom-call | tf_op jit(solution)/shard_map/transport/pallas_call | solution.py:110
  38.8 9.6 %all-to-all-done.3 = f32[8,32,768]{2,1,0:T(8,128)} async-done(((f32[8,32,768]{2,1,0:T(8,128)}), f32[8,32,768]{2,1,0:T(8,128)}, u32[]{:S(2)}, u32[]{:S(2)}) %all-to-all-start.3) | async-done | bytes 786464 | tf_op jit(solution)/shard_map/all_to_all | solution.py:219
  48.4 4.4 %all-to-all-start.1 = ((f32[8,32,768]{2,1,0:T(8,128)}), f32[8,32,768]{2,1,0:T(8,128)}, u32[]{:S(2)}, u32[]{:S(2)}) async-start(f32[8,32,768]{2,1,0:T(8,128)} %transport.2), calls=%async_computation.1 | async-start | bytes 1572864 | tf_op jit(solution)/shard_map/all_to_all | solution.py:219
  52.8 12.2 %react.3 = f32[256,768]{1,0:T(8,128)} custom-call(f32[256,768]{1,0:T(8,128)} %bitcast.22.cells, bf16[1024,512]{1,0:T(8,128)(2,1)S(1)} %get-tuple-element.34.pick1, bf16[1024,512]{1,0:T(8,128)(2,1)S(1)} %get-tuple-element.35.pick2, bf16[256,2048]{1,0:T(8,128)(2,1)S(1)} %subtract_convert_fusion.change, f32[8,128]{1,0:T(8,128)S(1)} %bitcast.31), custom_call_target="tpu_custom_call" | custom-call | tf_op jit(solution)/shard_map/react/pallas_call | solution.py:186
  65.0 0.7 all-to-all-done.1
  65.7 4.8 %all-to-all-start.4 = ((f32[8,32,768]{2,1,0:T(8,128)}), f32[8,32,768]{2,1,0:T(8,128)}, u32[]{:S(2)}, u32[]{:S(2)}) async-start(f32[8,32,768]{2,1,0:T(8,128)} %bitcast.33), calls=%async_computation.4 | async-start | bytes 1572864 | tf_op jit(solution)/shard_map/all_to_all | solution.py:219
  70.5 12.2 %react.2 = f32[256,768]{1,0:T(8,128)} custom-call(f32[256,768]{1,0:T(8,128)} %bitcast.12.cells, bf16[1024,512]{1,0:T(8,128)(2,1)S(1)} %get-tuple-element.34.pick1, bf16[1024,512]{1,0:T(8,128)(2,1)S(1)} %get-tuple-element.35.pick2, bf16[256,2048]{1,0:T(8,128)(2,1)S(1)} %subtract_convert_fusion.change, f32[8,128]{1,0:T(8,128)S(1)} %bitcast.32), custom_call_target="tpu_custom_call" | custom-call | tf_op jit(solution)/shard_map/react/pallas_call | solution.py:186
  82.7 0.3 all-to-all-done.4.y_ref
  83.1 5.4 %all-to-all-start.2 = ((f32[8,32,768]{2,1,0:T(8,128)}), f32[8,32,768]{2,1,0:T(8,128)S(1)}, u32[]{:S(2)}, u32[]{:S(2)}) async-start(f32[8,32,768]{2,1,0:T(8,128)} %bitcast.34), calls=%async_computation.2 | async-start | bytes 1572864 | tf_op jit(solution)/shard_map/all_to_all | solution.py:219
  88.5 2.7 %join.2.refs_0_ = f32[32,96,128]{2,1,0:T(8,128)} custom-call(f32[8,32,768]{2,1,0:T(8,128)} %all-to-all-done.4.y_ref), custom_call_target="tpu_custom_call" | custom-call | tf_op jit(solution)/shard_map/join/pallas_call | solution.py:141
  91.2 9.2 %all-to-all-done.2.y_ref = f32[8,32,768]{2,1,0:T(8,128)S(1)} async-done(((f32[8,32,768]{2,1,0:T(8,128)}), f32[8,32,768]{2,1,0:T(8,128)S(1)}, u32[]{:S(2)}, u32[]{:S(2)}) %all-to-all-start.2) | async-done | bytes 786464 | tf_op jit(solution)/shard_map/all_to_all | solution.py:219
  100.4 1.5 %join.3 = f32[32,96,128]{2,1,0:T(8,128)} custom-call(f32[8,32,768]{2,1,0:T(8,128)S(1)} %all-to-all-done.2.y_ref, f32[32,96,128]{2,1,0:T(8,128)} %join.2.refs_0_), custom_call_target="tpu_custom_call", output_to_operand_aliasing={{}: (1, {})} | custom-call | tf_op jit(solution)/shard_map/join/pallas_call | solution.py:141
  (17 shorter events, 0.1 us)
Async XLA Ops:
  0.0 7.4 %copy-start.4 = (f32[2,2,768]{2,1,0:T(2,128)S(1)}, f32[2,2,768]{2,1,0:T(2,128)}, u32[]{:S(2)}) copy-start(f32[2,2,768]{2,1,0:T(2,128)} %param.7) | copy-start | bytes 36868
  0.0 13.5 %copy-start.3 = (s32[1024]{0:T(1024)S(1)}, s32[1024]{0:T(1024)}, u32[]{:S(2)}) copy-start(s32[1024]{0:T(1024)} %param.9) | copy-start | bytes 12292
  0.0 13.5 %copy-start.2 = (s32[1024]{0:T(1024)S(1)}, s32[1024]{0:T(1024)}, u32[]{:S(2)}) copy-start(s32[1024]{0:T(1024)} %param.10) | copy-start | bytes 12292
  0.0 13.5 %copy-start.5 = (s32[1024]{0:T(1024)S(1)}, s32[1024]{0:T(1024)}, u32[]{:S(2)}) copy-start(s32[1024]{0:T(1024)} %param.11) | copy-start | bytes 12292
  0.0 7.3 %collective-permute-start.1 = (f32[2,2,768]{2,1,0:T(2,128)}, f32[2,2,768]{2,1,0:T(2,128)S(1)}, u32[]{:S(2)}, u32[]{:S(2)}) collective-permute-start(f32[2,2,768]{2,1,0:T(2,128)} %param.7), channel_id=1, source_target_pairs={{8,0},{16,8},{24,16},{32,24},{40,32},{48,40},{56,48},{64,56},{72,6... | collective-permute-start | bytes 36872 | tf_op jit(solution)/shard_map/ppermute | solution.py:200
  0.5 6.8 %collective-permute-start = (f32[2,2,768]{2,1,0:T(2,128)}, f32[2,2,768]{2,1,0:T(2,128)S(1)}, u32[]{:S(2)}, u32[]{:S(2)}) collective-permute-start(f32[2,2,768]{2,1,0:T(2,128)} %param.7), channel_id=1, source_target_pairs={{0,8},{8,16},{16,24},{24,32},{32,40},{40,48},{48,56},{56,64},{64,7... | collective-permute-start | bytes 36872 | tf_op jit(solution)/shard_map/ppermute | solution.py:199
  2.7 23.6 %collective-permute-start.4 = (f32[1536,128]{1,0:T(8,128)}, f32[1536,128]{1,0:T(8,128)}, u32[]{:S(2)}, u32[]{:S(2)}) collective-permute-start(f32[1536,128]{1,0:T(8,128)} %bitcast.16), channel_id=1, source_target_pairs={{0,8},{8,16},{16,24},{24,32},{32,40},{40,48},{48,56},{56,64},{64,7... | collective-permute-start | bytes 2359304 | tf_op jit(solution)/shard_map/ppermute | solution.py:199
  7.4 18.9 %collective-permute-start.5 = (f32[1536,128]{1,0:T(8,128)}, f32[1536,128]{1,0:T(8,128)}, u32[]{:S(2)}, u32[]{:S(2)}) collective-permute-start(f32[1536,128]{1,0:T(8,128)} %bitcast.16), channel_id=1, source_target_pairs={{8,0},{16,8},{24,16},{32,24},{40,32},{48,40},{56,48},{64,56},{72,6... | collective-permute-start | bytes 2359304 | tf_op jit(solution)/shard_map/ppermute | solution.py:200
  8.2 18.1 %all-to-all-start = ((f32[8,3,2,2,768]{4,3,2,1,0:T(2,128)}), f32[8,3,2,2,768]{4,3,2,1,0:T(2,128)S(1)}, u32[]{:S(2)}, u32[]{:S(2)}) async-start(f32[8,3,2,2,768]{4,3,2,1,0:T(2,128)} %broadcast_in_dim.2), calls=%async_computation | async-start | bytes 589824 | tf_op jit(solution)/shard_map/all_to_all | solution.py:219
  13.6 1.4 %copy-start.1 = (f32[32,2,6144]{2,1,0:T(2,128)S(1)}, f32[32,2,6144]{2,1,0:T(2,128)}, u32[]{:S(2)}) copy-start(f32[32,2,6144]{2,1,0:T(2,128)} %param.6) | copy-start | bytes 4718596
  15.9 19.2 %collective-permute-start.2 = (f32[1536,128]{1,0:T(8,128)}, f32[1536,128]{1,0:T(8,128)}, u32[]{:S(2)}, u32[]{:S(2)}) collective-permute-start(f32[1536,128]{1,0:T(8,128)} %bitcast.6), channel_id=1, source_target_pairs={{0,8},{8,16},{16,24},{24,32},{32,40},{40,48},{48,56},{56,64},{64,7... | collective-permute-start | bytes 2359304 | tf_op jit(solution)/shard_map/ppermute | solution.py:199
  16.1 19.0 %collective-permute-start.3 = (f32[1536,128]{1,0:T(8,128)}, f32[1536,128]{1,0:T(8,128)}, u32[]{:S(2)}, u32[]{:S(2)}) collective-permute-start(f32[1536,128]{1,0:T(8,128)} %bitcast.6), channel_id=1, source_target_pairs={{8,0},{16,8},{24,16},{32,24},{40,32},{48,40},{56,48},{64,56},{72,6... | collective-permute-start | bytes 2359304 | tf_op jit(solution)/shard_map/ppermute | solution.py:200
  30.0 18.4 %all-to-all-start.3 = ((f32[8,32,768]{2,1,0:T(8,128)}), f32[8,32,768]{2,1,0:T(8,128)}, u32[]{:S(2)}, u32[]{:S(2)}) async-start(f32[8,32,768]{2,1,0:T(8,128)} %transport.3), calls=%async_computation.3 | async-start | bytes 1572864 | tf_op jit(solution)/shard_map/all_to_all | solution.py:219
  38.8 14.0 %copy-start = (f32[1024]{0:T(1024)S(1)}, f32[1024]{0:T(1024)}, u32[]{:S(2)}) copy-start(f32[1024]{0:T(1024)} %param.8) | copy-start | bytes 12292
  48.4 17.3 %all-to-all-start.1 = ((f32[8,32,768]{2,1,0:T(8,128)}), f32[8,32,768]{2,1,0:T(8,128)}, u32[]{:S(2)}, u32[]{:S(2)}) async-start(f32[8,32,768]{2,1,0:T(8,128)} %transport.2), calls=%async_computation.1 | async-start | bytes 1572864 | tf_op jit(solution)/shard_map/all_to_all | solution.py:219
  65.7 17.4 %all-to-all-start.4 = ((f32[8,32,768]{2,1,0:T(8,128)}), f32[8,32,768]{2,1,0:T(8,128)}, u32[]{:S(2)}, u32[]{:S(2)}) async-start(f32[8,32,768]{2,1,0:T(8,128)} %bitcast.33), calls=%async_computation.4 | async-start | bytes 1572864 | tf_op jit(solution)/shard_map/all_to_all | solution.py:219
  83.1 17.3 %all-to-all-start.2 = ((f32[8,32,768]{2,1,0:T(8,128)}), f32[8,32,768]{2,1,0:T(8,128)S(1)}, u32[]{:S(2)}, u32[]{:S(2)}) async-start(f32[8,32,768]{2,1,0:T(8,128)} %bitcast.34), calls=%async_computation.2 | async-start | bytes 1572864 | tf_op jit(solution)/shard_map/all_to_all | solution.py:219

commit v11 on v10

--- a/solution.py
+++ b/solution.py
@@ -156,12 +156,15 @@
     return jnp.concatenate([high, low], axis=0)
 
 
-def react_kernel(cells, pick1, pick2, change, rates, out, done, sems):
-    amounts = cells[...]
+def react_kernel(cells, pick1, pick2, change, rates, out, held, done, sems, load_sem):
+    load = pltpu.make_async_copy(cells, held, load_sem)
+    load.start()
     rate = jnp.concatenate(
         [jnp.broadcast_to(rates[i : i + 1, :], (LANES, LANES)).T for i in range(rates.shape[0])], axis=0
     )
-    rate = jnp.concatenate([rate] * (amounts.shape[1] // LANES), axis=1)
+    rate = jnp.concatenate([rate] * (cells.shape[1] // LANES), axis=1)
+    load.wait()
+    amounts = held[...]
     tile = 256
     copies = []
     for step in range(SUBSTEPS):
@@ -185,13 +188,14 @@
 def react(cells, pick1, pick2, change, rates):
     return pl.pallas_call(
         react_kernel,
-        in_specs=[VMEM] * 5,
+        in_specs=[pl.BlockSpec(memory_space=pl.ANY)] + [VMEM] * 4,
         out_specs=pl.BlockSpec(memory_space=pltpu.HBM),
         out_shape=pltpu.HBM(cells.shape, F32),
-        scratch_shapes=[pltpu.VMEM(cells.shape, F32), pltpu.SemaphoreType.DMA((cells.shape[1] // 256,))],
+        scratch_shapes=[pltpu.VMEM(cells.shape, F32)] * 2
+        + [pltpu.SemaphoreType.DMA((cells.shape[1] // 256,)), pltpu.SemaphoreType.DMA(())],
         compiler_params=pltpu.CompilerParams(vmem_limit_bytes=24 << 20),
         name="react",
-    )(pltpu.with_memory_space_constraint(cells, pltpu.VMEM), pick1, pick2, change, rates)
+    )(cells, pick1, pick2, change, rates)
 
 
 def neighbours(array):

time: 103 us -> 103 us (level)
  no operation moved by 1% of the time
where the time goes in v11:
time: 103 us; the launch traced here: 102 us
  Pallas kernels  36.2 us (35%)
  starting transfers between devices  32 us (31%)
  waiting for transfers between devices  28.4 us (28%)
  local copies, waits for them, and re-layouts  3.87 us (4%)
  other arithmetic  1.35 us (1%)
    all_to_all x5, waiting for transfers between devices, exchange(): lax.all_to_all(blocks, 'tracer', split_axis=0, concat_axis=0, tiled=True)  28.4 us
    all_to_all x5, starting transfers between devices, exchange(): lax.all_to_all(blocks, 'tracer', split_axis=0, concat_axis=0, tiled=True)  25 us
    pallas_call x2, Pallas kernels, react(): pl.pallas_call(react_kernel, in_specs=[pl.BlockSpec(memory_space=pl.ANY)]...  24.5 us
    pallas_call x2, Pallas kernels, transport(): pl.pallas_call(functools.partial(transport_kernel, chunk), grid=(steps,),...  7.46 us
    ppermute x3, starting transfers between devices, neighbours(): lax.ppermute(array, 'region', [(i, (i + 1) % count) for i in range(count)])  4.97 us
    pallas_call x2, Pallas kernels, join(): pl.pallas_call(join_kernel, grid=(own // 8,), in_specs=[VMEM] + [pl.Block...  4.23 us
    slice x1, local copies, waits for them, and re-layouts, body(): raw = lax.slice_in_dim(tracers, 0, part, axis=2)  2.06 us
  transfers between devices with their start and end apart: 11, of which 5 were waited for; matrix products, arithmetic and copies ran while one was open for 5% of the time, Pallas kernels for 34%

profile of v11, /device:TPU:224, one launch (start us, length us, event | category | flops | bytes accessed | tf_op | source)
XLA Modules:
  0.0 101.9 jit_solution(14706525087718511588)
XLA Ops:
  0.0 0.5 collective-permute-start.1
  0.5 0.1 collective-permute-start
  0.6 2.1 %slice.6 = f32[32,2,3072]{2,1,0:T(2,128)} slice(f32[32,2,6144]{2,1,0:T(2,128)} %param.6), slice={[0:32], [0:2], [0:3072]} | slice | bytes 1572864 | tf_op jit(solution)/shard_map/slice | solution.py:234
  2.7 4.7 %collective-permute-start.4 = (f32[1536,128]{1,0:T(8,128)}, f32[1536,128]{1,0:T(8,128)}, u32[]{:S(2)}, u32[]{:S(2)}) collective-permute-start(f32[1536,128]{1,0:T(8,128)} %bitcast.16), channel_id=1, source_target_pairs={{0,8},{8,16},{16,24},{24,32},{32,40},{40,48},{48,56},{56,64},{64,7... | collective-permute-start | bytes 2359304 | tf_op jit(solution)/shard_map/ppermute | solution.py:203
  7.4 0.0 collective-permute-start.5
  7.4 0.0 collective-permute-done.1
  7.4 0.0 collective-permute-done
  7.4 0.8 broadcast_in_dim.2
  8.2 5.3 %all-to-all-start = ((f32[8,3,2,2,768]{4,3,2,1,0:T(2,128)}), f32[8,3,2,2,768]{4,3,2,1,0:T(2,128)S(1)}, u32[]{:S(2)}, u32[]{:S(2)}) async-start(f32[8,3,2,2,768]{4,3,2,1,0:T(2,128)} %broadcast_in_dim.2), calls=%async_computation | async-start | bytes 589824 | tf_op jit(solution)/shard_map/all_to_all | solution.py:223
  13.6 0.0 copy-start.1
  13.6 0.6 subtract_convert_fusion.change
  14.2 0.7 compare_convert_fusion
  14.9 0.1 copy-done.1
  15.0 0.9 slice.7
  15.9 0.2 collective-permute-start.2
  16.1 1.5 %collective-permute-start.3 = (f32[1536,128]{1,0:T(8,128)}, f32[1536,128]{1,0:T(8,128)}, u32[]{:S(2)}, u32[]{:S(2)}) collective-permute-start(f32[1536,128]{1,0:T(8,128)} %bitcast.6), channel_id=1, source_target_pairs={{8,0},{16,8},{24,16},{32,24},{40,32},{48,40},{56,48},{64,56},{72,6... | collective-permute-start | bytes 2359304 | tf_op jit(solution)/shard_map/ppermute | solution.py:204
  17.6 8.6 %all-to-all-done.winds = f32[8,3,2,2,768]{4,3,2,1,0:T(2,128)S(1)} async-done(((f32[8,3,2,2,768]{4,3,2,1,0:T(2,128)}), f32[8,3,2,2,768]{4,3,2,1,0:T(2,128)S(1)}, u32[]{:S(2)}, u32[]{:S(2)}) %all-to-all-start) | async-done | bytes 294944 | tf_op jit(solution)/shard_map/all_to_all | solution.py:223
  26.3 0.0 collective-permute-done.4
  26.3 3.7 %transport.3 = f32[8,32,768]{2,1,0:T(8,128)} custom-call(f32[8,3,2,2,768]{4,3,2,1,0:T(2,128)S(1)} %all-to-all-done.winds, f32[32,48,128]{2,1,0:T(8,128)} %bitcast.17.left, f32[32,48,128]{2,1,0:T(8,128)} %bitcast.19.own, f32[32,48,128]{2,1,0:T(8,128)} %bitcast.21.right), custom_call_target="tpu_custom_call" | custom-call | tf_op jit(solution)/shard_map/transport/pallas_call | solution.py:110
  30.0 5.1 %all-to-all-start.3 = ((f32[8,32,768]{2,1,0:T(8,128)}), f32[8,32,768]{2,1,0:T(8,128)}, u32[]{:S(2)}, u32[]{:S(2)}) async-start(f32[8,32,768]{2,1,0:T(8,128)} %transport.3), calls=%async_computation.3 | async-start | bytes 1572864 | tf_op jit(solution)/shard_map/all_to_all | solution.py:223
  35.1 3.7 %transport.2 = f32[8,32,768]{2,1,0:T(8,128)} custom-call(f32[8,3,2,2,768]{4,3,2,1,0:T(2,128)S(1)} %all-to-all-done.winds, f32[32,48,128]{2,1,0:T(8,128)} %bitcast.7.left, f32[32,48,128]{2,1,0:T(8,128)} %bitcast.9.own, f32[32,48,128]{2,1,0:T(8,128)} %bitcast.11.right), custom_call_target="tpu_custom_call" | custom-call | tf_op jit(solution)/shard_map/transport/pallas_call | solution.py:110
  38.8 9.6 %all-to-all-done.3 = f32[8,32,768]{2,1,0:T(8,128)} async-done(((f32[8,32,768]{2,1,0:T(8,128)}), f32[8,32,768]{2,1,0:T(8,128)}, u32[]{:S(2)}, u32[]{:S(2)}) %all-to-all-start.3) | async-done | bytes 786464 | tf_op jit(solution)/shard_map/all_to_all | solution.py:223
  48.4 4.4 %all-to-all-start.1 = ((f32[8,32,768]{2,1,0:T(8,128)}), f32[8,32,768]{2,1,0:T(8,128)}, u32[]{:S(2)}, u32[]{:S(2)}) async-start(f32[8,32,768]{2,1,0:T(8,128)} %transport.2), calls=%async_computation.1 | async-start | bytes 1572864 | tf_op jit(solution)/shard_map/all_to_all | solution.py:223
  52.8 12.2 %react.3 = f32[256,768]{1,0:T(8,128)} custom-call(f32[256,768]{1,0:T(8,128)} %bitcast.22.cells, bf16[1024,512]{1,0:T(8,128)(2,1)S(1)} %get-tuple-element.34.pick1, bf16[1024,512]{1,0:T(8,128)(2,1)S(1)} %get-tuple-element.35.pick2, bf16[256,2048]{1,0:T(8,128)(2,1)S(1)} %subtract_convert_fusion.change, f32[8,128]{1,0:T(8,128)S(1)} %bitcast.31), custom_call_target="tpu_custom_call" | custom-call | tf_op jit(solution)/shard_map/react/pallas_call | solution.py:189
  65.1 0.6 all-to-all-done.1
  65.7 4.8 %all-to-all-start.4 = ((f32[8,32,768]{2,1,0:T(8,128)}), f32[8,32,768]{2,1,0:T(8,128)}, u32[]{:S(2)}, u32[]{:S(2)}) async-start(f32[8,32,768]{2,1,0:T(8,128)} %bitcast.33), calls=%async_computation.4 | async-start | bytes 1572864 | tf_op jit(solution)/shard_map/all_to_all | solution.py:223
  70.5 12.3 %react.2 = f32[256,768]{1,0:T(8,128)} custom-call(f32[256,768]{1,0:T(8,128)} %bitcast.12.cells, bf16[1024,512]{1,0:T(8,128)(2,1)S(1)} %get-tuple-element.34.pick1, bf16[1024,512]{1,0:T(8,128)(2,1)S(1)} %get-tuple-element.35.pick2, bf16[256,2048]{1,0:T(8,128)(2,1)S(1)} %subtract_convert_fusion.change, f32[8,128]{1,0:T(8,128)S(1)} %bitcast.32), custom_call_target="tpu_custom_call" | custom-call | tf_op jit(solution)/shard_map/react/pallas_call | solution.py:189
  82.8 0.3 all-to-all-done.4.y_ref
  83.1 5.4 %all-to-all-start.2 = ((f32[8,32,768]{2,1,0:T(8,128)}), f32[8,32,768]{2,1,0:T(8,128)S(1)}, u32[]{:S(2)}, u32[]{:S(2)}) async-start(f32[8,32,768]{2,1,0:T(8,128)} %bitcast.34), calls=%async_computation.2 | async-start | bytes 1572864 | tf_op jit(solution)/shard_map/all_to_all | solution.py:223
  88.5 2.7 %join.2.refs_0_ = f32[32,96,128]{2,1,0:T(8,128)} custom-call(f32[8,32,768]{2,1,0:T(8,128)} %all-to-all-done.4.y_ref), custom_call_target="tpu_custom_call" | custom-call | tf_op jit(solution)/shard_map/join/pallas_call | solution.py:141
  91.2 9.2 %all-to-all-done.2.y_ref = f32[8,32,768]{2,1,0:T(8,128)S(1)} async-done(((f32[8,32,768]{2,1,0:T(8,128)}), f32[8,32,768]{2,1,0:T(8,128)S(1)}, u32[]{:S(2)}, u32[]{:S(2)}) %all-to-all-start.2) | async-done | bytes 786464 | tf_op jit(solution)/shard_map/all_to_all | solution.py:223
  100.4 1.5 %join.3 = f32[32,96,128]{2,1,0:T(8,128)} custom-call(f32[8,32,768]{2,1,0:T(8,128)S(1)} %all-to-all-done.2.y_ref, f32[32,96,128]{2,1,0:T(8,128)} %join.2.refs_0_), custom_call_target="tpu_custom_call", output_to_operand_aliasing={{}: (1, {})} | custom-call | tf_op jit(solution)/shard_map/join/pallas_call | solution.py:141
  (17 shorter events, 0.1 us)
Async XLA Ops:
  0.0 7.4 %copy-start.4 = (f32[2,2,768]{2,1,0:T(2,128)S(1)}, f32[2,2,768]{2,1,0:T(2,128)}, u32[]{:S(2)}) copy-start(f32[2,2,768]{2,1,0:T(2,128)} %param.7) | copy-start | bytes 36868
  0.0 13.5 %copy-start.3 = (s32[1024]{0:T(1024)S(1)}, s32[1024]{0:T(1024)}, u32[]{:S(2)}) copy-start(s32[1024]{0:T(1024)} %param.9) | copy-start | bytes 12292
  0.0 13.5 %copy-start.2 = (s32[1024]{0:T(1024)S(1)}, s32[1024]{0:T(1024)}, u32[]{:S(2)}) copy-start(s32[1024]{0:T(1024)} %param.10) | copy-start | bytes 12292
  0.0 13.5 %copy-start.5 = (s32[1024]{0:T(1024)S(1)}, s32[1024]{0:T(1024)}, u32[]{:S(2)}) copy-start(s32[1024]{0:T(1024)} %param.11) | copy-start | bytes 12292
  0.0 7.3 %collective-permute-start.1 = (f32[2,2,768]{2,1,0:T(2,128)}, f32[2,2,768]{2,1,0:T(2,128)S(1)}, u32[]{:S(2)}, u32[]{:S(2)}) collective-permute-start(f32[2,2,768]{2,1,0:T(2,128)} %param.7), channel_id=1, source_target_pairs={{8,0},{16,8},{24,16},{32,24},{40,32},{48,40},{56,48},{64,56},{72,6... | collective-permute-start | bytes 36872 | tf_op jit(solution)/shard_map/ppermute | solution.py:204
  0.5 6.8 %collective-permute-start = (f32[2,2,768]{2,1,0:T(2,128)}, f32[2,2,768]{2,1,0:T(2,128)S(1)}, u32[]{:S(2)}, u32[]{:S(2)}) collective-permute-start(f32[2,2,768]{2,1,0:T(2,128)} %param.7), channel_id=1, source_target_pairs={{0,8},{8,16},{16,24},{24,32},{32,40},{40,48},{48,56},{56,64},{64,7... | collective-permute-start | bytes 36872 | tf_op jit(solution)/shard_map/ppermute | solution.py:203
  2.7 23.6 %collective-permute-start.4 = (f32[1536,128]{1,0:T(8,128)}, f32[1536,128]{1,0:T(8,128)}, u32[]{:S(2)}, u32[]{:S(2)}) collective-permute-start(f32[1536,128]{1,0:T(8,128)} %bitcast.16), channel_id=1, source_target_pairs={{0,8},{8,16},{16,24},{24,32},{32,40},{40,48},{48,56},{56,64},{64,7... | collective-permute-start | bytes 2359304 | tf_op jit(solution)/shard_map/ppermute | solution.py:203
  7.4 18.9 %collective-permute-start.5 = (f32[1536,128]{1,0:T(8,128)}, f32[1536,128]{1,0:T(8,128)}, u32[]{:S(2)}, u32[]{:S(2)}) collective-permute-start(f32[1536,128]{1,0:T(8,128)} %bitcast.16), channel_id=1, source_target_pairs={{8,0},{16,8},{24,16},{32,24},{40,32},{48,40},{56,48},{64,56},{72,6... | collective-permute-start | bytes 2359304 | tf_op jit(solution)/shard_map/ppermute | solution.py:204
  8.2 18.1 %all-to-all-start = ((f32[8,3,2,2,768]{4,3,2,1,0:T(2,128)}), f32[8,3,2,2,768]{4,3,2,1,0:T(2,128)S(1)}, u32[]{:S(2)}, u32[]{:S(2)}) async-start(f32[8,3,2,2,768]{4,3,2,1,0:T(2,128)} %broadcast_in_dim.2), calls=%async_computation | async-start | bytes 589824 | tf_op jit(solution)/shard_map/all_to_all | solution.py:223
  13.6 1.4 %copy-start.1 = (f32[32,2,6144]{2,1,0:T(2,128)S(1)}, f32[32,2,6144]{2,1,0:T(2,128)}, u32[]{:S(2)}) copy-start(f32[32,2,6144]{2,1,0:T(2,128)} %param.6) | copy-start | bytes 4718596
  15.9 19.2 %collective-permute-start.2 = (f32[1536,128]{1,0:T(8,128)}, f32[1536,128]{1,0:T(8,128)}, u32[]{:S(2)}, u32[]{:S(2)}) collective-permute-start(f32[1536,128]{1,0:T(8,128)} %bitcast.6), channel_id=1, source_target_pairs={{0,8},{8,16},{16,24},{24,32},{32,40},{40,48},{48,56},{56,64},{64,7... | collective-permute-start | bytes 2359304 | tf_op jit(solution)/shard_map/ppermute | solution.py:203
  16.1 19.0 %collective-permute-start.3 = (f32[1536,128]{1,0:T(8,128)}, f32[1536,128]{1,0:T(8,128)}, u32[]{:S(2)}, u32[]{:S(2)}) collective-permute-start(f32[1536,128]{1,0:T(8,128)} %bitcast.6), channel_id=1, source_target_pairs={{8,0},{16,8},{24,16},{32,24},{40,32},{48,40},{56,48},{64,56},{72,6... | collective-permute-start | bytes 2359304 | tf_op jit(solution)/shard_map/ppermute | solution.py:204
  30.0 18.4 %all-to-all-start.3 = ((f32[8,32,768]{2,1,0:T(8,128)}), f32[8,32,768]{2,1,0:T(8,128)}, u32[]{:S(2)}, u32[]{:S(2)}) async-start(f32[8,32,768]{2,1,0:T(8,128)} %transport.3), calls=%async_computation.3 | async-start | bytes 1572864 | tf_op jit(solution)/shard_map/all_to_all | solution.py:223
  38.8 14.0 %copy-start = (f32[1024]{0:T(1024)S(1)}, f32[1024]{0:T(1024)}, u32[]{:S(2)}) copy-start(f32[1024]{0:T(1024)} %param.8) | copy-start | bytes 12292
  48.4 17.3 %all-to-all-start.1 = ((f32[8,32,768]{2,1,0:T(8,128)}), f32[8,32,768]{2,1,0:T(8,128)}, u32[]{:S(2)}, u32[]{:S(2)}) async-start(f32[8,32,768]{2,1,0:T(8,128)} %transport.2), calls=%async_computation.1 | async-start | bytes 1572864 | tf_op jit(solution)/shard_map/all_to_all | solution.py:223
  65.7 17.4 %all-to-all-start.4 = ((f32[8,32,768]{2,1,0:T(8,128)}), f32[8,32,768]{2,1,0:T(8,128)}, u32[]{:S(2)}, u32[]{:S(2)}) async-start(f32[8,32,768]{2,1,0:T(8,128)} %bitcast.33), calls=%async_computation.4 | async-start | bytes 1572864 | tf_op jit(solution)/shard_map/all_to_all | solution.py:223
  83.1 17.3 %all-to-all-start.2 = ((f32[8,32,768]{2,1,0:T(8,128)}), f32[8,32,768]{2,1,0:T(8,128)S(1)}, u32[]{:S(2)}, u32[]{:S(2)}) async-start(f32[8,32,768]{2,1,0:T(8,128)} %bitcast.34), calls=%async_computation.2 | async-start | bytes 1572864 | tf_op jit(solution)/shard_map/all_to_all | solution.py:223
